TPU v7x, 32 devices: a whole 2x2x4 slice. The times are simulated.
32 devices in a mesh: member: 8 (over z, x), section: 4 (over y, core).
Axes of the slice: x: 2, y: 2, z: 4, core: 2. Of those that a mesh axis runs over, the one named last changes fastest.
Arguments:
- inputs: bfloat16 [8, 2, 1, 14, 14, 512], P('member'), may hold values from -6 to 6
- cotangent: bfloat16 [8, 2, 1, 14, 14, 512], P('member'), may hold values from -6 to 6
- probe: bfloat16 [8, 1, 14, 14, 512], P('member'), may hold values from -6 to 6
- dw_kernel: float32 [8, 4, 7, 7, 512], P('member', 'section'), may hold values from -0.875 to 0.875
- dw_bias: float32 [8, 4, 512], P('member', 'section'), may hold values from -3 to 3
- norm_gain: float32 [8, 4, 512], P('member', 'section'), may hold values from 0.5 to 1.5
- norm_bias: float32 [8, 4, 512], P('member', 'section'), may hold values from -3 to 3
- w_in: float32 [8, 4, 512, 2048], P('member', 'section'), may hold values from -0.25 to 0.25
- b_in: float32 [8, 4, 2048], P('member', 'section'), may hold values from -3 to 3
- w_out: float32 [8, 4, 2048, 512], P('member', 'section'), may hold values from -0.125 to 0.125
- b_out: float32 [8, 4, 512], P('member', 'section'), may hold values from -3 to 3
- layer_scale: float32 [8, 4, 512], P('member', 'section'), may hold values from 0.3 to 1.5
- shuffle_mask: int32 [4, 32], P('section'), may hold values from 0 to 1, as said below
- source_member: int32 [4, 32, 8], P('section'), may hold values from 0 to 7, as said below
Outputs:
- new_w_in: float32 [8, 4, 512, 2048], P('member', 'section')
- new_w_out: float32 [8, 4, 2048, 512], P('member', 'section')
- features: bfloat16 [8, 4, 1, 14, 14, 512], P('member', 'section')
Inputs may be any that keep to these rules, and one draw needn't show every extreme that they name: `shuffle_mask`: each section marks exactly 16 of its 32 blocks. Each source_member[s, k] is a permutation of the members. For the marked blocks of a section no member is its own source, and no member is the source of more than 3 of another member's blocks; some pair of members reaches 3 in every section.
All inputs are finite; a program needn't handle non-finite values.
Results may differ from a plain program's by a relative error of at most 0.014.
Values may be sent and summed in bfloat16 or wider, within the bound.
No kernel may reach another device: no remote copies, remote signals or barrier semaphores. Data moves between devices by JAX's collectives and lax.ppermute only.
A program may use at most 192 MiB of HBM per device.

v0:
```python
import jax
import jax.numpy as jnp
from jax import lax
from jax.sharding import PartitionSpec as P

TILE = 128


learning_rate = 0.001
norm_epsilon = 1e-06


def from_behind(value, axis, steps):
    count = lax.axis_size(axis)
    first, last = (max(0, -steps), min(count, count - steps))
    return lax.ppermute(value, axis, [(source, source + steps) for source in range(first, last)])


def depthwise(widened, kernel):
    height = widened.shape[1]
    width = widened.shape[2]
    padded = jnp.pad(widened, ((0, 0), (3, 3), (3, 3), (0, 0)))
    total = jnp.zeros(widened.shape, jnp.float32)
    for row_off in range(7):
        for col_off in range(7):
            total = (
                total
                + kernel[row_off, col_off]
                * padded[:, row_off : row_off + height, col_off : col_off + width, :]
            )
    return total


def block(params, incoming):
    (
        kernel,
        conv_bias,
        gain,
        shift_bias,
        first_weight,
        first_bias,
        second_weight,
        second_bias,
        scale,
    ) = params
    widened = incoming.astype(jnp.float32)
    channels = widened.shape[-1]
    spread = depthwise(widened, kernel) + conv_bias
    center = jnp.mean(spread, axis=-1, keepdims=True)
    offset = spread - center
    variance = jnp.mean(offset * offset, axis=-1, keepdims=True)
    normed = (offset * lax.rsqrt(variance + norm_epsilon) * gain + shift_bias).astype(jnp.bfloat16)
    rows = normed.reshape(-1, channels)
    hidden = jax.nn.gelu(
        jnp.dot(rows, first_weight, preferred_element_type=jnp.float32) + first_bias,
        approximate=False,
    ).astype(jnp.bfloat16)
    mixed = jnp.dot(hidden, second_weight, preferred_element_type=jnp.float32) + second_bias
    return (widened + scale * mixed.reshape(widened.shape)).astype(jnp.bfloat16)


def lowered(params):
    return tuple(
        (
            leaf.astype(jnp.bfloat16) if position in (4, 6) else leaf
            for position, leaf in enumerate(params)
        )
    )


def pass_on(values):
    return from_behind(values, "section", 1)


def shuffle(first, second, marked, sources):
    member = lax.axis_index("member")
    members = lax.axis_size("member")
    blocks = marked.shape[0]
    capacity = (blocks // 2 + members - 2) // (members - 1)
    slots = members * capacity
    channels = first.shape[0]
    tile_count = first.shape[1] // TILE
    row_groups = second.shape[0] // channels
    column_tiles = channels // TILE
    member_ids = jnp.arange(members, dtype=jnp.int32)
    target = jnp.sum(jnp.where(sources == member, member_ids[None, :], 0), axis=1)
    anchor = lax.dynamic_index_in_dim(sources, member, axis=1, keepdims=False)
    block_ids = jnp.arange(blocks, dtype=jnp.int32)
    earlier = block_ids[:, None] > block_ids[None, :]
    counted = marked[None, :] == 1
    out_rank = jnp.sum(earlier & (target[:, None] == target[None, :]) & counted, axis=1)
    in_rank = jnp.sum(earlier & (anchor[:, None] == anchor[None, :]) & counted, axis=1)
    out_slot = target * capacity + out_rank
    in_slot = jnp.clip(anchor * capacity + in_rank, 0, slots - 1)
    slot_ids = jnp.arange(slots, dtype=jnp.int32)
    matches = (slot_ids[:, None] == out_slot[None, :]) & counted
    slot_used = jnp.any(matches, axis=1)
    slot_block = jnp.sum(jnp.where(matches, block_ids[None, :], 0), axis=1)
    first_tiles = jnp.transpose(first.reshape(channels, tile_count, TILE), (1, 0, 2))
    second_tiles = jnp.transpose(
        second.reshape(row_groups, channels, column_tiles, TILE), (2, 0, 1, 3)
    ).reshape(column_tiles * row_groups, channels, TILE)
    all_tiles = jnp.concatenate([first_tiles, second_tiles], axis=0)
    outgoing = jnp.where(slot_used[:, None, None], jnp.take(all_tiles, slot_block, axis=0), 0.0)
    incoming = lax.all_to_all(
        outgoing.astype(jnp.bfloat16), "member", split_axis=0, concat_axis=0, tiled=True
    ).astype(outgoing.dtype)
    new_tiles = jnp.where(
        (marked == 1)[:, None, None], jnp.take(incoming, in_slot, axis=0), all_tiles
    )
    new_first = jnp.transpose(new_tiles[:tile_count], (1, 0, 2)).reshape(first.shape)
    new_second = jnp.transpose(
        new_tiles[tile_count:].reshape(column_tiles, row_groups, channels, TILE), (1, 2, 0, 3)
    ).reshape(second.shape)
    return (new_first, new_second)


def local(
    inputs,
    cotangent,
    probe,
    dw_kernel,
    dw_bias,
    norm_gain,
    norm_bias,
    w_in,
    b_in,
    w_out,
    b_out,
    layer_scale,
    shuffle_mask,
    source_member,
):
    sections = lax.axis_size("section")
    section = lax.axis_index("section")
    micro_count = inputs.shape[1]
    floats = (
        dw_kernel[0, 0],
        dw_bias[0, 0],
        norm_gain[0, 0],
        norm_bias[0, 0],
        w_in[0, 0],
        b_in[0, 0],
        w_out[0, 0],
        b_out[0, 0],
        layer_scale[0, 0],
    )
    current_params = lowered(floats)
    images = inputs[0]
    slopes = cotangent[0]
    empty = jnp.zeros(images.shape[1:], jnp.bfloat16)
    stored = [empty for position in range(micro_count)]
    received = empty
    ticks = micro_count + sections - 1
    for tick in range(ticks):
        entry = images[min(tick, micro_count - 1)]
        current = jnp.where(section == 0, entry, received)
        which = tick - section
        stored = [
            jnp.where(which == position, current, kept) for position, kept in enumerate(stored)
        ]
        if tick < ticks - 1:
            received = pass_on(block(current_params, current))
    totals = tuple((jnp.zeros(leaf.shape, jnp.float32) for leaf in current_params))
    returning = empty
    for tick in range(ticks):
        which = tick - (sections - 1 - section)
        active = (which >= 0) & (which < micro_count)
        source = stored[0]
        slope = slopes[0]
        position = 1
        source = jnp.where(which == position, stored[position], source)
        slope = jnp.where(which == position, slopes[position], slope)
        slope = jnp.where(section == sections - 1, slope, returning)
        unused, pull = jax.vjp(block, current_params, source)
        delta, back = pull(slope)
        totals = tuple(
            (
                total + jnp.where(active, piece.astype(jnp.float32), 0.0)
                for total, piece in zip(totals, delta)
            )
        )
        if tick < ticks - 1:
            returning = from_behind(back, "section", -1)
    updated = tuple((leaf - learning_rate * total for leaf, total in zip(floats, totals)))
    new_first, new_second = shuffle(updated[4], updated[6], shuffle_mask[0], source_member[0])
    final_params = lowered(
        (
            updated[0],
            updated[1],
            updated[2],
            updated[3],
            new_first,
            updated[5],
            new_second,
            updated[7],
            updated[8],
        )
    )
    received = jnp.zeros(probe.shape[1:], jnp.bfloat16)
    kept_out = received
    for tick in range(sections):
        current = jnp.where(section == 0, probe[0], received)
        result = block(final_params, current)
        kept_out = jnp.where(section == tick, result, kept_out)
        if tick < sections - 1:
            received = pass_on(result)
    return (new_first[None, None], new_second[None, None], kept_out[None, None])


def solution(mesh):
    return jax.shard_map(
        local,
        mesh=mesh,
        in_specs=(
            P("member", None, None, None, None, None),
            P("member", None, None, None, None, None),
            P("member", None, None, None, None),
            P("member", "section", None, None, None),
            P("member", "section", None),
            P("member", "section", None),
            P("member", "section", None),
            P("member", "section", None, None),
            P("member", "section", None),
            P("member", "section", None, None),
            P("member", "section", None),
            P("member", "section", None),
            P("section", None),
            P("section", None, None),
        ),
        out_specs=(
            P("member", "section", None, None),
            P("member", "section", None, None),
            P("member", "section", None, None, None, None),
        ),
        check_vma=False,
    )
```

profile of v0, /device:TPU:1, one launch (start us, length us, event | category | flops | bytes accessed | tf_op | source)
XLA Modules:
  0.0 588.7 jit_solution(15532348930736870082)
XLA Ops:
  9.1 5.6 bitcast_convert_fusion.1
  17.1 7.4 %convolution_add_fusion.21 = f32[196,512]{1,0:T(8,128)} fusion(bf16[2048,512]{1,0:T(8,128)(2,1)} %get-tuple-element.345, bf16[196,512]{1,0:T(8,128)(2,1)S(1)} %reshape.3167, bf16[1,1,512,2048]{3,2,1,0:T(8,128)(2,1)} %get-tuple-element.343, f32[2048]{0:T(1024)S(1)} %bitcast.1718, f32[512]{0:T(512)S(1)} %bitcast.1788), kind=kOutput, calls=%fused_computation.946 | convolution fusion | flops 848676864 | bytes 4806656 | tf_op jit(solution)/shard_map/dot_general | solution.py:58
  43.5 7.4 %convolution_add_fusion.20 = f32[196,512]{1,0:T(8,128)} fusion(bf16[2048,512]{1,0:T(8,128)(2,1)} %get-tuple-element.345, bf16[196,512]{1,0:T(8,128)(2,1)S(1)} %reshape.3169, bf16[1,1,512,2048]{3,2,1,0:T(8,128)(2,1)} %get-tuple-element.343, f32[2048]{0:T(1024)S(1)} %bitcast.1719, f32[512]{0:T(512)S(1)} %bitcast.1789), kind=kOutput, calls=%fused_computation.945 | convolution fusion | flops 848676864 | bytes 4806656 | tf_op jit(solution)/shard_map/dot_general | solution.py:58
  61.9 7.3 %convolution_add_fusion.19 = f32[196,512]{1,0:T(8,128)} fusion(bf16[2048,512]{1,0:T(8,128)(2,1)} %get-tuple-element.345, bf16[196,512]{1,0:T(8,128)(2,1)S(1)} %reshape.3171, bf16[1,1,512,2048]{3,2,1,0:T(8,128)(2,1)} %get-tuple-element.343, f32[2048]{0:T(1024)S(1)} %bitcast.1720, f32[512]{0:T(512)S(1)} %bitcast.1790), kind=kOutput, calls=%fused_computation.944 | convolution fusion | flops 848676864 | bytes 4806656 | tf_op jit(solution)/shard_map/dot_general | solution.py:58
  85.2 7.3 %convolution_add_fusion.18 = f32[196,512]{1,0:T(8,128)} fusion(bf16[2048,512]{1,0:T(8,128)(2,1)} %get-tuple-element.345, bf16[196,512]{1,0:T(8,128)(2,1)} %reshape.3173, bf16[1,1,512,2048]{3,2,1,0:T(8,128)(2,1)} %get-tuple-element.343, f32[2048]{0:T(1024)} %bitcast.1712, f32[512]{0:T(512)} %bitcast.1787), kind=kOutput, calls=%fused_computation.943 | convolution fusion | flops 848676864 | bytes 4806656 | tf_op jit(solution)/shard_map/dot_general | solution.py:58
  129.0 6.5 %multiply_convert_fusion.4 = (bf16[196,2048]{1,0:T(8,128)(2,1)}, f32[196,2048]{1,0:T(8,128)S(1)}, f32[196,2048]{1,0:T(8,128)S(1)}) fusion(f32[2048]{0:T(1024)} %bitcast.1713, bf16[196,512]{1,0:T(8,128)(2,1)} %reshape.3175, bf16[1,1,512,2048]{3,2,1,0:T(8,128)(2,1)} %get-tuple-element.343), kind=kOutput, calls=%fused_computation.790 | convolution fusion | flops 437534720 | bytes 6320128 | tf_op jit(solution)/shard_map/jvp()/dot_general | solution.py:55
  156.8 6.4 %pad_add_fusion.3 = f32[1,20,20,512]{3,2,1,0:T(8,128)S(1)} fusion(f32[1,14,14,512]{3,2,1,0:T(8,128)S(1)} %get-tuple-element.500, f32[1,14,14,512]{3,2,1,0:T(8,128)} %get-tuple-element.501, f32[1,14,14,512]{3,2,1,0:T(8,128)} %get-tuple-element.502, f32[1,14,14,512]{3,2,1,0:T(8,128)} %get-tuple-element.503, f32[1,14,14,512]{3,2,1,0:T(8,128)} %get-tuple-element.504, ...), kind=kLoop, calls=%fused_computation.961 | loop fusion | flops 8601600 | bytes 18079744 | tf_op jit(solution)/shard_map/transpose(jvp())/add_any | solution.py:29
  168.1 7.3 %multiply_convert_fusion.3 = (bf16[196,2048]{1,0:T(8,128)(2,1)S(1)}, f32[196,2048]{1,0:T(8,128)}, f32[196,2048]{1,0:T(8,128)}) fusion(f32[2048]{0:T(1024)} %bitcast.1714, bf16[196,512]{1,0:T(8,128)(2,1)} %reshape.3176, bf16[1,1,512,2048]{3,2,1,0:T(8,128)(2,1)} %get-tuple-element.343), kind=kOutput, calls=%fused_computation.789 | convolution fusion | flops 437534720 | bytes 6320128 | tf_op jit(solution)/shard_map/jvp()/dot_general | solution.py:55
  181.2 7.3 %multiply_convert_fusion.2 = (bf16[196,2048]{1,0:T(8,128)(2,1)S(1)}, f32[196,2048]{1,0:T(8,128)}, f32[196,2048]{1,0:T(8,128)}) fusion(f32[2048]{0:T(1024)} %bitcast.1715, bf16[196,512]{1,0:T(8,128)(2,1)} %reshape.3178, bf16[1,1,512,2048]{3,2,1,0:T(8,128)(2,1)} %get-tuple-element.343), kind=kOutput, calls=%fused_computation.788 | convolution fusion | flops 437534720 | bytes 6320128 | tf_op jit(solution)/shard_map/jvp()/dot_general | solution.py:55
  194.2 7.5 %multiply_convert_fusion.1 = (bf16[196,2048]{1,0:T(8,128)(2,1)S(1)}, f32[196,2048]{1,0:T(8,128)}, f32[196,2048]{1,0:T(8,128)}) fusion(f32[2048]{0:T(1024)} %bitcast.1716, bf16[196,512]{1,0:T(8,128)(2,1)} %reshape.3180, bf16[1,1,512,2048]{3,2,1,0:T(8,128)(2,1)} %get-tuple-element.343), kind=kOutput, calls=%fused_computation.787 | convolution fusion | flops 437534720 | bytes 6320128 | tf_op jit(solution)/shard_map/jvp()/dot_general | solution.py:55
  207.4 7.3 %multiply_convert_fusion = (bf16[196,2048]{1,0:T(8,128)(2,1)S(1)}, f32[196,2048]{1,0:T(8,128)}, f32[196,2048]{1,0:T(8,128)}) fusion(f32[2048]{0:T(1024)} %bitcast.1717, bf16[196,512]{1,0:T(8,128)(2,1)} %reshape.3182, bf16[1,1,512,2048]{3,2,1,0:T(8,128)(2,1)} %get-tuple-element.343), kind=kOutput, calls=%fused_computation.786 | convolution fusion | flops 437534720 | bytes 6320128 | tf_op jit(solution)/shard_map/jvp()/dot_general | solution.py:55
  254.4 6.3 %pad_add_fusion.2 = f32[1,20,20,512]{3,2,1,0:T(8,128)S(1)} fusion(f32[1,14,14,512]{3,2,1,0:T(8,128)S(1)} %get-tuple-element.455, f32[1,14,14,512]{3,2,1,0:T(8,128)S(1)} %get-tuple-element.456, f32[1,14,14,512]{3,2,1,0:T(8,128)} %get-tuple-element.457, f32[1,14,14,512]{3,2,1,0:T(8,128)} %get-tuple-element.458, f32[1,14,14,512]{3,2,1,0:T(8,128)} %get-tuple-element.459, ...), kind=kLoop, calls=%fused_computation.960 | loop fusion | flops 8601600 | bytes 18079744 | tf_op jit(solution)/shard_map/transpose(jvp())/add_any | solution.py:29
  296.9 6.2 %pad_add_fusion.1 = f32[1,20,20,512]{3,2,1,0:T(8,128)S(1)} fusion(f32[1,14,14,512]{3,2,1,0:T(8,128)S(1)} %get-tuple-element.410, f32[1,14,14,512]{3,2,1,0:T(8,128)S(1)} %get-tuple-element.411, f32[1,14,14,512]{3,2,1,0:T(8,128)S(1)} %copy-done.65, f32[1,14,14,512]{3,2,1,0:T(8,128)} %get-tuple-element.413, f32[1,14,14,512]{3,2,1,0:T(8,128)} %get-tuple-element.414, ...), kind=kLoop, calls=%fused_computation.959 | loop fusion | flops 8601600 | bytes 18079744 | tf_op jit(solution)/shard_map/transpose(jvp())/add_any | solution.py:29
  336.8 6.2 %pad_add_fusion = f32[1,20,20,512]{3,2,1,0:T(8,128)S(1)} fusion(f32[1,14,14,512]{3,2,1,0:T(8,128)S(1)} %get-tuple-element.365, f32[1,14,14,512]{3,2,1,0:T(8,128)S(1)} %get-tuple-element.366, f32[1,14,14,512]{3,2,1,0:T(8,128)S(1)} %get-tuple-element.367, f32[1,14,14,512]{3,2,1,0:T(8,128)S(1)} %copy-done.64, f32[1,14,14,512]{3,2,1,0:T(8,128)} %get-tuple-element.369, ...), kind=kLoop, calls=%fused_computation.958 | loop fusion | flops 8601600 | bytes 18079744 | tf_op jit(solution)/shard_map/transpose(jvp())/add_any | solution.py:29
  358.8 6.7 %fusion = f32[64,16,8,128]{3,2,1,0:T(8,128)S(1)} fusion(f32[1,1,512,2048]{3,2,1,0:T(8,128)} %param.21, bf16[512,2048]{1,0:T(8,128)(2,1)} %fusion.1559, bf16[512,2048]{1,0:T(8,128)(2,1)} %fusion.1560, bf16[512,2048]{1,0:T(8,128)(2,1)} %fusion.1561, bf16[512,2048]{1,0:T(8,128)(2,1)S(1)} %copy-done.42, pred[]{:T(512)S(6)} %and.72, pred[]{:T(512)S(6)} %and.71, ...), kind=kOutput, calls=%fused_computation.635 | convolution fusion | flops 427819008 | bytes 17780740 | tf_op jit(solution)/shard_map/transpose(jvp())/dot_general | solution.py:55
  393.7 5.9 %all-to-all-start = ((bf16[24,512,128]{2,1,0:T(8,128)(2,1)}), bf16[24,512,128]{2,1,0:T(8,128)(2,1)}, u32[]{:S(2)}, u32[]{:S(2)}) async-start(bf16[24,512,128]{2,1,0:T(8,128)(2,1)} %select_convert_fusion), calls=%async_computation | async-start | bytes 6291456 | tf_op jit(solution)/shard_map/all_to_all | solution.py:105
  414.2 53.6 %all-to-all-done = bf16[24,512,128]{2,1,0:T(8,128)(2,1)} async-done(((bf16[24,512,128]{2,1,0:T(8,128)(2,1)}), bf16[24,512,128]{2,1,0:T(8,128)(2,1)}, u32[]{:S(2)}, u32[]{:S(2)}) %all-to-all-start) | async-done | bytes 3145760 | tf_op jit(solution)/shard_map/all_to_all | solution.py:105
  473.1 7.2 %gather_fusion.1 = f32[32,512,128]{2,1,0:T(8,128)} fusion(f32[24,512,128]{2,1,0:T(8,128)} %convert_element_type.647, s32[1024]{0:T(1024)} %pad_clamp_fusion), kind=kCustom, calls=%fused_computation.1 | custom fusion | bytes 16777344 | tf_op jit(solution)/shard_map/jit(_take)/gather | solution.py:109
  480.3 7.1 %select_select_fusion = f32[32,512,128]{2,1,0:T(8,128)S(1)} fusion(f32[32,512,128]{2,1,0:T(8,128)} %gather_fusion.1, pred[32]{0:T(512)(128)(4,1)S(1)} %copy-done.538, pred[32]{0:T(512)(128)(4,1)S(1)} %copy-done.537, f32[16,512,128]{2,1,0:T(8,128)} %bitcast.629, f32[16,512,128]{2,1,0:T(8,128)} %bitcast.626), kind=kLoop, calls=%fused_computation.627 | loop fusion | flops 6291456 | bytes 25165888 | tf_op jit(solution)/shard_map/jit(_where)/select_n | solution.py:108
  498.8 6.8 %fusion.152 = f32[196,512]{1,0:T(8,128)S(1)} fusion(bf16[256,8,4,128]{3,2,1,0:T(4,128)(2,1)} %bitcast.635, bf16[196,512]{1,0:T(8,128)(2,1)S(1)} %reshape.3192, bf16[512,2048]{0,1:T(8,128)(2,1)} %bitcast.639, f32[2048]{0:T(1024)S(1)} %multiply_subtract_fusion.1, f32[512]{0:T(512)S(1)} %multiply_subtract_fusion.2), kind=kOutput, calls=%fused_computation.933 | convolution fusion | flops 848676864 | bytes 4806656 | tf_op jit(solution)/shard_map/dot_general | solution.py:58
  516.2 6.9 %fusion.155 = f32[196,512]{1,0:T(8,128)} fusion(bf16[256,8,4,128]{3,2,1,0:T(4,128)(2,1)S(1)} %bitcast.636, bf16[196,512]{1,0:T(8,128)(2,1)S(1)} %reshape.3194, bf16[512,2048]{0,1:T(8,128)(2,1)} %bitcast.640, f32[2048]{0:T(1024)S(1)} %copy-done.527, f32[512]{0:T(512)S(1)} %copy-done.550), kind=kOutput, calls=%fused_computation.934 | convolution fusion | flops 848676864 | bytes 4806656 | tf_op jit(solution)/shard_map/dot_general | solution.py:58
  537.9 6.8 %fusion.158 = f32[196,512]{1,0:T(8,128)} fusion(bf16[256,8,4,128]{3,2,1,0:T(4,128)(2,1)S(1)} %bitcast.637, bf16[196,512]{1,0:T(8,128)(2,1)S(1)} %reshape.3196, bf16[512,2048]{0,1:T(8,128)(2,1)} %bitcast.641, f32[2048]{0:T(1024)S(1)} %copy-done.528, f32[512]{0:T(512)S(1)} %copy-done.551), kind=kOutput, calls=%fused_computation.935 | convolution fusion | flops 848676864 | bytes 4806656 | tf_op jit(solution)/shard_map/dot_general | solution.py:58
  551.6 6.8 %copy.95 = f32[4,4,512,128]{3,0,2,1:T(4,128)} copy(f32[4,4,512,128]{3,2,1,0:T(8,128)} %bitcast.631) | data formatting | bytes 8388608 | tf_op jit(solution)/shard_map/reshape | solution.py:113
  579.7 6.9 %fusion.161 = f32[196,512]{1,0:T(8,128)} fusion(bf16[256,8,4,128]{3,2,1,0:T(4,128)(2,1)S(1)} %bitcast.638, bf16[196,512]{1,0:T(8,128)(2,1)S(1)} %reshape.3198, bf16[512,2048]{0,1:T(8,128)(2,1)} %bitcast.642, f32[2048]{0:T(1024)} %copy-done.526, f32[512]{0:T(512)} %copy-done.549), kind=kOutput, calls=%fused_computation.936 | convolution fusion | flops 848676864 | bytes 4806656 | tf_op jit(solution)/shard_map/dot_general | solution.py:58
  (1389 shorter events, 368.8 us)
Async XLA Ops:
  26.3 10.2 %collective-permute-start = (bf16[1,14,14,512]{3,2,1,0:T(8,128)(2,1)}, bf16[1,14,14,512]{3,2,1,0:T(8,128)(2,1)}, u32[]{:S(2)}, u32[]{:S(2)}) collective-permute-start(bf16[1,14,14,512]{3,2,1,0:T(8,128)(2,1)} %add_convert_fusion.19), channel_id=1, source_target_pairs={{0,1},{1,2},{2,3},{4,5},{5,6},{6,7},{8,9},{9,10},{10,11},{12,13},{... | collective-permute-start | bytes 602120 | tf_op jit(solution)/shard_map/ppermute | solution.py:16
  52.3 4.9 collective-permute-start.1
  72.5 7.3 %collective-permute-start.2 = (bf16[1,14,14,512]{3,2,1,0:T(8,128)(2,1)S(1)}, bf16[1,14,14,512]{3,2,1,0:T(8,128)(2,1)S(1)}, u32[]{:S(2)}, u32[]{:S(2)}) collective-permute-start(bf16[1,14,14,512]{3,2,1,0:T(8,128)(2,1)S(1)} %add_convert_fusion.15), channel_id=1, source_target_pairs={{0,1},{1,2},{2,3},{4,5},{5,6},{6,7},{8,9},{9,10},{10,11},{12,13},{... | collective-permute-start | bytes 602120 | tf_op jit(solution)/shard_map/ppermute | solution.py:16
  95.5 7.3 %collective-permute-start.3 = (bf16[1,14,14,512]{3,2,1,0:T(8,128)(2,1)S(1)}, bf16[1,14,14,512]{3,2,1,0:T(8,128)(2,1)S(1)}, u32[]{:S(2)}, u32[]{:S(2)}) collective-permute-start(bf16[1,14,14,512]{3,2,1,0:T(8,128)(2,1)S(1)} %add_convert_fusion.13), channel_id=1, source_target_pairs={{0,1},{1,2},{2,3},{4,5},{5,6},{6,7},{8,9},{9,10},{10,11},{12,13},{... | collective-permute-start | bytes 602120 | tf_op jit(solution)/shard_map/ppermute | solution.py:16
  164.3 59.3 %collective-permute-start.4 = (bf16[1,14,14,512]{3,2,1,0:T(8,128)(2,1)}, bf16[1,14,14,512]{3,2,1,0:T(8,128)(2,1)}, u32[]{:S(2)}, u32[]{:S(2)}) collective-permute-start(bf16[1,14,14,512]{3,2,1,0:T(8,128)(2,1)} %fusion.1223), channel_id=1, source_target_pairs={{1,0},{2,1},{3,2},{5,4},{6,5},{7,6},{9,8},{10,9},{11,10},{13,12},{... | collective-permute-start | bytes 602120 | tf_op jit(solution)/shard_map/ppermute | solution.py:16
  261.2 8.2 %collective-permute-start.5 = (bf16[1,14,14,512]{3,2,1,0:T(8,128)(2,1)S(1)}, bf16[1,14,14,512]{3,2,1,0:T(8,128)(2,1)S(1)}, u32[]{:S(2)}, u32[]{:S(2)}) collective-permute-start(bf16[1,14,14,512]{3,2,1,0:T(8,128)(2,1)S(1)} %fusion.440), channel_id=1, source_target_pairs={{1,0},{2,1},{3,2},{5,4},{6,5},{7,6},{9,8},{10,9},{11,10},{13,12},{... | collective-permute-start | bytes 602120 | tf_op jit(solution)/shard_map/ppermute | solution.py:16
  303.6 7.5 %collective-permute-start.6 = (bf16[1,14,14,512]{3,2,1,0:T(8,128)(2,1)S(1)}, bf16[1,14,14,512]{3,2,1,0:T(8,128)(2,1)S(1)}, u32[]{:S(2)}, u32[]{:S(2)}) collective-permute-start(bf16[1,14,14,512]{3,2,1,0:T(8,128)(2,1)S(1)} %fusion.442), channel_id=1, source_target_pairs={{1,0},{2,1},{3,2},{5,4},{6,5},{7,6},{9,8},{10,9},{11,10},{13,12},{... | collective-permute-start | bytes 602120 | tf_op jit(solution)/shard_map/ppermute | solution.py:16
  343.4 7.5 %collective-permute-start.7 = (bf16[1,14,14,512]{3,2,1,0:T(8,128)(2,1)S(1)}, bf16[1,14,14,512]{3,2,1,0:T(8,128)(2,1)S(1)}, u32[]{:S(2)}, u32[]{:S(2)}) collective-permute-start(bf16[1,14,14,512]{3,2,1,0:T(8,128)(2,1)S(1)} %fusion.444), channel_id=1, source_target_pairs={{1,0},{2,1},{3,2},{5,4},{6,5},{7,6},{9,8},{10,9},{11,10},{13,12},{... | collective-permute-start | bytes 602120 | tf_op jit(solution)/shard_map/ppermute | solution.py:16
  393.7 74.1 %all-to-all-start = ((bf16[24,512,128]{2,1,0:T(8,128)(2,1)}), bf16[24,512,128]{2,1,0:T(8,128)(2,1)}, u32[]{:S(2)}, u32[]{:S(2)}) async-start(bf16[24,512,128]{2,1,0:T(8,128)(2,1)} %select_convert_fusion), calls=%async_computation | async-start | bytes 6291456 | tf_op jit(solution)/shard_map/all_to_all | solution.py:105
  409.2 102.1 %copy-start.369 = (f32[1,1,512]{2,1,0:T(1,128)}, f32[1,1,512]{2,1,0:T(1,128)S(1)}, u32[]{:S(2)}) copy-start(f32[1,1,512]{2,1,0:T(1,128)S(1)} %get-tuple-element.556) | copy-start | bytes 6148
  409.2 102.1 %copy-start.371 = (f32[1,1,512]{2,1,0:T(1,128)}, f32[1,1,512]{2,1,0:T(1,128)S(1)}, u32[]{:S(2)}) copy-start(f32[1,1,512]{2,1,0:T(1,128)S(1)} %get-tuple-element.557) | copy-start | bytes 6148
  409.2 102.1 %copy-start.373 = (f32[1,1,512]{2,1,0:T(1,128)}, f32[1,1,512]{2,1,0:T(1,128)S(1)}, u32[]{:S(2)}) copy-start(f32[1,1,512]{2,1,0:T(1,128)S(1)} %get-tuple-element.558) | copy-start | bytes 6148
  409.2 102.1 %copy-start.376 = (f32[1,1,512]{2,1,0:T(1,128)}, f32[1,1,512]{2,1,0:T(1,128)S(1)}, u32[]{:S(2)}) copy-start(f32[1,1,512]{2,1,0:T(1,128)S(1)} %get-tuple-element.559) | copy-start | bytes 6148
  409.2 102.1 %copy-start.379 = (f32[1,1,512]{2,1,0:T(1,128)}, f32[1,1,512]{2,1,0:T(1,128)S(1)}, u32[]{:S(2)}) copy-start(f32[1,1,512]{2,1,0:T(1,128)S(1)} %get-tuple-element.560) | copy-start | bytes 6148
  409.2 102.1 %copy-start.382 = (f32[1,1,512]{2,1,0:T(1,128)}, f32[1,1,512]{2,1,0:T(1,128)S(1)}, u32[]{:S(2)}) copy-start(f32[1,1,512]{2,1,0:T(1,128)S(1)} %get-tuple-element.561) | copy-start | bytes 6148
  409.2 102.1 %copy-start.385 = (f32[1,1,512]{2,1,0:T(1,128)}, f32[1,1,512]{2,1,0:T(1,128)S(1)}, u32[]{:S(2)}) copy-start(f32[1,1,512]{2,1,0:T(1,128)S(1)} %get-tuple-element.562) | copy-start | bytes 6148
  409.2 102.1 %copy-start.388 = (f32[1,1,512]{2,1,0:T(1,128)}, f32[1,1,512]{2,1,0:T(1,128)S(1)}, u32[]{:S(2)}) copy-start(f32[1,1,512]{2,1,0:T(1,128)S(1)} %get-tuple-element.563) | copy-start | bytes 6148
  409.2 102.1 %copy-start.391 = (f32[1,1,512]{2,1,0:T(1,128)}, f32[1,1,512]{2,1,0:T(1,128)S(1)}, u32[]{:S(2)}) copy-start(f32[1,1,512]{2,1,0:T(1,128)S(1)} %get-tuple-element.564) | copy-start | bytes 6148
  409.2 102.1 %copy-start.394 = (f32[1,1,512]{2,1,0:T(1,128)}, f32[1,1,512]{2,1,0:T(1,128)S(1)}, u32[]{:S(2)}) copy-start(f32[1,1,512]{2,1,0:T(1,128)S(1)} %get-tuple-element.565) | copy-start | bytes 6148
  413.7 102.3 %copy-start.463 = (f32[512]{0:T(512)}, f32[512]{0:T(512)S(1)}, u32[]{:S(2)}) copy-start(f32[512]{0:T(512)S(1)} %multiply_subtract_fusion.4) | copy-start | bytes 6148
  413.7 102.2 %copy-start.468 = (f32[512]{0:T(512)}, f32[512]{0:T(512)S(1)}, u32[]{:S(2)}) copy-start(f32[512]{0:T(512)S(1)} %multiply_subtract_fusion.3) | copy-start | bytes 6148
  505.8 5.4 collective-permute-start.8
  525.3 7.5 %collective-permute-start.9 = (bf16[1,14,14,512]{3,2,1,0:T(8,128)(2,1)S(1)}, bf16[1,14,14,512]{3,2,1,0:T(8,128)(2,1)S(1)}, u32[]{:S(2)}, u32[]{:S(2)}) collective-permute-start(bf16[1,14,14,512]{3,2,1,0:T(8,128)(2,1)S(1)} %add_convert_fusion.4), channel_id=1, source_target_pairs={{0,1},{1,2},{2,3},{4,5},{5,6},{6,7},{8,9},{9,10},{10,11},{12,13},{... | collective-permute-start | bytes 602120 | tf_op jit(solution)/shard_map/ppermute | solution.py:16
  547.2 27.8 %collective-permute-start.10 = (bf16[1,14,14,512]{3,2,1,0:T(8,128)(2,1)}, bf16[1,14,14,512]{3,2,1,0:T(8,128)(2,1)S(1)}, u32[]{:S(2)}, u32[]{:S(2)}) collective-permute-start(bf16[1,14,14,512]{3,2,1,0:T(8,128)(2,1)} %add_convert_fusion.2), channel_id=1, source_target_pairs={{0,1},{1,2},{2,3},{4,5},{5,6},{6,7},{8,9},{9,10},{10,11},{12,13},{... | collective-permute-start | bytes 602120 | tf_op jit(solution)/shard_map/ppermute | solution.py:16
  (550 other events, 5736.4 us)
where the time goes:
time: 598 us; the launch traced here: 589 us
  other arithmetic  196 us (33%)
  matrix products  156 us (26%)
  local copies, waits for them, and re-layouts  110 us (18%)
  waiting for transfers between devices  74.6 us (12%)
  starting transfers between devices  42.4 us (7%)
  between operations  9.23 us (2%)
    dot_general x23, matrix products, block(): jnp.dot(hidden, second_weight, preferred_element_type=jnp.float32)  95.9 us
    dot_general x15, matrix products, block(): jnp.dot(rows, first_weight, preferred_element_type=jnp.float32) + first_bias  60.3 us
    all_to_all x1, waiting for transfers between devices, shuffle(): lax.all_to_all(outgoing.astype(jnp.bfloat16), 'member', split_axis=0, con...  53.6 us
    reduce_sum x13, other arithmetic, block(): center = jnp.mean(spread, axis=-1, keepdims=True)  51.4 us
    ppermute x11, starting transfers between devices, from_behind(): lax.ppermute(value, axis, [(source, source + steps) for source in range(f...  36.5 us
    reduce_sum x15, other arithmetic, depthwise(): kernel[row_off, col_off]  28.9 us
    add_any x4, other arithmetic, depthwise(): padded[:, row_off:row_off + height, col_off:col_off + width, :]  25 us
    unnamed x1126, local copies, waits for them, and re-layouts  21.3 us
  transfers between devices with their start and end apart: 12, of which 9 were waited for; matrix products, arithmetic and copies ran while one was open for 18% of the time, Pallas kernels for 0%

commit v1 on v0

v1 whole, which is shorter than its diff:
```python
import functools
import math

import jax
import jax.numpy as jnp
from jax import lax
from jax.experimental import pallas as pl
from jax.experimental.pallas import tpu as pltpu
from jax.sharding import PartitionSpec as P

TILE = 128
learning_rate = 0.001
norm_epsilon = 1e-06
F32 = jnp.float32
BF16 = jnp.bfloat16
EDGE = 8
REACH = 3
TAPS = 2 * REACH + 1
VMEM_LIMIT = 40 * 1024 * 1024

ERF_TOP = (
    0.00022905065861350646,
    0.0034082910107109506,
    0.050955695062380861,
    0.18520832239976145,
    1.128379143519084,
)
ERF_LOW = (
    -1.1791602954361697e-7,
    0.000023547966471313185,
    0.0010179625278914885,
    0.014070470171167667,
    0.11098505178285362,
    0.49746925110067538,
    1.0,
)


def erf(value):
    value = jnp.clip(value, -3.832506856900711, 3.832506856900711)
    square = value * value
    top = jnp.full_like(square, ERF_TOP[0])
    for term in ERF_TOP[1:]:
        top = top * square + term
    low = jnp.full_like(square, ERF_LOW[0])
    for term in ERF_LOW[1:]:
        low = low * square + term
    return value * top / low


def whole(array):
    rank = len(array.shape)
    return pl.BlockSpec(array.shape, lambda *args: (0,) * rank)


def lanes(index):
    return pl.ds(pl.multiple_of(index * TILE, TILE), TILE)


def shaped(shape, dtype):
    return jax.ShapeDtypeStruct(shape, dtype)


def convolve(padded, chunk, kernel_ref, height, width, flip, store):
    totals = [None] * height
    for col in range(TAPS):
        taps = []
        for row in range(TAPS):
            at = row * TAPS + col
            if flip:
                at = TAPS * TAPS - 1 - at
            taps.append(kernel_ref[at : at + 1, lanes(chunk)])
        for line in range(height + TAPS - 1):
            values = padded[chunk, line, pl.ds(EDGE - REACH + col, width), :]
            for row in range(TAPS):
                out = line - row
                if 0 <= out < height:
                    term = values * taps[row]
                    totals[out] = term if totals[out] is None else totals[out] + term
    for out in range(height):
        store(out, totals[out])


def fill_padded(padded, maps):
    height, width, channels = maps.shape
    padded[...] = jnp.zeros(padded.shape, F32)
    for chunk in range(channels // TILE):
        padded[chunk, REACH : REACH + height, EDGE : EDGE + width, :] = maps[
            :, :, chunk * TILE : (chunk + 1) * TILE
        ]


def real_columns(shape, side):
    return lax.broadcasted_iota(jnp.int32, shape, 1) < side


def normalise(spread):
    center = jnp.mean(spread, axis=-1, keepdims=True)
    offset = spread - center
    variance = jnp.mean(offset * offset, axis=-1, keepdims=True)
    inverse = lax.rsqrt(variance + norm_epsilon)
    return offset * inverse, inverse


def forward_core(side, vectors, widened, padded, spread, total, weights, n_ref, hidden_store):
    kernel_ref, bias_ref, gain_ref, shift_ref, first_bias_ref, second_bias_ref, scale_ref = vectors
    height, width, channels = widened.shape
    rows = height * width
    hid = first_bias_ref.shape[1]
    fill_padded(padded, widened)

    def conv_body(chunk, carry):
        bias = bias_ref[0:1, lanes(chunk)]

        def store(out, value):
            spread[out * width : (out + 1) * width, lanes(chunk)] = value + bias

        convolve(padded, chunk, kernel_ref, height, width, False, store)
        return carry

    lax.fori_loop(0, channels // TILE, conv_body, 0)
    hat, inverse = normalise(spread[...])
    n_ref[...] = (hat * gain_ref[...] + shift_ref[...]).astype(BF16)
    total[...] = jnp.zeros(total.shape, F32)

    def mix_body(piece, carry):
        first, second = weights(piece)
        at = pl.ds(pl.multiple_of(piece * channels, channels), channels)
        pre = jnp.dot(n_ref[...], first, preferred_element_type=F32) + first_bias_ref[:, at]
        below = 0.5 + 0.5 * erf(pre * math.sqrt(0.5))
        hidden = (pre * below).astype(BF16)
        hidden_store(at, hidden, pre, below)
        total[...] += jnp.dot(hidden, second, preferred_element_type=F32)
        return carry

    lax.fori_loop(0, hid // channels, mix_body, 0)
    mixed = total[...] + second_bias_ref[...]
    result = widened + (scale_ref[...] * mixed).reshape(height, width, channels)
    result = jnp.where(real_columns(result.shape, side), result, 0.0)
    return result, mixed, hat, inverse


def is_active(sec_ref, tick, count):
    which = tick - sec_ref[0]
    return (which >= 0) & (which < count)


def slot_of(which, count):
    return jnp.where((which >= 0) & (which < count), which, count)


def train_kernel(tick, micro, side, kept, sec_ref, image_ref, received_ref, *refs):
    vectors, (first_ref, second_ref) = refs[:7], refs[7:9]
    refs = refs[9 + kept :]
    y_ref, x_ref, hat_ref, inverse_ref, n_ref, h_ref, slope_ref, mixed_ref = refs[:8]
    padded, spread, total = refs[8:]

    @pl.when(is_active(sec_ref, tick, micro))
    def _():
        channels = x_ref.shape[-1]
        entry = jnp.where(sec_ref[0] == 0, image_ref[0].astype(F32), received_ref[...].astype(F32))
        x_ref[0] = entry.astype(BF16)

        def weights(piece):
            at = pl.ds(pl.multiple_of(piece * channels, channels), channels)
            return first_ref[:, at], second_ref[at, :]

        def hidden_store(at, hidden, pre, below):
            h_ref[0, :, at] = hidden
            density = jnp.exp(-0.5 * pre * pre) * (1.0 / math.sqrt(2.0 * math.pi))
            slope_ref[0, :, at] = (below + pre * density).astype(BF16)

        result, mixed, hat, inverse = forward_core(
            side, vectors, entry, padded, spread, total, weights, n_ref.at[0], hidden_store
        )
        y_ref[...] = result.astype(BF16)
        hat_ref[0] = hat
        inverse_ref[0] = jnp.broadcast_to(inverse, inverse_ref.shape[1:])
        mixed_ref[0] = mixed


def probe_kernel(tick, side, sec_ref, marked_ref, slot_ref, image_ref, received_ref, *refs):
    vectors, (own_ref, arrived_ref) = refs[:7], refs[7:9]
    y_ref, padded, spread, total, n_ref = refs[9:]

    @pl.when(sec_ref[0] == tick)
    def _():
        channels = y_ref.shape[-1]
        tiles = channels // TILE
        groups = vectors[4].shape[1] // channels
        entry = image_ref[...] if tick == 0 else received_ref[...]

        def tile(block):
            taken = marked_ref[block] == 1
            return jnp.where(taken, arrived_ref[slot_ref[block]], own_ref[block])

        def weights(piece):
            first = [tile(piece * tiles + item) for item in range(tiles)]
            second = [tile(groups * tiles + item * groups + piece) for item in range(tiles)]
            return jnp.concatenate(first, axis=1), jnp.concatenate(second, axis=1)

        result, mixed, hat, inverse = forward_core(
            side,
            vectors,
            entry.astype(F32),
            padded,
            spread,
            total,
            weights,
            n_ref,
            lambda at, hidden, pre, below: None,
        )
        y_ref[...] = result.astype(BF16)


def back_kernel(tick, micro, side, sections, kept, sec_ref, slope_in_ref, returned_ref, *refs):
    kernel_ref, gain_ref, scale_ref, first_ref, second_ref = refs[:5]
    hat_ref, inverse_ref, slope_ref = refs[5:8]
    refs = refs[8 + kept :]
    dx_ref, dy_ref, dmix_ref, dpre_ref, dn_ref, dspread_ref = refs[:6]
    padded, total, conv_out = refs[6:]
    which = tick - (sections - 1 - sec_ref[0])

    @pl.when((which >= 0) & (which < micro))
    def _():
        height, width, channels = dx_ref.shape
        rows = height * width
        hid = slope_ref.shape[-1]
        dy = jnp.where(
            sec_ref[0] == sections - 1, slope_in_ref[0].astype(F32), returned_ref[...].astype(F32)
        )
        flat = dy.reshape(rows, channels)
        dy_ref[0] = flat.astype(BF16)
        dmix_ref[0] = (flat * scale_ref[...]).astype(BF16)
        total[...] = jnp.zeros(total.shape, F32)
        contract = (((1,), (1,)), ((), ()))

        def body(piece, carry):
            at = pl.ds(pl.multiple_of(piece * channels, channels), channels)
            dh = lax.dot_general(dmix_ref[0], second_ref[at, :], contract, preferred_element_type=F32)
            dpre = (dh * slope_ref[0, :, at].astype(F32)).astype(BF16)
            dpre_ref[0, :, at] = dpre
            total[...] += lax.dot_general(
                dpre, first_ref[:, at], contract, preferred_element_type=F32
            )
            return carry

        lax.fori_loop(0, hid // channels, body, 0)
        dn = total[...]
        dn_ref[0] = dn.astype(BF16)
        hat = hat_ref[0]
        dhat = dn * gain_ref[...]
        mean = jnp.mean(dhat, axis=-1, keepdims=True)
        along = jnp.mean(dhat * hat, axis=-1, keepdims=True)
        dspread = inverse_ref[0, :, 0:1] * (dhat - mean - hat * along)
        dspread_ref[0] = dspread
        if tick < micro + sections - 2:
            fill_padded(padded, dspread.reshape(height, width, channels))

            def conv_body(chunk, carry):
                def store(out, value):
                    conv_out[out, :, lanes(chunk)] = value

                convolve(padded, chunk, kernel_ref, height, width, True, store)
                return carry

            lax.fori_loop(0, channels // TILE, conv_body, 0)
            dx = dy + conv_out[...]
            dx = jnp.where(real_columns(dx.shape, side), dx, 0.0)
            dx_ref[...] = dx.astype(BF16)


def small_kernel(micro, *refs):
    (kernel_ref, bias_ref, gain_ref, shift_ref, first_bias_ref, second_bias_ref, scale_ref) = refs[:7]
    x_ref, hat_ref, mixed_ref, dy_ref, dpre_ref, dn_ref, dspread_ref = refs[7:14]
    outs = refs[14:21]
    padded = refs[21]
    height, width, channels = x_ref.shape[1:]

    def total(values):
        return jnp.sum(values, axis=0, keepdims=True)

    def chunk_body(chunk, carry):
        at = lanes(chunk)
        scale = scale_ref[0:1, at]
        sums = [0.0] * 5
        for item in range(micro):
            dy = dy_ref[item, :, at].astype(F32)
            dn = dn_ref[item, :, at].astype(F32)
            sums[0] += total(dspread_ref[item, :, at])
            sums[1] += total(dn * hat_ref[item, :, at])
            sums[2] += total(dn)
            sums[3] += total(dy)
            sums[4] += total(dy * mixed_ref[item, :, at])
        outs[1][0:1, at] = bias_ref[0:1, at] - learning_rate * sums[0]
        outs[2][0:1, at] = gain_ref[0:1, at] - learning_rate * sums[1]
        outs[3][0:1, at] = shift_ref[0:1, at] - learning_rate * sums[2]
        outs[5][0:1, at] = second_bias_ref[0:1, at] - learning_rate * (scale * sums[3])
        outs[6][0:1, at] = scale - learning_rate * sums[4]
        padded[...] = jnp.zeros(padded.shape, F32)
        for item in range(micro):
            padded[item, REACH : REACH + height, EDGE : EDGE + width, :] = x_ref[
                item, :, :, at
            ].astype(F32)
        for col in range(TAPS):
            for row in range(TAPS):
                acc = None
                for item in range(micro):
                    for out in range(height):
                        term = (
                            padded[item, out + row, pl.ds(EDGE - REACH + col, width), :]
                            * dspread_ref[item, out * width : (out + 1) * width, at]
                        )
                        acc = term if acc is None else acc + term
                tap = row * TAPS + col
                outs[0][tap : tap + 1, at] = kernel_ref[tap : tap + 1, at] - learning_rate * total(acc)
        return carry

    lax.fori_loop(0, channels // TILE, chunk_body, 0)
    hid = first_bias_ref.shape[1]

    def bias_body(piece, carry):
        at = lanes(piece)
        acc = 0.0
        for item in range(micro):
            acc += total(dpre_ref[item, :, at].astype(F32))
        outs[4][0:1, at] = first_bias_ref[0:1, at] - learning_rate * acc
        return carry

    lax.fori_loop(0, hid // TILE, bias_body, 0)


def weight_step(first_tiles, groups, block, n_ref, dpre_ref, h_ref, dmix_ref, first_ref, second_ref, emit):
    rows = n_ref.shape[0] * n_ref.shape[1]
    channels = n_ref.shape[2]
    contract = (((0,), (0,)), ((), ()))

    @pl.when(block < first_tiles)
    def _():
        grad = lax.dot_general(
            n_ref[...].reshape(rows, channels),
            dpre_ref[...].reshape(rows, TILE),
            contract,
            preferred_element_type=F32,
        )
        emit(True, first_ref[...] - learning_rate * grad)

    @pl.when(block >= first_tiles)
    def _():
        group = lax.rem(block - first_tiles, groups)
        at = pl.ds(pl.multiple_of(group * channels, channels), channels)
        grad = lax.dot_general(
            h_ref[:, :, at].reshape(rows, channels),
            dmix_ref[...].reshape(rows, TILE),
            contract,
            preferred_element_type=F32,
        )
        emit(False, second_ref[...] - learning_rate * grad)


def send_kernel(first_tiles, groups, order_ref, slot_ref, n, dpre, h, dmix, first, second, send_ref):
    step = pl.program_id(0)

    def emit(is_first, updated):
        send_ref[0] = updated.astype(BF16)

    weight_step(first_tiles, groups, order_ref[step], n, dpre, h, dmix, first, second, emit)


def keep_kernel(
    first_tiles, groups, order_ref, edge_ref, n, dpre, h, dmix, first, second, own_ref, new_first, new_second
):
    step = pl.program_id(0)

    def emit(is_first, updated):
        own_ref[0] = updated.astype(BF16)
        if is_first:
            new_first[...] = updated
        else:
            new_second[...] = updated

    weight_step(first_tiles, groups, order_ref[step], n, dpre, h, dmix, first, second, emit)


def place_kernel(
    first_tiles, order_ref, edge_ref, slot_ref, arrived_ref, old_first, old_second, new_first, new_second
):
    step = pl.program_id(0)
    block = order_ref[step]

    @pl.when(step == 0)
    def _():
        new_first[...] = old_first[...]
        new_second[...] = old_second[...]

    @pl.when(block < first_tiles)
    def _():
        new_first[...] = arrived_ref[0].astype(F32)

    @pl.when(block >= first_tiles)
    def _():
        new_second[...] = arrived_ref[0].astype(F32)


def params_of(limit=VMEM_LIMIT):
    return pltpu.CompilerParams(vmem_limit_bytes=limit)


def cost(flops, read):
    return pl.CostEstimate(flops=flops, bytes_accessed=read, transcendentals=0)


def any_spec():
    return pl.BlockSpec(memory_space=pl.ANY)


def train_step(tick, micro, side, sec, images, received, vectors, weights, saved):
    height, width, channels = received.shape
    rows = height * width
    hid = vectors[4].shape[1]

    def slotted(*shape):
        rank = len(shape)
        return pl.BlockSpec(
            (1,) + shape, lambda i, s: (slot_of(tick - s[0], micro),) + (0,) * rank
        )

    saved_shapes = [
        ((height, width, channels), BF16),
        ((rows, channels), F32),
        ((rows, TILE), F32),
        ((rows, channels), BF16),
        ((rows, hid), BF16),
        ((rows, hid), BF16),
        ((rows, channels), F32),
    ]
    kept = 0 if saved is None else len(saved)
    at = min(tick, micro - 1)
    operands = [images, received, *vectors, *weights] + ([] if saved is None else list(saved))
    in_specs = [pl.BlockSpec((1, height, width, channels), lambda i, s: (at, 0, 0, 0))]
    in_specs += [whole(item) for item in operands[1 : len(operands) - kept]]
    in_specs += [any_spec()] * kept
    outs = pl.pallas_call(
        functools.partial(train_kernel, tick, micro, side, kept),
        grid_spec=pltpu.PrefetchScalarGridSpec(
            num_scalar_prefetch=1,
            grid=(1,),
            in_specs=in_specs,
            out_specs=[whole(received)] + [slotted(*shape) for shape, _ in saved_shapes],
            scratch_shapes=[
                pltpu.VMEM((channels // TILE, height + 2 * REACH, width + 2 * EDGE, TILE), F32),
                pltpu.VMEM((rows, channels), F32),
                pltpu.VMEM((rows, channels), F32),
            ],
        ),
        out_shape=[shaped(received.shape, BF16)]
        + [shaped((micro + 1,) + shape, dtype) for shape, dtype in saved_shapes],
        input_output_aliases={1 + len(operands) - kept + i: 1 + i for i in range(kept)},
        compiler_params=params_of(),
        cost_estimate=cost(4 * rows * channels * hid, 8 << 20),
        name=f"train{tick}",
    )(sec, *operands)
    return outs[0], outs[1:]


def back_step(tick, micro, side, sections, sec, slopes, returned, params, saved, kept_out):
    height, width, channels = returned.shape
    rows = height * width
    kernel, gain, scale, first, second = params
    hat, inverse, slope = saved
    hid = slope.shape[-1]

    def which(s):
        return tick - (sections - 1 - s[0])

    def slotted(*shape):
        rank = len(shape)
        return pl.BlockSpec((1,) + shape, lambda i, s: (slot_of(which(s), micro),) + (0,) * rank)

    def held(*shape):
        rank = len(shape)
        return pl.BlockSpec(
            (1,) + shape, lambda i, s: (jnp.clip(which(s), 0, micro - 1),) + (0,) * rank
        )

    shapes = [
        ((rows, channels), BF16),
        ((rows, channels), BF16),
        ((rows, hid), BF16),
        ((rows, channels), BF16),
        ((rows, channels), F32),
    ]
    kept = 0 if kept_out is None else len(kept_out)
    operands = [slopes, returned, kernel, gain, scale, first, second, hat, inverse, slope]
    at = min(tick, micro - 1)
    in_specs = [pl.BlockSpec((1, height, width, channels), lambda i, s: (at, 0, 0, 0))]
    in_specs += [whole(item) for item in operands[1:7]]
    in_specs += [held(rows, channels), held(rows, TILE), held(rows, hid)]
    in_specs += [any_spec()] * kept
    base = len(operands)
    operands += [] if kept_out is None else list(kept_out)
    outs = pl.pallas_call(
        functools.partial(back_kernel, tick, micro, side, sections, kept),
        grid_spec=pltpu.PrefetchScalarGridSpec(
            num_scalar_prefetch=1,
            grid=(1,),
            in_specs=in_specs,
            out_specs=[whole(returned)] + [slotted(*shape) for shape, _ in shapes],
            scratch_shapes=[
                pltpu.VMEM((channels // TILE, height + 2 * REACH, width + 2 * EDGE, TILE), F32),
                pltpu.VMEM((rows, channels), F32),
                pltpu.VMEM((height, width, channels), F32),
            ],
        ),
        out_shape=[shaped(returned.shape, BF16)]
        + [shaped((micro + 1,) + shape, dtype) for shape, dtype in shapes],
        input_output_aliases={1 + base + i: 1 + i for i in range(kept)},
        compiler_params=params_of(),
        cost_estimate=cost(4 * rows * channels * hid, 8 << 20),
        name=f"back{tick}",
    )(sec, *operands)
    return outs[0], outs[1:]


def small_step(micro, vectors, grads):
    x = grads[0]
    height, width, channels = x.shape[1:]

    def first_ones(array):
        rank = len(array.shape)
        return pl.BlockSpec((micro,) + array.shape[1:], lambda i: (0,) * rank)

    return pl.pallas_call(
        functools.partial(small_kernel, micro),
        grid=(1,),
        in_specs=[whole(item) for item in vectors] + [first_ones(item) for item in grads],
        out_specs=[whole(item) for item in vectors],
        out_shape=[shaped(item.shape, F32) for item in vectors],
        scratch_shapes=[pltpu.VMEM((micro, height + 2 * REACH, width + 2 * EDGE, TILE), F32)],
        compiler_params=params_of(),
        cost_estimate=cost(1 << 28, 8 << 20),
        name="small",
    )(*vectors, *grads)


def tables(marked, sources, first_tiles):
    member = lax.axis_index("member")
    members = sources.shape[1]
    blocks = marked.shape[0]
    taken = blocks // 2
    capacity = (taken + members - 2) // (members - 1)
    ids = jnp.arange(blocks, dtype=jnp.int32)
    member_ids = jnp.arange(members, dtype=jnp.int32)
    target = jnp.sum(jnp.where(sources == member, member_ids[None, :], 0), axis=1)
    anchor = jnp.sum(jnp.where(member_ids[None, :] == member, sources, 0), axis=1)
    earlier = ids[:, None] > ids[None, :]
    counted = marked[None, :] == 1
    out_rank = jnp.sum(earlier & (target[:, None] == target[None, :]) & counted, axis=1)
    in_rank = jnp.sum(earlier & (anchor[:, None] == anchor[None, :]) & counted, axis=1)
    out_slot = (target * capacity + out_rank).astype(jnp.int32)
    in_slot = (anchor * capacity + in_rank).astype(jnp.int32)
    steps = jnp.arange(taken, dtype=jnp.int32)
    top = members * capacity - 1

    def listed(flags):
        place = jnp.sum(earlier & flags[None, :], axis=1)
        hits = flags[None, :] & (place[None, :] == steps[:, None])
        return hits, jnp.sum(jnp.where(hits, ids[None, :], 0), axis=1)

    def edges(flags):
        low = jnp.max(jnp.where(flags & (ids < first_tiles), ids, -1))
        low = jnp.where(low < 0, first_tiles - 1, low)
        high = jnp.min(jnp.where(flags & (ids >= first_tiles), ids, blocks))
        high = jnp.where(high >= blocks, first_tiles, high)
        return jnp.stack([low, high]).astype(jnp.int32)

    is_marked = marked == 1
    hits, marked_order = listed(is_marked)
    send_slots = jnp.clip(jnp.sum(jnp.where(hits, out_slot[None, :], 0), axis=1), 0, top)
    take_slots = jnp.clip(jnp.sum(jnp.where(hits, in_slot[None, :], 0), axis=1), 0, top)
    _, plain_order = listed(~is_marked)
    return dict(
        slots=members * capacity,
        in_slot=jnp.clip(in_slot, 0, top),
        marked_order=marked_order.astype(jnp.int32),
        plain_order=plain_order.astype(jnp.int32),
        send_slots=send_slots.astype(jnp.int32),
        take_slots=take_slots.astype(jnp.int32),
        marked_edges=edges(is_marked),
        plain_edges=edges(~is_marked),
    )


def weight_specs(micro, rows, channels, hid, first_tiles, groups):
    def low(block):
        return jnp.minimum(block, first_tiles - 1)

    def high(block):
        return jnp.maximum(block - first_tiles, 0)

    return [
        pl.BlockSpec((micro, rows, channels), lambda i, o, e: (0, 0, 0)),
        pl.BlockSpec((micro, rows, TILE), lambda i, o, e: (0, 0, low(o[i]))),
        pl.BlockSpec((micro, rows, hid), lambda i, o, e: (0, 0, 0)),
        pl.BlockSpec((micro, rows, TILE), lambda i, o, e: (0, 0, high(o[i]) // groups)),
        pl.BlockSpec((channels, TILE), lambda i, o, e: (0, low(o[i]))),
        pl.BlockSpec((channels, TILE), lambda i, o, e: (high(o[i]) % groups, high(o[i]) // groups)),
    ]


def local(
    inputs,
    cotangent,
    probe,
    dw_kernel,
    dw_bias,
    norm_gain,
    norm_bias,
    w_in,
    b_in,
    w_out,
    b_out,
    layer_scale,
    shuffle_mask,
    source_member,
):
    sections = lax.axis_size("section")
    sec = lax.axis_index("section").astype(jnp.int32).reshape(1)
    micro = inputs.shape[1]
    height, side, channels = inputs.shape[3:]
    width = (side + 15) // 16 * 16
    rows = height * width
    hid = w_in.shape[3]
    first_tiles = hid // TILE
    groups = hid // channels
    vectors = [
        dw_kernel.reshape(TAPS * TAPS, channels),
        dw_bias[0],
        norm_gain[0],
        norm_bias[0],
        b_in[0],
        b_out[0],
        layer_scale[0],
    ]
    first = w_in[0, 0]
    second = w_out[0, 0]
    lowered = [first.astype(BF16), second.astype(BF16)]

    def padded(maps):
        return jnp.pad(maps, ((0, 0), (0, 0), (0, width - side), (0, 0)))

    images = padded(inputs[0, :, 0])
    slopes = padded(cotangent[0, :, 0])
    trial = padded(probe[0])[0]
    ticks = micro + sections - 1
    received = images[0]
    saved = None
    for tick in range(ticks):
        current, saved = train_step(
            tick, micro, side, sec, images, received, vectors, lowered, saved
        )
        if tick < ticks - 1:
            pairs = [(s, s + 1) for s in range(sections - 1) if 0 <= tick - s < micro]
            received = lax.ppermute(current, "section", pairs)
    xs, hats, inverses, ns, hs, gelu_slopes, mixes = saved
    kernel, gain, scale = vectors[0], vectors[2], vectors[6]
    returned = slopes[0]
    grads = None
    for tick in range(ticks):
        current, grads = back_step(
            tick,
            micro,
            side,
            sections,
            sec,
            slopes,
            returned,
            (kernel, gain, scale, *lowered),
            (hats, inverses, gelu_slopes),
            grads,
        )
        if tick < ticks - 1:
            pairs = [
                (s, s - 1) for s in range(1, sections) if 0 <= tick - (sections - 1 - s) < micro
            ]
            returned = lax.ppermute(current, "section", pairs)
    dys, dmixes, dpres, dns, dspreads = grads

    table = tables(shuffle_mask[0], source_member[0], first_tiles)
    taken = table["marked_order"].shape[0]
    blocks = shuffle_mask.shape[1]
    weight_ins = (ns, dpres, hs, dmixes, first, second)
    specs = weight_specs(micro, rows, channels, hid, first_tiles, groups)
    tile = (1, channels, TILE)
    outgoing = pl.pallas_call(
        functools.partial(send_kernel, first_tiles, groups),
        grid_spec=pltpu.PrefetchScalarGridSpec(
            num_scalar_prefetch=2,
            grid=(taken,),
            in_specs=specs,
            out_specs=pl.BlockSpec(tile, lambda i, o, e: (e[i], 0, 0)),
        ),
        out_shape=shaped((table["slots"], channels, TILE), BF16),
        compiler_params=params_of(),
        cost_estimate=cost(1 << 30, 8 << 20),
        name="send",
    )(table["marked_order"], table["send_slots"], *weight_ins)
    arrived = lax.all_to_all(outgoing, "member", split_axis=0, concat_axis=0, tiled=True)

    def low_at(i, o, e):
        return (0, jnp.minimum(o[i], e[0]))

    def high_at(i, o, e):
        at = jnp.maximum(o[i], e[1]) - first_tiles
        return (at % groups, at // groups)

    own, new_first, new_second = pl.pallas_call(
        functools.partial(keep_kernel, first_tiles, groups),
        grid_spec=pltpu.PrefetchScalarGridSpec(
            num_scalar_prefetch=2,
            grid=(blocks - taken,),
            in_specs=specs,
            out_specs=[
                pl.BlockSpec(tile, lambda i, o, e: (o[i], 0, 0)),
                pl.BlockSpec((channels, TILE), low_at),
                pl.BlockSpec((channels, TILE), high_at),
            ],
        ),
        out_shape=[
            shaped((blocks, channels, TILE), BF16),
            shaped(first.shape, F32),
            shaped(second.shape, F32),
        ],
        compiler_params=params_of(),
        cost_estimate=cost(1 << 30, 8 << 20),
        name="keep",
    )(table["plain_order"], table["plain_edges"], *weight_ins)
    vectors = small_step(micro, vectors, (xs, hats, mixes, dys, dpres, dns, dspreads))

    new_first, new_second = pl.pallas_call(
        functools.partial(place_kernel, first_tiles),
        grid_spec=pltpu.PrefetchScalarGridSpec(
            num_scalar_prefetch=3,
            grid=(taken,),
            in_specs=[
                pl.BlockSpec(tile, lambda i, o, e, s: (s[i], 0, 0)),
                pl.BlockSpec((channels, TILE), lambda i, o, e, s: low_at(0, o, e)),
                pl.BlockSpec((channels, TILE), lambda i, o, e, s: high_at(0, o, e)),
            ],
            out_specs=[
                pl.BlockSpec((channels, TILE), lambda i, o, e, s: low_at(i, o, e)),
                pl.BlockSpec((channels, TILE), lambda i, o, e, s: high_at(i, o, e)),
            ],
        ),
        out_shape=[shaped(first.shape, F32), shaped(second.shape, F32)],
        input_output_aliases={4: 0, 5: 1},
        compiler_params=params_of(),
        cost_estimate=cost(0, 8 << 20),
        name="place",
    )(
        table["marked_order"],
        table["marked_edges"],
        table["take_slots"],
        arrived,
        new_first,
        new_second,
    )

    received = trial
    kept_out = None
    for tick in range(sections):
        operands = [trial, received, *vectors, own, arrived]
        result = pl.pallas_call(
            functools.partial(probe_kernel, tick, side),
            grid_spec=pltpu.PrefetchScalarGridSpec(
                num_scalar_prefetch=3,
                grid=(1,),
                in_specs=[whole(item) for item in operands],
                out_specs=whole(trial),
                scratch_shapes=[
                    pltpu.VMEM(
                        (channels // TILE, height + 2 * REACH, width + 2 * EDGE, TILE), F32
                    ),
                    pltpu.VMEM((rows, channels), F32),
                    pltpu.VMEM((rows, channels), F32),
                    pltpu.VMEM((rows, channels), BF16),
                ],
            ),
            out_shape=shaped(trial.shape, BF16),
            compiler_params=params_of(),
            cost_estimate=cost(4 * rows * channels * hid, 8 << 20),
            name=f"probe{tick}",
        )(sec, shuffle_mask[0], table["in_slot"], *operands)
        kept_out = result if tick == 0 else jnp.where(sec[0] == tick, result, kept_out)
        if tick < sections - 1:
            received = lax.ppermute(result, "section", [(tick, tick + 1)])
    features = kept_out[:, :side, :]
    return (new_first[None, None], new_second[None, None], features[None, None, None])


def solution(mesh):
    return jax.shard_map(
        local,
        mesh=mesh,
        in_specs=(
            P("member", None, None, None, None, None),
            P("member", None, None, None, None, None),
            P("member", None, None, None, None),
            P("member", "section", None, None, None),
            P("member", "section", None),
            P("member", "section", None),
            P("member", "section", None),
            P("member", "section", None, None),
            P("member", "section", None),
            P("member", "section", None, None),
            P("member", "section", None),
            P("member", "section", None),
            P("section", None),
            P("section", None, None),
        ),
        out_specs=(
            P("member", "section", None, None),
            P("member", "section", None, None),
            P("member", "section", None, None, None, None),
        ),
        check_vma=False,
    )
```

time: 598 us -> 287 us (0.48)
  the two profiles are of different devices: /device:TPU:1 before, /device:TPU:4 now
where the time goes in v1:
time: 287 us; the launch traced here: 285 us
  waiting for transfers between devices  103 us (36%)
  Pallas kernels  94.4 us (33%)
  local copies, waits for them, and re-layouts  49.5 us (17%)
  starting transfers between devices  24.2 us (8%)
  other arithmetic  7.47 us (3%)
  between operations  6.47 us (2%)
    unnamed x144, local copies, waits for them, and re-layouts  48 us
    ppermute x3, waiting for transfers between devices, local(): received = lax.ppermute(result, 'section', [(tick, tick + 1)])  36.3 us
    all_to_all x1, waiting for transfers between devices, local(): lax.all_to_all(outgoing, 'member', split_axis=0, concat_axis=0, tiled=True)  24 us
    ppermute x4, waiting for transfers between devices, local(): received = lax.ppermute(current, 'section', pairs)  23.7 us
    ppermute x4, waiting for transfers between devices, local(): returned = lax.ppermute(current, 'section', pairs)  19.2 us
    pallas_call x5, Pallas kernels, train_step(): pl.pallas_call(functools.partial(train_kernel, tick, micro, side, kept),...  17.5 us
    pallas_call x5, Pallas kernels, back_step(): pl.pallas_call(functools.partial(back_kernel, tick, micro, side, sections...  17.5 us
    pallas_call x4, Pallas kernels, local(): pl.pallas_call(functools.partial(probe_kernel, tick, side), grid_spec=plt...  17.4 us
  transfers between devices with their start and end apart: 12, of which 8 were waited for; matrix products, arithmetic and copies ran while one was open for 1% of the time, Pallas kernels for 11%

profile of v1, /device:TPU:4, one launch (start us, length us, event | category | flops | bytes accessed | tf_op | source)
XLA Modules:
  0.0 285.2 jit_solution(6715686383789722772)
XLA Ops:
  2.4 2.6 bitcast_convert_fusion.refs_8_.refs_4_
  11.2 17.3 %collective-permute-done.1.received_ref = bf16[14,16,512]{2,1,0:T(8,128)(2,1)S(1)} collective-permute-done((bf16[14,16,512]{2,1,0:T(8,128)(2,1)S(1)}, bf16[14,16,512]{2,1,0:T(8,128)(2,1)S(1)}, u32[]{:S(2)}, u32[]{:S(2)}) %collective-permute-start.1) | collective-permute-done | bytes 229408 | tf_op jit(solution)/shard_map/ppermute | solution.py:664
  28.5 7.2 %train2.1 = (bf16[14,16,512]{2,1,0:T(8,128)(2,1)S(1)}, bf16[3,14,16,512]{3,2,1,0:T(8,128)(2,1)S(1)}, f32[3,224,512]{2,1,0:T(8,128)S(1)}, f32[3,224,128]{2,1,0:T(...) custom-call(s32[1]{0:T(128)} %bitcast.5.sec_ref, ...), custom_call_target="tpu_custom_call", output_to_operand_aliasing={{1}: (12, {}), {2}: (13, {}), {3}: (14, {}), {4}: (15, {}),... | custom-call | flops 939524096 | bytes 8388608 | tf_op jit(solution)/shard_map/train2/pallas_call | solution.py:443
  37.6 5.4 %collective-permute-done.2.received_ref = bf16[14,16,512]{2,1,0:T(8,128)(2,1)S(1)} collective-permute-done((bf16[14,16,512]{2,1,0:T(8,128)(2,1)S(1)}, bf16[14,16,512]{2,1,0:T(8,128)(2,1)S(1)}, u32[]{:S(2)}, u32[]{:S(2)}) %collective-permute-start.2) | collective-permute-done | bytes 229408 | tf_op jit(solution)/shard_map/ppermute | solution.py:664
  43.1 7.2 %train3.1 = (bf16[14,16,512]{2,1,0:T(8,128)(2,1)S(1)}, bf16[3,14,16,512]{3,2,1,0:T(8,128)(2,1)S(1)}, f32[3,224,512]{2,1,0:T(8,128)S(1)}, f32[3,224,128]{2,1,0:T(...) custom-call(s32[1]{0:T(128)} %bitcast.5.sec_ref, ...), custom_call_target="tpu_custom_call", output_to_operand_aliasing={{1}: (12, {}), {2}: (13, {}), {3}: (14, {}), {4}: (15, {}),... | custom-call | flops 939524096 | bytes 8388608 | tf_op jit(solution)/shard_map/train3/pallas_call | solution.py:443
  55.7 2.6 back0.1
  64.9 12.5 %collective-permute-done.4.returned_ref = bf16[14,16,512]{2,1,0:T(8,128)(2,1)} collective-permute-done((bf16[14,16,512]{2,1,0:T(8,128)(2,1)}, bf16[14,16,512]{2,1,0:T(8,128)(2,1)}, u32[]{:S(2)}, u32[]{:S(2)}) %collective-permute-start.4) | collective-permute-done | bytes 229408 | tf_op jit(solution)/shard_map/ppermute | solution.py:686
  88.3 5.9 %back1.1 = (bf16[14,16,512]{2,1,0:T(8,128)(2,1)S(1)}, bf16[3,224,512]{2,1,0:T(8,128)(2,1)S(1)}, bf16[3,224,512]{2,1,0:T(8,128)(2,1)S(1)}, bf16[3,224,2048]{2,1,0...) custom-call(s32[1]{0:T(128)} %bitcast.5.sec_ref, ...), custom_call_target="tpu_custom_call", output_to_operand_aliasing={{1}: (11, {}), {2}: (12, {}), {3}: (13, {}), {4}: (14, {}),... | custom-call | flops 939524096 | bytes 8388608 | tf_op jit(solution)/shard_map/back1/pallas_call | solution.py:502
  96.2 3.4 %collective-permute-done.5.returned_ref = bf16[14,16,512]{2,1,0:T(8,128)(2,1)S(1)} collective-permute-done((bf16[14,16,512]{2,1,0:T(8,128)(2,1)S(1)}, bf16[14,16,512]{2,1,0:T(8,128)(2,1)S(1)}, u32[]{:S(2)}, u32[]{:S(2)}) %collective-permute-start.5) | collective-permute-done | bytes 229408 | tf_op jit(solution)/shard_map/ppermute | solution.py:686
  99.6 5.7 %back2.1 = (bf16[14,16,512]{2,1,0:T(8,128)(2,1)S(1)}, bf16[3,224,512]{2,1,0:T(8,128)(2,1)S(1)}, bf16[3,224,512]{2,1,0:T(8,128)(2,1)S(1)}, bf16[3,224,2048]{2,1,0...) custom-call(s32[1]{0:T(128)} %bitcast.5.sec_ref, ...), custom_call_target="tpu_custom_call", output_to_operand_aliasing={{1}: (11, {}), {2}: (12, {}), {3}: (13, {}), {4}: (14, {}),... | custom-call | flops 939524096 | bytes 8388608 | tf_op jit(solution)/shard_map/back2/pallas_call | solution.py:502
  105.4 3.8 %collective-permute-start.6 = (bf16[14,16,512]{2,1,0:T(8,128)(2,1)S(1)}, bf16[14,16,512]{2,1,0:T(8,128)(2,1)S(1)}, u32[]{:S(2)}, u32[]{:S(2)}) collective-permute-start(bf16[14,16,512]{2,1,0:T(8,128)(2,1)S(1)} %get-tuple-element.131), channel_id=1, source_target_pairs={{1,0},{2,1},{5,4},{6,5},{9,8},{10,9},{13,12},{14,13},{17,16},{18,1... | collective-permute-start | bytes 688136 | tf_op jit(solution)/shard_map/ppermute | solution.py:686
  109.4 3.3 %collective-permute-done.6.returned_ref = bf16[14,16,512]{2,1,0:T(8,128)(2,1)S(1)} collective-permute-done((bf16[14,16,512]{2,1,0:T(8,128)(2,1)S(1)}, bf16[14,16,512]{2,1,0:T(8,128)(2,1)S(1)}, u32[]{:S(2)}, u32[]{:S(2)}) %collective-permute-start.6) | collective-permute-done | bytes 229408 | tf_op jit(solution)/shard_map/ppermute | solution.py:686
  123.0 11.0 %send.1 = bf16[24,512,128]{2,1,0:T(8,128)(2,1)S(1)} custom-call(s32[16]{0:T(128)S(1)} %get-tuple-element.167.order_ref, s32[16]{0:T(128)S(1)} %broadcast_clamp_fusion.1.slot_ref, bf16[3,224,512]{2,1,0:T(8,128)(2,1)S(1)} %copy-done.26, bf16[3,224,2048]{2,1,0:T(8,128)(2,1)S(1)} %copy-done.5, bf16[3,224,2048]{2,1,0:T(8,128)(2,1)S(1)} %copy-done.9, ...), custom_call_target="tpu_custom_call" | custom-call | flops 1073741824 | bytes 8388608 | tf_op jit(solution)/shard_map/send/pallas_call | solution.py:695
  136.6 7.4 %all-to-all-start = ((bf16[24,512,128]{2,1,0:T(8,128)(2,1)}), bf16[24,512,128]{2,1,0:T(8,128)(2,1)}, u32[]{:S(2)}, u32[]{:S(2)}) async-start(bf16[24,512,128]{2,1,0:T(8,128)(2,1)} %copy-done.48), calls=%async_computation | async-start | bytes 6291456 | tf_op jit(solution)/shard_map/all_to_all | solution.py:708
  155.8 6.2 %small.1 = (f32[49,512]{1,0:T(8,128)S(1)}, f32[1,512]{1,0:T(1,128)S(1)}, f32[1,512]{1,0:T(1,128)S(1)}, f32[1,512]{1,0:T(1,128)S(1)}, f32[1,2048]{1,0:T(1,128)S(1...) custom-call(f32[49,512]{1,0:T(8,128)S(1)} %copy-done.47, f32[1,512]{1,0:T(1,128)S(1)} %bitcast.88, f32[1,512]{1,0:T(1,128)S(1)} %bitcast.71, ...), custom_call_target="tpu_custom_call" | custom-call | flops 268435456 | bytes 8388608 | tf_op jit(solution)/shard_map/small/pallas_call | solution.py:533
  162.7 13.7 %keep.1 = (bf16[32,512,128]{2,1,0:T(8,128)(2,1)S(1)}, f32[512,2048]{1,0:T(8,128)}, f32[2048,512]{1,0:T(8,128)}) custom-call(s32[16]{0:T(128)S(1)} %select_reduce_fusion.order_ref, s32[2]{0:T(128)S(1)} %pad_add_fusion.1.edge_ref, bf16[3,224,512]{2,1,0:T(8,128)(2,1)S(1)} %copy-done.27, bf16[3,224,2048]{2,1,0:T(8,128)(2,1)S(1)} %copy-done.7, ...), custom_call_target="tpu_custom_call" | custom-call | flops 1073741824 | bytes 8388608 | tf_op jit(solution)/shard_map/keep/pallas_call | solution.py:717
  178.4 24.0 %all-to-all-done.arrived_ref.refs_8_ = bf16[24,512,128]{2,1,0:T(8,128)(2,1)} async-done(((bf16[24,512,128]{2,1,0:T(8,128)(2,1)}), bf16[24,512,128]{2,1,0:T(8,128)(2,1)}, u32[]{:S(2)}, u32[]{:S(2)}) %all-to-all-start) | async-done | bytes 3145760 | tf_op jit(solution)/shard_map/all_to_all | solution.py:708
  202.4 2.2 copy-done.12
  206.4 2.4 probe0.1
  210.3 3.1 %probe1.1 = bf16[14,16,512]{2,1,0:T(8,128)(2,1)} custom-call(s32[1]{0:T(128)} %bitcast.5.sec_ref, s32[32]{0:T(128)S(1)} %bitcast.102, s32[32]{0:T(128)S(1)} %get-tuple-element.175.slot_ref, bf16[14,16,512]{2,1,0:T(8,128)(2,1)S(1)} %copy-done.49, bf16[14,16,512]{2,1,0:T(8,128)(2,1)S(1)} %collective-permute-done.8.received_ref, f32[49,512]{1,0:T(8,128)S(1)} %copy-done.53, ...), custom_call_target="tpu_custom_call" | custom-call | flops 939524096 | bytes 8388608 | tf_op jit(solution)/shard_map/probe1/pallas_call | solution.py:773
  217.3 36.3 %collective-permute-done.9.received_ref = bf16[14,16,512]{2,1,0:T(8,128)(2,1)S(1)} collective-permute-done((bf16[14,16,512]{2,1,0:T(8,128)(2,1)}, bf16[14,16,512]{2,1,0:T(8,128)(2,1)S(1)}, u32[]{:S(2)}, u32[]{:S(2)}) %collective-permute-start.9) | collective-permute-done | bytes 229408 | tf_op jit(solution)/shard_map/ppermute | solution.py:796
  258.3 9.3 %probe2.1 = bf16[14,16,512]{2,1,0:T(8,128)(2,1)} custom-call(s32[1]{0:T(128)} %bitcast.5.sec_ref, s32[32]{0:T(128)S(1)} %bitcast.103, s32[32]{0:T(128)S(1)} %get-tuple-element.175.slot_ref, bf16[14,16,512]{2,1,0:T(8,128)(2,1)S(1)} %copy-done.49, bf16[14,16,512]{2,1,0:T(8,128)(2,1)S(1)} %copy-done.62, f32[49,512]{1,0:T(8,128)S(1)} %copy-done.54, ...), custom_call_target="tpu_custom_call" | custom-call | flops 939524096 | bytes 8388608 | tf_op jit(solution)/shard_map/probe2/pallas_call | solution.py:773
  269.7 11.1 %place.1 = (f32[512,2048]{1,0:T(8,128)}, f32[2048,512]{1,0:T(8,128)}) custom-call(s32[16]{0:T(128)S(1)} %get-tuple-element.167.order_ref, s32[2]{0:T(128)S(1)} %pad_add_fusion.edge_ref, s32[16]{0:T(128)S(1)} %broadcast_clamp_fusion.2.slot_ref, bf16[24,512,128]{2,1,0:T(8,128)(2,1)} %all-to-all-done.arrived_ref.refs_8_, ...), custom_call_target="tpu_custom_call", output_to_operand_aliasing={{0}: (4, {}), {1}: (5, {})} | custom-call | bytes 8388608 | tf_op jit(solution)/shard_map/place/pallas_call | solution.py:740
  280.9 2.6 probe3.1
  (185 shorter events, 72.4 us)
Async XLA Ops:
  6.9 48.8 %copy-start = (bf16[512,2048]{1,0:T(8,128)(2,1)}, bf16[512,2048]{1,0:T(8,128)(2,1)S(1)}, u32[]{:S(2)}) copy-start(bf16[512,2048]{1,0:T(8,128)(2,1)S(1)} %bitcast_convert_fusion.1.refs_7_.refs_3_) | copy-start | bytes 6291460
  8.3 0.7 collective-permute-start
  9.9 18.6 %collective-permute-start.1 = (bf16[14,16,512]{2,1,0:T(8,128)(2,1)S(1)}, bf16[14,16,512]{2,1,0:T(8,128)(2,1)S(1)}, u32[]{:S(2)}, u32[]{:S(2)}) collective-permute-start(bf16[14,16,512]{2,1,0:T(8,128)(2,1)S(1)} %get-tuple-element.91), channel_id=1, source_target_pairs={{0,1},{1,2},{4,5},{5,6},{8,9},{9,10},{12,13},{13,14},{16,17},{17,1... | collective-permute-start | bytes 688136 | tf_op jit(solution)/shard_map/ppermute | solution.py:664
  35.7 7.3 %collective-permute-start.2 = (bf16[14,16,512]{2,1,0:T(8,128)(2,1)S(1)}, bf16[14,16,512]{2,1,0:T(8,128)(2,1)S(1)}, u32[]{:S(2)}, u32[]{:S(2)}) collective-permute-start(bf16[14,16,512]{2,1,0:T(8,128)(2,1)S(1)} %get-tuple-element.99), channel_id=1, source_target_pairs={{1,2},{2,3},{5,6},{6,7},{9,10},{10,11},{13,14},{14,15},{17,18},{18... | collective-permute-start | bytes 688136 | tf_op jit(solution)/shard_map/ppermute | solution.py:664
  43.1 8.5 %copy-start.68 = (bf16[1,2,1,14,14,512]{5,1,4,3,2,0:T(2,128)(2,1)S(1)}, bf16[1,2,1,14,14,512]{5,1,4,3,2,0:T(2,128)(2,1)}, u32[]{:S(2)}) copy-start(bf16[1,2,1,14,14,512]{5,1,4,3,2,0:T(2,128)(2,1)} %param.15) | copy-start | bytes 1204228
  50.3 2.4 collective-permute-start.3
  63.6 13.8 %collective-permute-start.4 = (bf16[14,16,512]{2,1,0:T(8,128)(2,1)}, bf16[14,16,512]{2,1,0:T(8,128)(2,1)}, u32[]{:S(2)}, u32[]{:S(2)}) collective-permute-start(bf16[14,16,512]{2,1,0:T(8,128)(2,1)} %get-tuple-element.119), channel_id=1, source_target_pairs={{3,2},{7,6},{11,10},{15,14},{19,18},{23,22},{27,26},{31,30}} | collective-permute-start | bytes 688136 | tf_op jit(solution)/shard_map/ppermute | solution.py:686
  88.3 7.8 %copy-start.70 = (s32[1,32,8]{1,2,0:T(8,128)S(1)}, s32[1,32,8]{1,2,0:T(8,128)}, u32[]{:S(2)}) copy-start(s32[1,32,8]{1,2,0:T(8,128)} %param.27) | copy-start | bytes 3076
  88.3 7.9 %copy-start.66 = (s32[1,32]{1,0:T(1,128)S(1)}, s32[1,32]{1,0:T(1,128)}, u32[]{:S(2)}) copy-start(s32[1,32]{1,0:T(1,128)} %param.26) | copy-start | bytes 388
  94.2 5.4 %collective-permute-start.5 = (bf16[14,16,512]{2,1,0:T(8,128)(2,1)S(1)}, bf16[14,16,512]{2,1,0:T(8,128)(2,1)S(1)}, u32[]{:S(2)}, u32[]{:S(2)}) collective-permute-start(bf16[14,16,512]{2,1,0:T(8,128)(2,1)S(1)} %get-tuple-element.125), channel_id=1, source_target_pairs={{2,1},{3,2},{6,5},{7,6},{10,9},{11,10},{14,13},{15,14},{18,17},{19... | collective-permute-start | bytes 688136 | tf_op jit(solution)/shard_map/ppermute | solution.py:686
  105.4 7.3 %collective-permute-start.6 = (bf16[14,16,512]{2,1,0:T(8,128)(2,1)S(1)}, bf16[14,16,512]{2,1,0:T(8,128)(2,1)S(1)}, u32[]{:S(2)}, u32[]{:S(2)}) collective-permute-start(bf16[14,16,512]{2,1,0:T(8,128)(2,1)S(1)} %get-tuple-element.131), channel_id=1, source_target_pairs={{1,0},{2,1},{5,4},{6,5},{9,8},{10,9},{13,12},{14,13},{17,16},{18,1... | collective-permute-start | bytes 688136 | tf_op jit(solution)/shard_map/ppermute | solution.py:686
  113.9 0.8 collective-permute-start.7
  136.6 11.2 %copy-start.69 = (bf16[1,1,14,14,512]{4,3,2,1,0:T(8,128)(2,1)S(1)}, bf16[1,1,14,14,512]{4,3,2,1,0:T(8,128)(2,1)}, u32[]{:S(2)}) copy-start(bf16[1,1,14,14,512]{4,3,2,1,0:T(8,128)(2,1)} %param.16) | copy-start | bytes 602116
  136.6 11.9 %copy-start.18 = (f32[3,224,512]{2,1,0:T(8,128)S(1)}, f32[3,224,512]{2,1,0:T(8,128)}, u32[]{:S(2)}) copy-start(f32[3,224,512]{2,1,0:T(8,128)} %copy-done.17) | copy-start | bytes 4128772
  136.6 65.8 %all-to-all-start = ((bf16[24,512,128]{2,1,0:T(8,128)(2,1)}), bf16[24,512,128]{2,1,0:T(8,128)(2,1)}, u32[]{:S(2)}, u32[]{:S(2)}) async-start(bf16[24,512,128]{2,1,0:T(8,128)(2,1)} %copy-done.48), calls=%async_computation | async-start | bytes 6291456 | tf_op jit(solution)/shard_map/all_to_all | solution.py:708
  155.8 6.8 %copy-start.10 = (bf16[3,224,2048]{2,1,0:T(8,128)(2,1)S(1)}, bf16[3,224,2048]{2,1,0:T(8,128)(2,1)}, u32[]{:S(2)}) copy-start(bf16[3,224,2048]{2,1,0:T(8,128)(2,1)} %copy-done.8) | copy-start | bytes 8257540
  155.8 6.8 %copy-start.27 = (bf16[3,224,512]{2,1,0:T(8,128)(2,1)S(1)}, bf16[3,224,512]{2,1,0:T(8,128)(2,1)}, u32[]{:S(2)}) copy-start(bf16[3,224,512]{2,1,0:T(8,128)(2,1)} %copy-done.25) | copy-start | bytes 2064388
  155.8 6.8 %copy-start.31 = (bf16[3,224,512]{2,1,0:T(8,128)(2,1)S(1)}, bf16[3,224,512]{2,1,0:T(8,128)(2,1)}, u32[]{:S(2)}) copy-start(bf16[3,224,512]{2,1,0:T(8,128)(2,1)} %copy-done.30) | copy-start | bytes 2064388
  209.6 0.7 collective-permute-start.8
  213.4 40.2 %collective-permute-start.9 = (bf16[14,16,512]{2,1,0:T(8,128)(2,1)}, bf16[14,16,512]{2,1,0:T(8,128)(2,1)S(1)}, u32[]{:S(2)}, u32[]{:S(2)}) collective-permute-start(bf16[14,16,512]{2,1,0:T(8,128)(2,1)} %probe1.1), channel_id=1, source_target_pairs={{1,2},{5,6},{9,10},{13,14},{17,18},{21,22},{25,26},{29,30}} | collective-permute-start | bytes 688136 | tf_op jit(solution)/shard_map/ppermute | solution.py:796
  267.6 13.2 %collective-permute-start.10 = (bf16[14,16,512]{2,1,0:T(8,128)(2,1)}, bf16[14,16,512]{2,1,0:T(8,128)(2,1)}, u32[]{:S(2)}, u32[]{:S(2)}) collective-permute-start(bf16[14,16,512]{2,1,0:T(8,128)(2,1)} %probe2.1), channel_id=1, source_target_pairs={{2,3},{6,7},{10,11},{14,15},{18,19},{22,23},{26,27},{30,31}} | collective-permute-start | bytes 688136 | tf_op jit(solution)/shard_map/ppermute | solution.py:796
  269.7 11.2 %copy-start.14 = (bf16[32,512,128]{2,1,0:T(8,128)(2,1)S(1)}, bf16[32,512,128]{2,1,0:T(8,128)(2,1)}, u32[]{:S(2)}) copy-start(bf16[32,512,128]{2,1,0:T(8,128)(2,1)} %copy-done.11) | copy-start | bytes 12582916
  269.7 11.2 %copy-start.50 = (bf16[14,16,512]{2,1,0:T(8,128)(2,1)S(1)}, bf16[14,16,512]{2,1,0:T(8,128)(2,1)}, u32[]{:S(2)}) copy-start(bf16[14,16,512]{2,1,0:T(8,128)(2,1)} %pad_bitcast_fusion.image_ref.received_ref) | copy-start | bytes 688132
  269.7 11.2 %copy-start.55 = (f32[49,512]{1,0:T(8,128)S(1)}, f32[49,512]{1,0:T(8,128)}, u32[]{:S(2)}) copy-start(f32[49,512]{1,0:T(8,128)} %copy-done.51) | copy-start | bytes 301060
  (59 other events, 105.3 us)

commit v2 on v1

v2 whole, which is shorter than its diff:
```python
import functools
import math

import jax
import jax.numpy as jnp
from jax import lax
from jax.experimental import pallas as pl
from jax.experimental.pallas import tpu as pltpu
from jax.sharding import PartitionSpec as P

TILE = 128
learning_rate = 0.001
norm_epsilon = 1e-06
F32 = jnp.float32
BF16 = jnp.bfloat16
EDGE = 8
REACH = 3
TAPS = 2 * REACH + 1
VMEM_LIMIT = 44 * 1024 * 1024

ERF_TOP = (
    0.00022905065861350646,
    0.0034082910107109506,
    0.050955695062380861,
    0.18520832239976145,
    1.128379143519084,
)
ERF_LOW = (
    -1.1791602954361697e-7,
    0.000023547966471313185,
    0.0010179625278914885,
    0.014070470171167667,
    0.11098505178285362,
    0.49746925110067538,
    1.0,
)


def erf(value):
    value = jnp.clip(value, -3.832506856900711, 3.832506856900711)
    square = value * value
    top = jnp.full_like(square, ERF_TOP[0])
    for term in ERF_TOP[1:]:
        top = top * square + term
    low = jnp.full_like(square, ERF_LOW[0])
    for term in ERF_LOW[1:]:
        low = low * square + term
    return value * top / low


def whole(array):
    rank = len(array.shape)
    return pl.BlockSpec(array.shape, lambda *args: (0,) * rank)


def lanes(index):
    return pl.ds(pl.multiple_of(index * TILE, TILE), TILE)


def shaped(shape, dtype):
    return jax.ShapeDtypeStruct(shape, dtype)


def convolve(padded, chunk, kernel_ref, height, width, flip, store):
    totals = [None] * height
    for col in range(TAPS):
        taps = []
        for row in range(TAPS):
            at = row * TAPS + col
            if flip:
                at = TAPS * TAPS - 1 - at
            taps.append(kernel_ref[at, 0:1, lanes(chunk)])
        for line in range(height + TAPS - 1):
            values = padded[chunk, line, pl.ds(EDGE - REACH + col, width), :]
            for row in range(TAPS):
                out = line - row
                if 0 <= out < height:
                    term = values * taps[row]
                    totals[out] = term if totals[out] is None else totals[out] + term
    for out in range(height):
        store(out, totals[out])


def fill_padded(padded, maps):
    height, width, channels = maps.shape
    padded[...] = jnp.zeros(padded.shape, F32)
    for chunk in range(channels // TILE):
        padded[chunk, REACH : REACH + height, EDGE : EDGE + width, :] = maps[
            :, :, chunk * TILE : (chunk + 1) * TILE
        ]


def real_columns(shape, side):
    return lax.broadcasted_iota(jnp.int32, shape, 1) < side


def normalise(spread):
    center = jnp.mean(spread, axis=-1, keepdims=True)
    offset = spread - center
    variance = jnp.mean(offset * offset, axis=-1, keepdims=True)
    inverse = lax.rsqrt(variance + norm_epsilon)
    return offset * inverse, inverse


def forward_core(
    side, vectors, widened, padded, spread, total, weights, n_ref, hat_store, hidden_store
):
    kernel_ref, bias_ref, gain_ref, shift_ref, first_bias_ref, second_bias_ref, scale_ref = vectors
    height, width, channels = widened.shape
    hid = first_bias_ref.shape[1]
    fill_padded(padded, widened)

    def conv_body(chunk, carry):
        bias = bias_ref[0:1, lanes(chunk)]

        def store(out, value):
            spread[out * width : (out + 1) * width, lanes(chunk)] = value + bias

        convolve(padded, chunk, kernel_ref, height, width, False, store)
        return carry

    lax.fori_loop(0, channels // TILE, conv_body, 0)
    hat, inverse = normalise(spread[...])
    n_ref[...] = (hat * gain_ref[...] + shift_ref[...]).astype(BF16)
    hat_store(hat, inverse)
    total[...] = jnp.zeros(total.shape, F32)

    def mix_body(piece, carry):
        first, second = weights(piece)
        at = pl.ds(pl.multiple_of(piece * channels, channels), channels)
        pre = jnp.dot(n_ref[...], first, preferred_element_type=F32) + first_bias_ref[:, at]
        below = 0.5 + 0.5 * erf(pre * math.sqrt(0.5))
        hidden = (pre * below).astype(BF16)
        hidden_store(piece, hidden, pre, below)
        total[...] += jnp.dot(hidden, second, preferred_element_type=F32)
        return carry

    lax.fori_loop(0, hid // channels, mix_body, 0)
    mixed = total[...] + second_bias_ref[...]
    result = widened + (scale_ref[...] * mixed).reshape(height, width, channels)
    result = jnp.where(real_columns(result.shape, side), result, 0.0)
    return result, mixed


def is_active(sec_ref, tick, count):
    which = tick - sec_ref[0]
    return (which >= 0) & (which < count)


def columns(piece, channels):
    return pl.ds(pl.multiple_of(piece * channels, channels), channels)


def train_kernel(tick, micro, side, kept, sec_ref, image_ref, received_ref, *refs):
    vectors, (first_ref, second_ref) = refs[:7], refs[7:9]
    refs = refs[9 + kept :]
    y_ref, outs, bufs = refs[0], refs[1:8], refs[8:15]
    padded, spread, total, sems, piece_sems = refs[15:]
    x_buf, hat_buf, inverse_buf, n_buf, mixed_buf, h_buf, slope_buf = bufs
    h_out, slope_out = outs[5:]

    @pl.when(is_active(sec_ref, tick, micro))
    def _():
        slot = tick - sec_ref[0]
        channels = x_buf.shape[-1]
        pieces = h_buf.shape[-1] // channels
        entry = jnp.where(sec_ref[0] == 0, image_ref[0].astype(F32), received_ref[...].astype(F32))
        x_buf[...] = entry.astype(BF16)

        def weights(piece):
            at = columns(piece, channels)
            return first_ref[:, at], second_ref[at, :]

        def piece_copies(piece):
            at = columns(piece, channels)
            return [
                pltpu.make_async_copy(h_buf.at[:, at], h_out.at[slot, :, at], piece_sems.at[0, piece]),
                pltpu.make_async_copy(
                    slope_buf.at[:, at], slope_out.at[slot, :, at], piece_sems.at[1, piece]
                ),
            ]

        def hidden_store(piece, hidden, pre, below):
            at = columns(piece, channels)
            h_buf[:, at] = hidden
            density = jnp.exp(-0.5 * pre * pre) * (1.0 / math.sqrt(2.0 * math.pi))
            slope_buf[:, at] = (below + pre * density).astype(BF16)
            for copy in piece_copies(piece):
                copy.start()

        copies = [
            pltpu.make_async_copy(buf, out.at[slot], sems.at[index])
            for index, (buf, out) in enumerate(zip(bufs[:5], outs[:5]))
        ]

        def hat_store(hat, inverse):
            hat_buf[...] = hat
            inverse_buf[...] = jnp.broadcast_to(inverse, inverse_buf.shape)
            for copy in copies[:4]:
                copy.start()

        result, mixed = forward_core(
            side, vectors, entry, padded, spread, total, weights, n_buf, hat_store, hidden_store
        )
        y_ref[...] = result.astype(BF16)
        mixed_buf[...] = mixed
        copies[4].start()
        for copy in copies:
            copy.wait()
        for piece in range(pieces):
            for copy in piece_copies(piece):
                copy.wait()


def probe_kernel(tick, side, kept, sec_ref, marked_ref, slot_ref, image_ref, received_ref, *refs):
    vectors, (own_ref, arrived_ref) = refs[:7], refs[7:9]
    refs = refs[9 + kept :]
    y_ref, feature_ref, feature_buf, tiles_buf, padded, spread, total, n_ref, sems, end_sem = refs

    @pl.when(sec_ref[0] == tick)
    def _():
        channels = y_ref.shape[-1]
        tiles = channels // TILE
        blocks = tiles_buf.shape[0]
        groups = vectors[4].shape[1] // channels
        for block in range(blocks):
            taken = marked_ref[block] == 1

            @pl.when(taken)
            def _():
                pltpu.make_async_copy(
                    arrived_ref.at[slot_ref[block]], tiles_buf.at[block], sems.at[block]
                ).start()

            @pl.when(jnp.logical_not(taken))
            def _():
                pltpu.make_async_copy(
                    own_ref.at[block], tiles_buf.at[block], sems.at[block]
                ).start()

        entry = image_ref[...] if tick == 0 else received_ref[...]

        def tile(block):
            pltpu.make_async_copy(own_ref.at[block], tiles_buf.at[block], sems.at[block]).wait()
            return tiles_buf[block]

        def weights(piece):
            first = [tile(piece * tiles + item) for item in range(tiles)]
            second = [tile(groups * tiles + item * groups + piece) for item in range(tiles)]
            return jnp.concatenate(first, axis=1), jnp.concatenate(second, axis=1)

        result, mixed = forward_core(
            side,
            vectors,
            entry.astype(F32),
            padded,
            spread,
            total,
            weights,
            n_ref,
            lambda hat, inverse: None,
            lambda piece, hidden, pre, below: None,
        )
        output = result.astype(BF16)
        y_ref[...] = output
        feature_buf[...] = output[:, :side, :]
        done = pltpu.make_async_copy(feature_buf, feature_ref, end_sem)
        done.start()
        done.wait()


def back_kernel(tick, micro, side, sections, kept, turns, sec_ref, slope_in_ref, returned_ref, *refs):
    kernel_ref, gain_ref, scale_ref, first_ref, second_ref = refs[:5]
    hat_ref, inverse_ref, slope_ref, n_ref, h_ref = refs[5:10]
    refs = refs[10 + kept :]
    dx_ref, outs, turned_ref = refs[0], refs[1:5], refs[5]
    dy_buf, dn_buf, dspread_buf, both_buf, turned_buf = refs[6:11]
    hat_buf, inverse_buf, slope_buf, n_buf, h_buf = refs[11:16]
    padded, total, conv_out, sems, piece_sems, in_sems = refs[16:]
    both_out = outs[3]
    which = tick - (sections - 1 - sec_ref[0])
    channels = dx_ref.shape[-1]
    hid = h_buf.shape[-1]
    pieces = hid // channels

    @pl.when((which >= 0) & (which < micro))
    def _():
        height, width, _ = dx_ref.shape
        rows = height * width
        ins = [
            pltpu.make_async_copy(
                slope_ref.at[which, :, columns(piece, channels)],
                slope_buf.at[:, columns(piece, channels)],
                in_sems.at[piece],
            )
            for piece in range(pieces)
        ]
        ins.append(pltpu.make_async_copy(hat_ref.at[which], hat_buf, in_sems.at[pieces]))
        ins.append(pltpu.make_async_copy(inverse_ref.at[which], inverse_buf, in_sems.at[pieces + 1]))
        for copy in ins:
            copy.start()
        dy = jnp.where(
            sec_ref[0] == sections - 1, slope_in_ref[0].astype(F32), returned_ref[...].astype(F32)
        )
        flat = dy.reshape(rows, channels)
        dy_buf[...] = flat.astype(BF16)
        mix_at = columns(pieces, channels)
        both_buf[:, mix_at] = (flat * scale_ref[...]).astype(BF16)
        total[...] = jnp.zeros(total.shape, F32)
        contract = (((1,), (1,)), ((), ()))
        copies = [
            pltpu.make_async_copy(buf, out.at[which], sems.at[index])
            for index, (buf, out) in enumerate(zip((dy_buf, dn_buf, dspread_buf), outs))
        ]
        copies[0].start()

        def both_copy(piece):
            at = columns(piece, channels)
            return pltpu.make_async_copy(
                both_buf.at[:, at], both_out.at[which, :, at], piece_sems.at[piece]
            )

        both_copy(pieces).start()

        def body(piece, carry):
            at = columns(piece, channels)
            dh = lax.dot_general(
                both_buf[:, mix_at], second_ref[at, :], contract, preferred_element_type=F32
            )
            pltpu.make_async_copy(
                slope_ref.at[which, :, at], slope_buf.at[:, at], in_sems.at[piece]
            ).wait()
            dpre = (dh * slope_buf[:, at].astype(F32)).astype(BF16)
            both_buf[:, at] = dpre
            both_copy(piece).start()
            total[...] += lax.dot_general(
                dpre, first_ref[:, at], contract, preferred_element_type=F32
            )
            return carry

        lax.fori_loop(0, pieces, body, 0)
        ins[pieces].wait()
        ins[pieces + 1].wait()
        dn = total[...]
        dn_buf[...] = dn.astype(BF16)
        copies[1].start()
        hat = hat_buf[...]
        dhat = dn * gain_ref[...]
        mean = jnp.mean(dhat, axis=-1, keepdims=True)
        along = jnp.mean(dhat * hat, axis=-1, keepdims=True)
        dspread = inverse_buf[:, 0:1] * (dhat - mean - hat * along)
        dspread_buf[...] = dspread
        copies[2].start()
        if tick < micro + sections - 2:
            fill_padded(padded, dspread.reshape(height, width, channels))

            def conv_body(chunk, carry):
                def store(out, value):
                    conv_out[out, :, lanes(chunk)] = value

                convolve(padded, chunk, kernel_ref, height, width, True, store)
                return carry

            lax.fori_loop(0, channels // TILE, conv_body, 0)
            dx = dy + conv_out[...]
            dx = jnp.where(real_columns(dx.shape, side), dx, 0.0)
            dx_ref[...] = dx.astype(BF16)
        for copy in copies:
            copy.wait()
        for piece in range(pieces + 1):
            both_copy(piece).wait()

    if turns:
        wanted = which == -1
        if tick == micro:
            wanted = wanted | (sec_ref[0] == sections - 1)

        @pl.when(wanted)
        def _():
            get_n = pltpu.make_async_copy(n_ref, n_buf, sems.at[0])
            get_h = pltpu.make_async_copy(h_ref, h_buf, sems.at[1])
            get_n.start()
            get_h.start()
            get_h.wait()
            get_n.wait()
            depth = turned_buf.shape[1]

            def turn(piece, carry):
                at = columns(piece, channels)
                turned_buf[at, :] = h_buf[:, :, at].reshape(depth, channels).T
                return carry

            lax.fori_loop(0, pieces, turn, 0)
            turned_buf[columns(pieces, channels), :] = n_buf[...].reshape(depth, channels).T
            put = pltpu.make_async_copy(turned_buf, turned_ref, sems.at[2])
            put.start()
            put.wait()


def small_kernel(micro, *refs):
    (kernel_ref, bias_ref, gain_ref, shift_ref, first_bias_ref, second_bias_ref, scale_ref) = refs[:7]
    x_ref, hat_ref, mixed_ref, dy_ref, dn_ref, dspread_ref, both_ref = refs[7:14]
    outs = refs[14:21]
    padded = refs[21]
    height, width, channels = x_ref.shape[1:]

    def total(values):
        return jnp.sum(values, axis=0, keepdims=True)

    def chunk_body(chunk, carry):
        at = lanes(chunk)
        scale = scale_ref[0:1, at]
        sums = [0.0] * 5
        for item in range(micro):
            dy = dy_ref[item, :, at].astype(F32)
            dn = dn_ref[item, :, at].astype(F32)
            sums[0] += total(dspread_ref[item, :, at])
            sums[1] += total(dn * hat_ref[item, :, at])
            sums[2] += total(dn)
            sums[3] += total(dy)
            sums[4] += total(dy * mixed_ref[item, :, at])
        outs[1][0:1, at] = bias_ref[0:1, at] - learning_rate * sums[0]
        outs[2][0:1, at] = gain_ref[0:1, at] - learning_rate * sums[1]
        outs[3][0:1, at] = shift_ref[0:1, at] - learning_rate * sums[2]
        outs[5][0:1, at] = second_bias_ref[0:1, at] - learning_rate * (scale * sums[3])
        outs[6][0:1, at] = scale - learning_rate * sums[4]
        padded[...] = jnp.zeros(padded.shape, F32)
        for item in range(micro):
            padded[item, REACH : REACH + height, EDGE : EDGE + width, :] = x_ref[
                item, :, :, at
            ].astype(F32)
        for col in range(TAPS):
            for row in range(TAPS):
                acc = None
                for item in range(micro):
                    for out in range(height):
                        term = (
                            padded[item, out + row, pl.ds(EDGE - REACH + col, width), :]
                            * dspread_ref[item, out * width : (out + 1) * width, at]
                        )
                        acc = term if acc is None else acc + term
                tap = row * TAPS + col
                outs[0][tap, 0:1, at] = kernel_ref[tap, 0:1, at] - learning_rate * total(acc)
        return carry

    lax.fori_loop(0, channels // TILE, chunk_body, 0)
    hid = first_bias_ref.shape[1]

    def bias_body(piece, carry):
        at = lanes(piece)
        acc = 0.0
        for item in range(micro):
            acc += total(both_ref[item, :, at].astype(F32))
        outs[4][0:1, at] = first_bias_ref[0:1, at] - learning_rate * acc
        return carry

    lax.fori_loop(0, hid // TILE, bias_body, 0)


def block_views(block, first_tiles, groups, channels, first_ref, second_ref, act):
    @pl.when(block < first_tiles)
    def _():
        act(first_ref.at[:, lanes(block)])

    @pl.when(block >= first_tiles)
    def _():
        place = block - first_tiles
        group = lax.rem(place, groups)
        act(second_ref.at[columns(group, channels), lanes(lax.div(place, groups))])


def update_kernel(
    first_tiles, groups, sending, order_ref, slot_ref, turned_ref, both_ref, first_ref, second_ref, *refs
):
    if sending:
        (send_ref, wide_buf, slim_buf, in_sems, out_sems) = refs
    else:
        (own_ref, new_first, new_second, wide_buf, slim_buf, in_sems, out_sems, wide_sems) = refs
    count = wide_buf.shape[0]
    channels = wide_buf.shape[1]
    micro, rows, _ = both_ref.shape

    def fetch(step, carry):
        def act(view):
            pltpu.make_async_copy(view, wide_buf.at[step], in_sems.at[step]).start()

        block_views(order_ref[step], first_tiles, groups, channels, first_ref, second_ref, act)
        return carry

    lax.fori_loop(0, count, fetch, 0)

    def slim_copy(step):
        target = send_ref.at[slot_ref[step]] if sending else own_ref.at[order_ref[step]]
        return pltpu.make_async_copy(slim_buf.at[step], target, out_sems.at[step])

    def body(step, carry):
        block = order_ref[step]
        is_first = block < first_tiles
        place = jnp.maximum(block - first_tiles, 0)
        group = jnp.where(is_first, groups, lax.rem(place, groups))
        column = jnp.where(is_first, block, first_tiles + lax.div(place, groups))
        grad = jnp.dot(
            turned_ref[columns(group, channels), :],
            both_ref[:, :, lanes(column)].reshape(micro * rows, TILE),
            preferred_element_type=F32,
        )
        pltpu.make_async_copy(
            first_ref.at[:, lanes(0)], wide_buf.at[step], in_sems.at[step]
        ).wait()
        updated = wide_buf[step] - learning_rate * grad
        slim_buf[step] = updated.astype(BF16)
        slim_copy(step).start()
        if not sending:
            wide_buf[step] = updated

            def act(view):
                pltpu.make_async_copy(wide_buf.at[step], view, wide_sems.at[step]).start()

            block_views(block, first_tiles, groups, channels, new_first, new_second, act)
        return carry

    lax.fori_loop(0, count, body, 0)

    def drain(step, carry):
        slim_copy(step).wait()
        if not sending:
            pltpu.make_async_copy(
                wide_buf.at[step], new_first.at[:, lanes(0)], wide_sems.at[step]
            ).wait()
        return carry

    lax.fori_loop(0, count, drain, 0)


def place_kernel(
    first_tiles, groups, order_ref, slot_ref, arrived_ref, old_first, old_second, new_first, new_second, *refs
):
    wide_buf, slim_buf, in_sems, out_sems = refs
    count, channels, _ = wide_buf.shape

    def fetch(step, carry):
        pltpu.make_async_copy(
            arrived_ref.at[slot_ref[step]], slim_buf.at[step], in_sems.at[step]
        ).start()
        return carry

    lax.fori_loop(0, count, fetch, 0)

    def body(step, carry):
        pltpu.make_async_copy(arrived_ref.at[0], slim_buf.at[step], in_sems.at[step]).wait()
        wide_buf[step] = slim_buf[step].astype(F32)

        def act(view):
            pltpu.make_async_copy(wide_buf.at[step], view, out_sems.at[step]).start()

        block_views(order_ref[step], first_tiles, groups, channels, new_first, new_second, act)
        return carry

    lax.fori_loop(0, count, body, 0)

    def drain(step, carry):
        pltpu.make_async_copy(
            wide_buf.at[step], new_first.at[:, lanes(0)], out_sems.at[step]
        ).wait()
        return carry

    lax.fori_loop(0, count, drain, 0)


def params_of(limit=VMEM_LIMIT):
    return pltpu.CompilerParams(vmem_limit_bytes=limit)


def cost(flops, read):
    return pl.CostEstimate(flops=flops, bytes_accessed=read, transcendentals=0)


def hbm_spec():
    return pl.BlockSpec(memory_space=pltpu.HBM)


def train_step(tick, micro, side, sec, images, received, vectors, weights, saved):
    height, width, channels = received.shape
    rows = height * width
    hid = vectors[4].shape[1]
    saved_shapes = [
        ((height, width, channels), BF16),
        ((rows, channels), F32),
        ((rows, TILE), F32),
        ((rows, channels), BF16),
        ((rows, channels), F32),
        ((rows, hid), BF16),
        ((rows, hid), BF16),
    ]
    kept = 0 if saved is None else len(saved)
    at = min(tick, micro - 1)
    operands = [images, received, *vectors, *weights] + ([] if saved is None else list(saved))
    in_specs = [pl.BlockSpec((1, height, width, channels), lambda i, s: (at, 0, 0, 0))]
    in_specs += [whole(item) for item in operands[1 : len(operands) - kept]]
    in_specs += [hbm_spec()] * kept
    outs = pl.pallas_call(
        functools.partial(train_kernel, tick, micro, side, kept),
        grid_spec=pltpu.PrefetchScalarGridSpec(
            num_scalar_prefetch=1,
            grid=(1,),
            in_specs=in_specs,
            out_specs=[whole(received)] + [hbm_spec() for _ in saved_shapes],
            scratch_shapes=[pltpu.VMEM(shape, dtype) for shape, dtype in saved_shapes]
            + [
                pltpu.VMEM((channels // TILE, height + 2 * REACH, width + 2 * EDGE, TILE), F32),
                pltpu.VMEM((rows, channels), F32),
                pltpu.VMEM((rows, channels), F32),
                pltpu.SemaphoreType.DMA((5,)),
                pltpu.SemaphoreType.DMA((2, hid // channels)),
            ],
        ),
        out_shape=[shaped(received.shape, BF16)]
        + [pltpu.HBM((micro,) + shape, dtype) for shape, dtype in saved_shapes],
        input_output_aliases={1 + len(operands) - kept + i: 1 + i for i in range(kept)},
        compiler_params=params_of(),
        cost_estimate=cost(4 * rows * channels * hid, 8 << 20),
        name=f"train{tick}",
    )(sec, *operands)
    return outs[0], outs[1:]


def back_step(tick, micro, side, sections, sec, slopes, returned, params, saved, kept_out):
    height, width, channels = returned.shape
    rows = height * width
    hid = saved[2].shape[-1]
    shapes = [
        ((rows, channels), BF16),
        ((rows, channels), BF16),
        ((rows, channels), F32),
        ((rows, hid + channels), BF16),
    ]
    turned = ((hid + channels, micro * rows), BF16)
    kept = 0 if kept_out is None else len(kept_out)
    operands = [slopes, returned, *params, *saved]
    at = min(tick, micro - 1)
    in_specs = [pl.BlockSpec((1, height, width, channels), lambda i, s: (at, 0, 0, 0))]
    in_specs += [whole(item) for item in operands[1:7]]
    in_specs += [hbm_spec()] * (len(saved) + kept)
    base = len(operands)
    operands += [] if kept_out is None else list(kept_out)
    turns = tick <= max(sections - 2, micro)
    outs = pl.pallas_call(
        functools.partial(back_kernel, tick, micro, side, sections, kept, turns),
        grid_spec=pltpu.PrefetchScalarGridSpec(
            num_scalar_prefetch=1,
            grid=(1,),
            in_specs=in_specs,
            out_specs=[whole(returned)] + [hbm_spec()] * (len(shapes) + 1),
            scratch_shapes=[pltpu.VMEM(shape, dtype) for shape, dtype in shapes]
            + [
                pltpu.VMEM(*turned),
                pltpu.VMEM((rows, channels), F32),
                pltpu.VMEM((rows, TILE), F32),
                pltpu.VMEM((rows, hid), BF16),
                pltpu.VMEM((micro, rows, channels), BF16),
                pltpu.VMEM((micro, rows, hid), BF16),
                pltpu.VMEM((channels // TILE, height + 2 * REACH, width + 2 * EDGE, TILE), F32),
                pltpu.VMEM((rows, channels), F32),
                pltpu.VMEM((height, width, channels), F32),
                pltpu.SemaphoreType.DMA((3,)),
                pltpu.SemaphoreType.DMA((hid // channels + 1,)),
                pltpu.SemaphoreType.DMA((hid // channels + 2,)),
            ],
        ),
        out_shape=[shaped(returned.shape, BF16)]
        + [pltpu.HBM((micro,) + shape, dtype) for shape, dtype in shapes]
        + [pltpu.HBM(*turned)],
        input_output_aliases={1 + base + i: 1 + i for i in range(kept)},
        compiler_params=params_of(),
        cost_estimate=cost(4 * rows * channels * hid, 8 << 20),
        name=f"back{tick}",
    )(sec, *operands)
    return outs[0], outs[1:]


def small_step(micro, vectors, grads):
    x = grads[0]
    height, width, channels = x.shape[1:]
    return pl.pallas_call(
        functools.partial(small_kernel, micro),
        grid=(1,),
        in_specs=[whole(item) for item in vectors] + [whole(item) for item in grads],
        out_specs=[whole(item) for item in vectors],
        out_shape=[shaped(item.shape, F32) for item in vectors],
        scratch_shapes=[pltpu.VMEM((micro, height + 2 * REACH, width + 2 * EDGE, TILE), F32)],
        compiler_params=params_of(),
        cost_estimate=cost(1 << 28, 8 << 20),
        name="small",
    )(*vectors, *grads)


def tables(marked, sources):
    member = lax.axis_index("member")
    members = sources.shape[1]
    blocks = marked.shape[0]
    taken = blocks // 2
    capacity = (taken + members - 2) // (members - 1)
    ids = jnp.arange(blocks, dtype=jnp.int32)
    member_ids = jnp.arange(members, dtype=jnp.int32)
    target = jnp.sum(jnp.where(sources == member, member_ids[None, :], 0), axis=1)
    anchor = jnp.sum(jnp.where(member_ids[None, :] == member, sources, 0), axis=1)
    earlier = ids[:, None] > ids[None, :]
    counted = marked[None, :] == 1
    out_rank = jnp.sum(earlier & (target[:, None] == target[None, :]) & counted, axis=1)
    in_rank = jnp.sum(earlier & (anchor[:, None] == anchor[None, :]) & counted, axis=1)
    out_slot = (target * capacity + out_rank).astype(jnp.int32)
    in_slot = (anchor * capacity + in_rank).astype(jnp.int32)
    steps = jnp.arange(taken, dtype=jnp.int32)
    top = members * capacity - 1

    def listed(flags):
        place = jnp.sum(earlier & flags[None, :], axis=1)
        hits = flags[None, :] & (place[None, :] == steps[:, None])
        return hits, jnp.sum(jnp.where(hits, ids[None, :], 0), axis=1)

    is_marked = marked == 1
    hits, marked_order = listed(is_marked)
    send_slots = jnp.clip(jnp.sum(jnp.where(hits, out_slot[None, :], 0), axis=1), 0, top)
    take_slots = jnp.clip(jnp.sum(jnp.where(hits, in_slot[None, :], 0), axis=1), 0, top)
    _, plain_order = listed(~is_marked)
    return dict(
        slots=members * capacity,
        in_slot=jnp.clip(in_slot, 0, top),
        marked_order=marked_order.astype(jnp.int32),
        plain_order=plain_order.astype(jnp.int32),
        send_slots=send_slots.astype(jnp.int32),
        take_slots=take_slots.astype(jnp.int32),
    )


def update_step(sending, order, slots, turned, both, first, second, out_shape):
    count = order.shape[0]
    channels = first.shape[0]
    first_tiles = first.shape[1] // TILE
    groups = second.shape[0] // channels
    sems = [pltpu.SemaphoreType.DMA((count,))] * (2 if sending else 3)
    return pl.pallas_call(
        functools.partial(update_kernel, first_tiles, groups, sending),
        grid_spec=pltpu.PrefetchScalarGridSpec(
            num_scalar_prefetch=2,
            grid=(1,),
            in_specs=[whole(turned), whole(both), hbm_spec(), hbm_spec()],
            out_specs=[hbm_spec() for _ in out_shape],
            scratch_shapes=[
                pltpu.VMEM((count, channels, TILE), F32),
                pltpu.VMEM((count, channels, TILE), BF16),
                *sems,
            ],
        ),
        out_shape=out_shape,
        compiler_params=params_of(),
        cost_estimate=cost(1 << 30, 8 << 20),
        name="send" if sending else "keep",
    )(order, slots, turned, both, first, second)


def local(
    inputs,
    cotangent,
    probe,
    dw_kernel,
    dw_bias,
    norm_gain,
    norm_bias,
    w_in,
    b_in,
    w_out,
    b_out,
    layer_scale,
    shuffle_mask,
    source_member,
):
    sections = lax.axis_size("section")
    sec = lax.axis_index("section").astype(jnp.int32).reshape(1)
    micro = inputs.shape[1]
    height, side, channels = inputs.shape[3:]
    width = (side + 15) // 16 * 16
    rows = height * width
    hid = w_in.shape[3]
    first_tiles = hid // TILE
    groups = hid // channels
    vectors = [
        dw_kernel.reshape(TAPS * TAPS, 1, channels),
        dw_bias[0],
        norm_gain[0],
        norm_bias[0],
        b_in[0],
        b_out[0],
        layer_scale[0],
    ]
    first = w_in[0, 0]
    second = w_out[0, 0]
    lowered = [first.astype(BF16), second.astype(BF16)]

    def padded(maps):
        return jnp.pad(maps, ((0, 0), (0, 0), (0, width - side), (0, 0)))

    images = padded(inputs[0, :, 0])
    slopes = padded(cotangent[0, :, 0])
    trial = padded(probe[0])[0]
    ticks = micro + sections - 1
    received = images[0]
    saved = None
    for tick in range(ticks):
        current, saved = train_step(
            tick, micro, side, sec, images, received, vectors, lowered, saved
        )
        if tick < ticks - 1:
            pairs = [(s, s + 1) for s in range(sections - 1) if 0 <= tick - s < micro]
            received = lax.ppermute(current, "section", pairs)
    xs, hats, inverses, ns, mixes, hs, gelu_slopes = saved
    kernel, gain, scale = vectors[0], vectors[2], vectors[6]
    returned = slopes[0]
    grads = None
    for tick in range(ticks):
        current, grads = back_step(
            tick,
            micro,
            side,
            sections,
            sec,
            slopes,
            returned,
            (kernel, gain, scale, *lowered),
            (hats, inverses, gelu_slopes, ns, hs),
            grads,
        )
        if tick < ticks - 1:
            pairs = [
                (s, s - 1) for s in range(1, sections) if 0 <= tick - (sections - 1 - s) < micro
            ]
            returned = lax.ppermute(current, "section", pairs)
    dys, dns, dspreads, boths, turned = grads

    table = tables(shuffle_mask[0], source_member[0])
    taken = table["marked_order"].shape[0]
    blocks = shuffle_mask.shape[1]
    (outgoing,) = update_step(
        True,
        table["marked_order"],
        table["send_slots"],
        turned,
        boths,
        first,
        second,
        [pltpu.HBM((table["slots"], channels, TILE), BF16)],
    )
    arrived = lax.all_to_all(outgoing, "member", split_axis=0, concat_axis=0, tiled=True)
    own, new_first, new_second = update_step(
        False,
        table["plain_order"],
        table["plain_order"],
        turned,
        boths,
        first,
        second,
        [
            pltpu.HBM((blocks, channels, TILE), BF16),
            pltpu.HBM(first.shape, F32),
            pltpu.HBM(second.shape, F32),
        ],
    )
    vectors = small_step(micro, vectors, (xs, hats, mixes, dys, dns, dspreads, boths))

    new_first, new_second = pl.pallas_call(
        functools.partial(place_kernel, first_tiles, groups),
        grid_spec=pltpu.PrefetchScalarGridSpec(
            num_scalar_prefetch=2,
            grid=(1,),
            in_specs=[hbm_spec()] * 3,
            out_specs=[hbm_spec()] * 2,
            scratch_shapes=[
                pltpu.VMEM((taken, channels, TILE), F32),
                pltpu.VMEM((taken, channels, TILE), BF16),
                pltpu.SemaphoreType.DMA((taken,)),
                pltpu.SemaphoreType.DMA((taken,)),
            ],
        ),
        out_shape=[pltpu.HBM(first.shape, F32), pltpu.HBM(second.shape, F32)],
        input_output_aliases={3: 0, 4: 1},
        compiler_params=params_of(),
        cost_estimate=cost(0, 8 << 20),
        name="place",
    )(table["marked_order"], table["take_slots"], arrived, new_first, new_second)

    received = trial
    features = None
    for tick in range(sections):
        operands = [trial, received, *vectors, own, arrived]
        in_specs = [whole(item) for item in operands[:-2]] + [hbm_spec(), hbm_spec()]
        kept = 0 if features is None else 1
        if kept:
            operands.append(features)
            in_specs.append(hbm_spec())
        result, features = pl.pallas_call(
            functools.partial(probe_kernel, tick, side, kept),
            grid_spec=pltpu.PrefetchScalarGridSpec(
                num_scalar_prefetch=3,
                grid=(1,),
                in_specs=in_specs,
                out_specs=[whole(trial), hbm_spec()],
                scratch_shapes=[
                    pltpu.VMEM((height, side, channels), BF16),
                    pltpu.VMEM((blocks, channels, TILE), BF16),
                    pltpu.VMEM(
                        (channels // TILE, height + 2 * REACH, width + 2 * EDGE, TILE), F32
                    ),
                    pltpu.VMEM((rows, channels), F32),
                    pltpu.VMEM((rows, channels), F32),
                    pltpu.VMEM((rows, channels), BF16),
                    pltpu.SemaphoreType.DMA((blocks,)),
                    pltpu.SemaphoreType.DMA,
                ],
            ),
            out_shape=[shaped(trial.shape, BF16), pltpu.HBM((height, side, channels), BF16)],
            input_output_aliases={2 + len(operands): 1} if kept else {},
            compiler_params=params_of(),
            cost_estimate=cost(4 * rows * channels * hid, 8 << 20),
            name=f"probe{tick}",
        )(sec, shuffle_mask[0], table["in_slot"], *operands)
        if tick < sections - 1:
            received = lax.ppermute(result, "section", [(tick, tick + 1)])
    return (new_first[None, None], new_second[None, None], features[None, None, None])


def solution(mesh):
    return jax.shard_map(
        local,
        mesh=mesh,
        in_specs=(
            P("member", None, None, None, None, None),
            P("member", None, None, None, None, None),
            P("member", None, None, None, None),
            P("member", "section", None, None, None),
            P("member", "section", None),
            P("member", "section", None),
            P("member", "section", None),
            P("member", "section", None, None),
            P("member", "section", None),
            P("member", "section", None, None),
            P("member", "section", None),
            P("member", "section", None),
            P("section", None),
            P("section", None, None),
        ),
        out_specs=(
            P("member", "section", None, None),
            P("member", "section", None, None),
            P("member", "section", None, None, None, None),
        ),
        check_vma=False,
    )
```

time: 287 us -> 283 us (0.986)
  the two profiles are of different devices: /device:TPU:4 before, /device:TPU:5 now
where the time goes in v2:
time: 283 us; the launch traced here: 282 us
  waiting for transfers between devices  140 us (49%)
  Pallas kernels  83.7 us (30%)
  local copies, waits for them, and re-layouts  32.7 us (12%)
  starting transfers between devices  19.3 us (7%)
  other arithmetic  5.11 us (2%)
    ppermute x3, waiting for transfers between devices, local(): received = lax.ppermute(result, 'section', [(tick, tick + 1)])  67.1 us
    all_to_all x1, waiting for transfers between devices, local(): lax.all_to_all(outgoing, 'member', split_axis=0, concat_axis=0, tiled=True)  37.6 us
    ppermute x4, waiting for transfers between devices, local(): received = lax.ppermute(current, 'section', pairs)  33.8 us
    unnamed x112, local copies, waits for them, and re-layouts  31.6 us
    pallas_call x5, Pallas kernels, back_step(): pl.pallas_call(functools.partial(back_kernel, tick, micro, side, sections...  24.4 us
    pallas_call x4, Pallas kernels, local(): pl.pallas_call(functools.partial(probe_kernel, tick, side, kept), grid_sp...  17.2 us
    pallas_call x2, Pallas kernels, update_step(): pl.pallas_call(functools.partial(update_kernel, first_tiles, groups, send...  15.3 us
    pallas_call x5, Pallas kernels, train_step(): pl.pallas_call(functools.partial(train_kernel, tick, micro, side, kept),...  15.1 us
  transfers between devices with their start and end apart: 12, of which 6 were waited for; matrix products, arithmetic and copies ran while one was open for 1% of the time, Pallas kernels for 7%

profile of v2, /device:TPU:5, one launch (start us, length us, event | category | flops | bytes accessed | tf_op | source)
XLA Modules:
  0.0 282.1 jit_solution(12322831080859139262)
XLA Ops:
  0.6 2.6 bitcast_convert_fusion.refs_8_.refs_4_
  9.6 28.5 %collective-permute-done.2.received_ref = bf16[14,16,512]{2,1,0:T(8,128)(2,1)S(1)} collective-permute-done((bf16[14,16,512]{2,1,0:T(8,128)(2,1)S(1)}, bf16[14,16,512]{2,1,0:T(8,128)(2,1)S(1)}, u32[]{:S(2)}, u32[]{:S(2)}) %collective-permute-start.2) | collective-permute-done | bytes 229408 | tf_op jit(solution)/shard_map/ppermute | solution.py:815
  38.1 7.0 %train3.1 = (bf16[14,16,512]{2,1,0:T(8,128)(2,1)S(1)}, bf16[2,14,16,512]{3,2,1,0:T(8,128)(2,1)}, f32[2,224,512]{2,1,0:T(8,128)}, f32[2,224,128]{2,1,0:T(8,128)},...) custom-call(s32[1]{0:T(128)} %bitcast.2.sec_ref, ...), custom_call_target="tpu_custom_call", output_to_operand_aliasing={{1}: (12, {}), {2}: (13, {}), {3}: (14, {}), {4}: (15, {}),... | custom-call | flops 939524096 | bytes 8388608 | tf_op jit(solution)/shard_map/train3/pallas_call | solution.py:601
  46.6 5.3 %collective-permute-done.3.received_ref = bf16[14,16,512]{2,1,0:T(8,128)(2,1)S(1)} collective-permute-done((bf16[14,16,512]{2,1,0:T(8,128)(2,1)S(1)}, bf16[14,16,512]{2,1,0:T(8,128)(2,1)S(1)}, u32[]{:S(2)}, u32[]{:S(2)}) %collective-permute-start.3) | collective-permute-done | bytes 229408 | tf_op jit(solution)/shard_map/ppermute | solution.py:815
  51.8 7.7 %train4.1 = (bf16[14,16,512]{2,1,0:T(8,128)(2,1)}, bf16[2,14,16,512]{3,2,1,0:T(8,128)(2,1)}, f32[2,224,512]{2,1,0:T(8,128)}, f32[2,224,128]{2,1,0:T(8,128)}, bf1...) custom-call(s32[1]{0:T(128)} %bitcast.2.sec_ref, ...), custom_call_target="tpu_custom_call", output_to_operand_aliasing={{1}: (12, {}), {2}: (13, {}), {3}: (14, {}), {4}: (15, {}),... | custom-call | flops 939524096 | bytes 8388608 | tf_op jit(solution)/shard_map/train4/pallas_call | solution.py:601
  65.7 8.1 %back0.1 = (bf16[14,16,512]{2,1,0:T(8,128)(2,1)}, bf16[2,224,512]{2,1,0:T(8,128)(2,1)}, bf16[2,224,512]{2,1,0:T(8,128)(2,1)}, f32[2,224,512]{2,1,0:T(8,128)}, bf...) custom-call(s32[1]{0:T(128)} %bitcast.2.sec_ref, bf16[2,14,16,512]{3,2,1,0:T(8,128)(2,1)S(1)} %pad.11.slope_in_ref, ...), custom_call_target="tpu_custom_call" | custom-call | flops 939524096 | bytes 8388608 | tf_op jit(solution)/shard_map/back0/pallas_call | solution.py:647
  73.9 2.0 collective-permute-start.4
  81.4 7.4 %back1.1 = (bf16[14,16,512]{2,1,0:T(8,128)(2,1)S(1)}, bf16[2,224,512]{2,1,0:T(8,128)(2,1)}, bf16[2,224,512]{2,1,0:T(8,128)(2,1)}, f32[2,224,512]{2,1,0:T(8,128)}...) custom-call(s32[1]{0:T(128)} %bitcast.2.sec_ref, ...), custom_call_target="tpu_custom_call", output_to_operand_aliasing={{1}: (13, {}), {2}: (14, {}), {3}: (15, {}), {4}: (16, {}),... | custom-call | flops 939524096 | bytes 8388608 | tf_op jit(solution)/shard_map/back1/pallas_call | solution.py:647
  88.8 2.3 collective-permute-start.5
  92.2 4.6 %back2.1 = (bf16[14,16,512]{2,1,0:T(8,128)(2,1)S(1)}, bf16[2,224,512]{2,1,0:T(8,128)(2,1)}, bf16[2,224,512]{2,1,0:T(8,128)(2,1)}, f32[2,224,512]{2,1,0:T(8,128)}...) custom-call(s32[1]{0:T(128)} %bitcast.2.sec_ref, ...), custom_call_target="tpu_custom_call", output_to_operand_aliasing={{1}: (13, {}), {2}: (14, {}), {3}: (15, {}), {4}: (16, {}),... | custom-call | flops 939524096 | bytes 8388608 | tf_op jit(solution)/shard_map/back2/pallas_call | solution.py:647
  98.1 1.7 back3.1
  101.2 2.6 back4.1
  104.1 1.6 copy-done.7
  105.8 1.7 copy-done.10
  107.5 7.5 %send.1 = bf16[24,512,128]{2,1,0:T(8,128)(2,1)} custom-call(s32[16]{0:T(128)S(1)} %get-tuple-element.181.order_ref, s32[16]{0:T(128)S(1)} %broadcast_clamp_fusion.1.slot_ref, bf16[2560,448]{1,0:T(8,128)(2,1)S(1)} %copy-done.10, bf16[2,224,2560]{2,1,0:T(8,128)(2,1)S(1)} %copy-done.7, f32[512,2048]{1,0:T(8,128)S(1)} %bitcast.40, f32[2048,512]{1,0:T(8,128)} %bitcast.103), custom_call_target="tpu_custom_call" | custom-call | flops 1073741824 | bytes 8388608 | tf_op jit(solution)/shard_map/send/pallas_call | solution.py:742
  115.1 7.1 %all-to-all-start = ((bf16[24,512,128]{2,1,0:T(8,128)(2,1)}), bf16[24,512,128]{2,1,0:T(8,128)(2,1)S(1)}, u32[]{:S(2)}, u32[]{:S(2)}) async-start(bf16[24,512,128]{2,1,0:T(8,128)(2,1)} %send.1), calls=%async_computation | async-start | bytes 6291456 | tf_op jit(solution)/shard_map/all_to_all | solution.py:853
  131.7 6.1 %small.1 = (f32[49,1,512]{2,1,0:T(1,128)S(1)}, f32[1,512]{1,0:T(1,128)S(1)}, f32[1,512]{1,0:T(1,128)S(1)}, f32[1,512]{1,0:T(1,128)S(1)}, f32[1,2048]{1,0:T(1,128...) custom-call(f32[49,1,512]{2,1,0:T(1,128)S(1)} %bitcast.52, f32[1,512]{1,0:T(1,128)S(1)} %bitcast.86, ...), custom_call_target="tpu_custom_call" | custom-call | flops 268435456 | bytes 8388608 | tf_op jit(solution)/shard_map/small/pallas_call | solution.py:684
  138.5 2.2 copy-done.19
  140.7 7.8 %keep.1 = (bf16[32,512,128]{2,1,0:T(8,128)(2,1)}, f32[512,2048]{1,0:T(8,128)}, f32[2048,512]{1,0:T(8,128)}) custom-call(s32[16]{0:T(128)S(1)} %select_reduce_fusion.order_ref.slot_ref, s32[16]{0:T(128)S(1)} %select_reduce_fusion.order_ref.slot_ref, bf16[2560,448]{1,0:T(8,128)(2,1)S(1)} %copy-done.11, bf16[2,224,2560]{2,1,0:T(8,128)(2,1)S(1)} %copy-done.9, ...), custom_call_target="tpu_custom_call" | custom-call | flops 1073741824 | bytes 8388608 | tf_op jit(solution)/shard_map/keep/pallas_call | solution.py:742
  148.4 37.6 %all-to-all-done.arrived_ref.refs_8_ = bf16[24,512,128]{2,1,0:T(8,128)(2,1)S(1)} async-done(((bf16[24,512,128]{2,1,0:T(8,128)(2,1)}), bf16[24,512,128]{2,1,0:T(8,128)(2,1)S(1)}, u32[]{:S(2)}, u32[]{:S(2)}) %all-to-all-start) | async-done | bytes 3145760 | tf_op jit(solution)/shard_map/all_to_all | solution.py:853
  186.1 2.2 copy-done.15
  194.7 5.7 %place.1 = (f32[512,2048]{1,0:T(8,128)}, f32[2048,512]{1,0:T(8,128)}) custom-call(s32[16]{0:T(128)S(1)} %copy-done.49, s32[16]{0:T(128)S(1)} %broadcast_clamp_fusion.2.slot_ref, bf16[24,512,128]{2,1,0:T(8,128)(2,1)S(1)} %all-to-all-done.arrived_ref.refs_8_, f32[512,2048]{1,0:T(8,128)} %get-tuple-element.153.old_first, ...), custom_call_target="tpu_custom_call", output_to_operand_aliasing={{0}: (3, {}), {1}: (4, {})} | custom-call | bytes 8388608 | tf_op jit(solution)/shard_map/place/pallas_call | solution.py:870
  200.4 67.1 %collective-permute-done.10.received_ref = bf16[14,16,512]{2,1,0:T(8,128)(2,1)S(1)} collective-permute-done((bf16[14,16,512]{2,1,0:T(8,128)(2,1)S(1)}, bf16[14,16,512]{2,1,0:T(8,128)(2,1)S(1)}, u32[]{:S(2)}, u32[]{:S(2)}) %collective-permute-start.10) | collective-permute-done | bytes 229408 | tf_op jit(solution)/shard_map/ppermute | solution.py:927
  267.5 14.5 %probe3.1 = (bf16[14,16,512]{2,1,0:T(8,128)(2,1)}, bf16[14,14,512]{2,1,0:T(8,128)(2,1)}) custom-call(s32[1]{0:T(128)} %bitcast.2.sec_ref, s32[32]{0:T(128)S(1)} %bitcast.102, s32[32]{0:T(128)S(1)} %copy-done.45, bf16[14,16,512]{2,1,0:T(8,128)(2,1)S(1)} %pad_bitcast_fusion.image_ref.received_ref, ...), custom_call_target="tpu_custom_call", output_to_operand_aliasing={{1}: (14, {})} | custom-call | flops 939524096 | bytes 8388608 | tf_op jit(solution)/shard_map/probe3/pallas_call | solution.py:900
  (147 shorter events, 39.8 us)
Async XLA Ops:
  4.1 47.7 %copy-start = (bf16[2048,512]{1,0:T(8,128)(2,1)}, bf16[2048,512]{1,0:T(8,128)(2,1)S(1)}, u32[]{:S(2)}) copy-start(bf16[2048,512]{1,0:T(8,128)(2,1)S(1)} %bitcast_convert_fusion.refs_8_.refs_4_) | copy-start | bytes 6291460
  5.3 54.2 %copy-start.1 = (bf16[512,2048]{1,0:T(8,128)(2,1)}, bf16[512,2048]{1,0:T(8,128)(2,1)S(1)}, u32[]{:S(2)}) copy-start(bf16[512,2048]{1,0:T(8,128)(2,1)S(1)} %bitcast_convert_fusion.1.refs_7_.refs_3_) | copy-start | bytes 6291460
  6.6 0.7 collective-permute-start
  7.4 0.7 collective-permute-start.1
  8.3 29.8 %collective-permute-start.2 = (bf16[14,16,512]{2,1,0:T(8,128)(2,1)S(1)}, bf16[14,16,512]{2,1,0:T(8,128)(2,1)S(1)}, u32[]{:S(2)}, u32[]{:S(2)}) collective-permute-start(bf16[14,16,512]{2,1,0:T(8,128)(2,1)S(1)} %get-tuple-element.106), channel_id=1, source_target_pairs={{1,2},{2,3},{5,6},{6,7},{9,10},{10,11},{13,14},{14,15},{17,18},{18... | collective-permute-start | bytes 688136 | tf_op jit(solution)/shard_map/ppermute | solution.py:815
  45.1 6.7 %collective-permute-start.3 = (bf16[14,16,512]{2,1,0:T(8,128)(2,1)S(1)}, bf16[14,16,512]{2,1,0:T(8,128)(2,1)S(1)}, u32[]{:S(2)}, u32[]{:S(2)}) collective-permute-start(bf16[14,16,512]{2,1,0:T(8,128)(2,1)S(1)} %get-tuple-element.114), channel_id=1, source_target_pairs={{2,3},{6,7},{10,11},{14,15},{18,19},{22,23},{26,27},{30,31}} | collective-permute-start | bytes 688136 | tf_op jit(solution)/shard_map/ppermute | solution.py:815
  46.5 13.0 %copy-start.26 = (bf16[2,14,16,512]{3,2,1,0:T(8,128)(2,1)}, bf16[2,14,16,512]{3,2,1,0:T(8,128)(2,1)S(1)}, u32[]{:S(2)}) copy-start(bf16[2,14,16,512]{3,2,1,0:T(8,128)(2,1)S(1)} %pad.11.slope_in_ref) | copy-start | bytes 1376260
  65.7 10.9 %copy-start.4 = (bf16[2,224,2048]{2,1,0:T(8,128)(2,1)S(1)}, bf16[2,224,2048]{2,1,0:T(8,128)(2,1)}, u32[]{:S(2)}) copy-start(bf16[2,224,2048]{2,1,0:T(8,128)(2,1)} %get-tuple-element.126.refs_9_) | copy-start | bytes 5505028
  65.7 10.9 %copy-start.13 = (f32[2,224,512]{2,1,0:T(8,128)S(1)}, f32[2,224,512]{2,1,0:T(8,128)}, u32[]{:S(2)}) copy-start(f32[2,224,512]{2,1,0:T(8,128)} %get-tuple-element.122.refs_5_.refs_8_) | copy-start | bytes 2752516
  65.7 10.9 %copy-start.21 = (bf16[2,224,512]{2,1,0:T(8,128)(2,1)S(1)}, bf16[2,224,512]{2,1,0:T(8,128)(2,1)}, u32[]{:S(2)}) copy-start(bf16[2,224,512]{2,1,0:T(8,128)(2,1)} %get-tuple-element.125.refs_8_) | copy-start | bytes 1376260
  65.7 10.9 %copy-start.25 = (f32[2,224,128]{2,1,0:T(8,128)S(1)}, f32[2,224,128]{2,1,0:T(8,128)}, u32[]{:S(2)}) copy-start(f32[2,224,128]{2,1,0:T(8,128)} %get-tuple-element.123.refs_6_) | copy-start | bytes 688132
  73.9 2.7 collective-permute-start.4
  81.4 9.7 %copy-start.52 = (s32[1,32,8]{1,2,0:T(8,128)S(1)}, s32[1,32,8]{1,2,0:T(8,128)}, u32[]{:S(2)}) copy-start(s32[1,32,8]{1,2,0:T(8,128)} %param.27) | copy-start | bytes 3076
  81.4 9.8 %copy-start.46 = (s32[1,32]{1,0:T(1,128)S(1)}, s32[1,32]{1,0:T(1,128)}, u32[]{:S(2)}) copy-start(s32[1,32]{1,0:T(1,128)} %param.26) | copy-start | bytes 388
  88.8 3.4 %collective-permute-start.5 = (bf16[14,16,512]{2,1,0:T(8,128)(2,1)S(1)}, bf16[14,16,512]{2,1,0:T(8,128)(2,1)S(1)}, u32[]{:S(2)}, u32[]{:S(2)}) collective-permute-start(bf16[14,16,512]{2,1,0:T(8,128)(2,1)S(1)} %get-tuple-element.133), channel_id=1, source_target_pairs={{2,1},{3,2},{6,5},{7,6},{10,9},{11,10},{14,13},{15,14},{18,17},{19... | collective-permute-start | bytes 688136 | tf_op jit(solution)/shard_map/ppermute | solution.py:837
  96.7 1.4 collective-permute-start.6
  99.9 1.3 collective-permute-start.7
  115.1 71.0 %all-to-all-start = ((bf16[24,512,128]{2,1,0:T(8,128)(2,1)}), bf16[24,512,128]{2,1,0:T(8,128)(2,1)S(1)}, u32[]{:S(2)}, u32[]{:S(2)}) async-start(bf16[24,512,128]{2,1,0:T(8,128)(2,1)} %send.1), calls=%async_computation | async-start | bytes 6291456 | tf_op jit(solution)/shard_map/all_to_all | solution.py:853
  140.7 45.4 %copy-start.45 = (s32[32]{0:T(128)S(1)}, s32[32]{0:T(128)}, u32[]{:S(2)}) copy-start(s32[32]{0:T(128)} %get-tuple-element.185.slot_ref) | copy-start | bytes 388
  140.7 45.4 %copy-start.47 = (s32[1,32]{1,0:T(1,128)S(1)}, s32[1,32]{1,0:T(1,128)}, u32[]{:S(2)}) copy-start(s32[1,32]{1,0:T(1,128)} %param.26) | copy-start | bytes 388
  190.0 0.7 collective-permute-start.8
  191.8 0.7 collective-permute-start.9
  193.4 74.1 %collective-permute-start.10 = (bf16[14,16,512]{2,1,0:T(8,128)(2,1)S(1)}, bf16[14,16,512]{2,1,0:T(8,128)(2,1)S(1)}, u32[]{:S(2)}, u32[]{:S(2)}) collective-permute-start(bf16[14,16,512]{2,1,0:T(8,128)(2,1)S(1)} %get-tuple-element.174), channel_id=1, source_target_pairs={{2,3},{6,7},{10,11},{14,15},{18,19},{22,23},{26,27},{30,31}} | collective-permute-start | bytes 688136 | tf_op jit(solution)/shard_map/ppermute | solution.py:927
  194.7 72.8 %copy-start.16 = (bf16[32,512,128]{2,1,0:T(8,128)(2,1)S(1)}, bf16[32,512,128]{2,1,0:T(8,128)(2,1)}, u32[]{:S(2)}) copy-start(bf16[32,512,128]{2,1,0:T(8,128)(2,1)} %get-tuple-element.169.refs_7_) | copy-start | bytes 12582916
  (43 other events, 112.7 us)

commit v3 on v2

--- a/solution.py
+++ b/solution.py
@@ -16,7 +16,7 @@
 EDGE = 8
 REACH = 3
 TAPS = 2 * REACH + 1
-VMEM_LIMIT = 44 * 1024 * 1024
+VMEM_LIMIT = 30 * 1024 * 1024
 
 ERF_TOP = (
     0.00022905065861350646,
@@ -575,6 +575,10 @@
     return pl.CostEstimate(flops=flops, bytes_accessed=read, transcendentals=0)
 
 
+def pinned(arrays):
+    return [pltpu.with_memory_space_constraint(item, pltpu.HBM) for item in arrays]
+
+
 def hbm_spec():
     return pl.BlockSpec(memory_space=pltpu.HBM)
 
@@ -594,7 +598,7 @@
     ]
     kept = 0 if saved is None else len(saved)
     at = min(tick, micro - 1)
-    operands = [images, received, *vectors, *weights] + ([] if saved is None else list(saved))
+    operands = [images, received, *vectors, *weights] + ([] if saved is None else pinned(saved))
     in_specs = [pl.BlockSpec((1, height, width, channels), lambda i, s: (at, 0, 0, 0))]
     in_specs += [whole(item) for item in operands[1 : len(operands) - kept]]
     in_specs += [hbm_spec()] * kept
@@ -636,13 +640,13 @@
     ]
     turned = ((hid + channels, micro * rows), BF16)
     kept = 0 if kept_out is None else len(kept_out)
-    operands = [slopes, returned, *params, *saved]
+    operands = [slopes, returned, *params, *pinned(saved)]
     at = min(tick, micro - 1)
     in_specs = [pl.BlockSpec((1, height, width, channels), lambda i, s: (at, 0, 0, 0))]
     in_specs += [whole(item) for item in operands[1:7]]
     in_specs += [hbm_spec()] * (len(saved) + kept)
     base = len(operands)
-    operands += [] if kept_out is None else list(kept_out)
+    operands += [] if kept_out is None else pinned(kept_out)
     turns = tick <= max(sections - 2, micro)
     outs = pl.pallas_call(
         functools.partial(back_kernel, tick, micro, side, sections, kept, turns),
@@ -691,7 +695,7 @@
         compiler_params=params_of(),
         cost_estimate=cost(1 << 28, 8 << 20),
         name="small",
-    )(*vectors, *grads)
+    )(*vectors, *pinned(grads))
 
 
 def tables(marked, sources):
@@ -756,7 +760,7 @@
         compiler_params=params_of(),
         cost_estimate=cost(1 << 30, 8 << 20),
         name="send" if sending else "keep",
-    )(order, slots, turned, both, first, second)
+    )(order, slots, *pinned((turned, both, first, second)))
 
 
 def local(
@@ -886,16 +890,16 @@
         compiler_params=params_of(),
         cost_estimate=cost(0, 8 << 20),
         name="place",
-    )(table["marked_order"], table["take_slots"], arrived, new_first, new_second)
+    )(table["marked_order"], table["take_slots"], *pinned((arrived, new_first, new_second)))
 
     received = trial
     features = None
     for tick in range(sections):
-        operands = [trial, received, *vectors, own, arrived]
+        operands = [trial, received, *vectors, *pinned((own, arrived))]
         in_specs = [whole(item) for item in operands[:-2]] + [hbm_spec(), hbm_spec()]
         kept = 0 if features is None else 1
         if kept:
-            operands.append(features)
+            operands += pinned([features])
             in_specs.append(hbm_spec())
         result, features = pl.pallas_call(
             functools.partial(probe_kernel, tick, side, kept),

time: 283 us -> 236 us (0.83)
  local copies, waits for them, and re-layouts: 32.7 us -> 4.32 us
  waiting for transfers between devices: 140 us -> 132 us
  Pallas kernels: 83.7 us -> 76.1 us
    unnamed x112 -> x32, local copies, waits for them, and re-layouts: 31.6 us -> 4.16 us
    ppermute x3, waiting for transfers between devices: 67.1 us -> 50.8 us  [local(): received = lax.ppermute(result, 'section', [(tick, tick + 1)])]
    all_to_all x1, waiting for transfers between devices: 37.6 us -> 45.3 us  [local(): lax.all_to_all(outgoing, 'member', split_axis=0, concat_axis=0, tiled=True)]
    pallas_call x5, Pallas kernels: 24.4 us -> 16.7 us  [back_step(): pl.pallas_call(functools.partial(back_kernel, tick, micro, side, sections...]
    pallas_call x4, Pallas kernels: 17.2 us -> 11.5 us  [local(): pl.pallas_call(functools.partial(probe_kernel, tick, side, kept), grid_sp...]
    pallas_call x2, Pallas kernels: 15.3 us -> 20.2 us  [update_step(): pl.pallas_call(functools.partial(update_kernel, first_tiles, groups, send...]
    pallas_call x1, Pallas kernels: 6.1 us -> 8.98 us  [small_step(): pl.pallas_call(functools.partial(small_kernel, micro), grid=(1,), in_spec...]
  transfers between devices with their start and end apart: 12 -> 12, of which waited for: 6 -> 6; matrix products, arithmetic and copies ran while one was open for 1% -> 0% of each run, Pallas kernels for 7% -> 10%
where the time goes in v3:
time: 236 us
  waiting for transfers between devices  132 us (56%)
  Pallas kernels  76.1 us (32%)
  starting transfers between devices  18.7 us (8%)
  local copies, waits for them, and re-layouts  4.32 us (2%)
  other arithmetic  3.64 us (2%)
    ppermute x3, waiting for transfers between devices, local(): received = lax.ppermute(result, 'section', [(tick, tick + 1)])  50.8 us
    all_to_all x1, waiting for transfers between devices, local(): lax.all_to_all(outgoing, 'member', split_axis=0, concat_axis=0, tiled=True)  45.3 us
    ppermute x4, waiting for transfers between devices, local(): received = lax.ppermute(current, 'section', pairs)  33.6 us
    pallas_call x2, Pallas kernels, update_step(): pl.pallas_call(functools.partial(update_kernel, first_tiles, groups, send...  20.2 us
    pallas_call x5, Pallas kernels, back_step(): pl.pallas_call(functools.partial(back_kernel, tick, micro, side, sections...  16.7 us
    pallas_call x5, Pallas kernels, train_step(): pl.pallas_call(functools.partial(train_kernel, tick, micro, side, kept),...  15 us
    pallas_call x4, Pallas kernels, local(): pl.pallas_call(functools.partial(probe_kernel, tick, side, kept), grid_sp...  11.5 us
    pallas_call x1, Pallas kernels, small_step(): pl.pallas_call(functools.partial(small_kernel, micro), grid=(1,), in_spec...  8.98 us
  transfers between devices with their start and end apart: 12, of which 6 were waited for; matrix products, arithmetic and copies ran while one was open for 0% of the time, Pallas kernels for 10%

profile of v3, /device:TPU:5, one launch (start us, length us, event | category | flops | bytes accessed | tf_op | source)
XLA Modules:
  0.0 235.8 jit_solution(7502475753890770462)
XLA Ops:
  0.6 2.6 %bitcast_convert_fusion.refs_8_.refs_4_ = bf16[2048,512]{1,0:T(8,128)(2,1)S(1)} fusion(f32[1,1,2048,512]{3,2,1,0:T(8,128)} %param.23), kind=kLoop, calls=%fused_computation.36 | loop fusion | flops 1048576 | bytes 6291456 | tf_op jit(solution)/shard_map/convert_element_type | solution.py:802
  8.0 1.3 collective-permute-start.2
  9.3 28.4 %collective-permute-done.2.received_ref = bf16[14,16,512]{2,1,0:T(8,128)(2,1)S(1)} collective-permute-done((bf16[14,16,512]{2,1,0:T(8,128)(2,1)S(1)}, bf16[14,16,512]{2,1,0:T(8,128)(2,1)S(1)}, u32[]{:S(2)}, u32[]{:S(2)}) %collective-permute-start.2) | collective-permute-done | bytes 229408 | tf_op jit(solution)/shard_map/ppermute | solution.py:819
  37.7 7.0 %train3.1 = (bf16[14,16,512]{2,1,0:T(8,128)(2,1)S(1)}, bf16[2,14,16,512]{3,2,1,0:T(8,128)(2,1)}, f32[2,224,512]{2,1,0:T(8,128)}, f32[2,224,128]{2,1,0:T(8,128)},...) custom-call(s32[1]{0:T(128)} %bitcast.2.sec_ref, ...), custom_call_target="tpu_custom_call", output_to_operand_aliasing={{1}: (12, {}), {2}: (13, {}), {3}: (14, {}), {4}: (15, {}),... | custom-call | flops 939524096 | bytes 8388608 | tf_op jit(solution)/shard_map/train3/pallas_call | solution.py:605
  44.7 1.3 collective-permute-start.3
  46.1 5.2 %collective-permute-done.3.received_ref = bf16[14,16,512]{2,1,0:T(8,128)(2,1)S(1)} collective-permute-done((bf16[14,16,512]{2,1,0:T(8,128)(2,1)S(1)}, bf16[14,16,512]{2,1,0:T(8,128)(2,1)S(1)}, u32[]{:S(2)}, u32[]{:S(2)}) %collective-permute-start.3) | collective-permute-done | bytes 229408 | tf_op jit(solution)/shard_map/ppermute | solution.py:819
  51.4 7.7 %train4.1 = (bf16[14,16,512]{2,1,0:T(8,128)(2,1)}, bf16[2,14,16,512]{3,2,1,0:T(8,128)(2,1)}, f32[2,224,512]{2,1,0:T(8,128)}, f32[2,224,128]{2,1,0:T(8,128)}, bf1...) custom-call(s32[1]{0:T(128)} %bitcast.2.sec_ref, ...), custom_call_target="tpu_custom_call", output_to_operand_aliasing={{1}: (12, {}), {2}: (13, {}), {3}: (14, {}), {4}: (15, {}),... | custom-call | flops 939524096 | bytes 8388608 | tf_op jit(solution)/shard_map/train4/pallas_call | solution.py:605
  59.0 5.6 %back0.1 = (bf16[14,16,512]{2,1,0:T(8,128)(2,1)S(1)}, bf16[2,224,512]{2,1,0:T(8,128)(2,1)}, bf16[2,224,512]{2,1,0:T(8,128)(2,1)}, f32[2,224,512]{2,1,0:T(8,128)}...) custom-call(s32[1]{0:T(128)} %bitcast.2.sec_ref, bf16[2,14,16,512]{3,2,1,0:T(8,128)(2,1)S(1)} %pad.11.slope_in_ref, ...), custom_call_target="tpu_custom_call" | custom-call | flops 939524096 | bytes 8388608 | tf_op jit(solution)/shard_map/back0/pallas_call | solution.py:651
  64.7 1.3 collective-permute-start.4
  66.0 1.1 collective-permute-done.4.returned_ref
  67.1 1.6 copy-done.1
  68.7 5.7 %back1.1 = (bf16[14,16,512]{2,1,0:T(8,128)(2,1)S(1)}, bf16[2,224,512]{2,1,0:T(8,128)(2,1)}, bf16[2,224,512]{2,1,0:T(8,128)(2,1)}, f32[2,224,512]{2,1,0:T(8,128)}...) custom-call(s32[1]{0:T(128)} %bitcast.2.sec_ref, ...), custom_call_target="tpu_custom_call", output_to_operand_aliasing={{1}: (13, {}), {2}: (14, {}), {3}: (15, {}), {4}: (16, {}),... | custom-call | flops 939524096 | bytes 8388608 | tf_op jit(solution)/shard_map/back1/pallas_call | solution.py:651
  74.4 2.3 collective-permute-start.5
  77.8 4.3 %back2.1 = (bf16[14,16,512]{2,1,0:T(8,128)(2,1)S(1)}, bf16[2,224,512]{2,1,0:T(8,128)(2,1)}, bf16[2,224,512]{2,1,0:T(8,128)(2,1)}, f32[2,224,512]{2,1,0:T(8,128)}...) custom-call(s32[1]{0:T(128)} %bitcast.2.sec_ref, ...), custom_call_target="tpu_custom_call", output_to_operand_aliasing={{1}: (13, {}), {2}: (14, {}), {3}: (15, {}), {4}: (16, {}),... | custom-call | flops 939524096 | bytes 8388608 | tf_op jit(solution)/shard_map/back2/pallas_call | solution.py:651
  84.9 9.9 %send.1 = bf16[24,512,128]{2,1,0:T(8,128)(2,1)} custom-call(s32[16]{0:T(128)S(1)} %get-tuple-element.181.order_ref, s32[16]{0:T(128)S(1)} %broadcast_clamp_fusion.1.slot_ref, bf16[2560,448]{1,0:T(8,128)(2,1)} %get-tuple-element.151.turned_ref, bf16[2,224,2560]{2,1,0:T(8,128)(2,1)} %get-tuple-element.152.both_ref.refs_13_, f32[512,2048]{1,0:T(8,128)} %bitcast.101, ...), custom_call_target="tpu_custom_call" | custom-call | flops 1073741824 | bytes 8388608 | tf_op jit(solution)/shard_map/send/pallas_call | solution.py:746
  94.8 7.1 %all-to-all-start = ((bf16[24,512,128]{2,1,0:T(8,128)(2,1)}), bf16[24,512,128]{2,1,0:T(8,128)(2,1)}, u32[]{:S(2)}, u32[]{:S(2)}) async-start(bf16[24,512,128]{2,1,0:T(8,128)(2,1)} %send.1), calls=%async_computation | async-start | bytes 6291456 | tf_op jit(solution)/shard_map/all_to_all | solution.py:857
  102.3 9.0 %small.1 = (f32[49,1,512]{2,1,0:T(1,128)S(1)}, f32[1,512]{1,0:T(1,128)S(1)}, f32[1,512]{1,0:T(1,128)S(1)}, f32[1,512]{1,0:T(1,128)S(1)}, f32[1,2048]{1,0:T(1,128...) custom-call(f32[49,1,512]{2,1,0:T(1,128)S(1)} %bitcast.50, f32[1,512]{1,0:T(1,128)S(1)} %bitcast.84, ...), custom_call_target="tpu_custom_call" | custom-call | flops 268435456 | bytes 8388608 | tf_op jit(solution)/shard_map/small/pallas_call | solution.py:688
  111.2 10.3 %keep.1 = (bf16[32,512,128]{2,1,0:T(8,128)(2,1)}, f32[512,2048]{1,0:T(8,128)}, f32[2048,512]{1,0:T(8,128)}) custom-call(s32[16]{0:T(128)S(1)} %select_reduce_fusion.order_ref.slot_ref, s32[16]{0:T(128)S(1)} %select_reduce_fusion.order_ref.slot_ref, bf16[2560,448]{1,0:T(8,128)(2,1)} %get-tuple-element.151.turned_ref, ...), custom_call_target="tpu_custom_call" | custom-call | flops 1073741824 | bytes 8388608 | tf_op jit(solution)/shard_map/keep/pallas_call | solution.py:746
  121.5 45.3 %all-to-all-done.arrived_ref.refs_8_ = bf16[24,512,128]{2,1,0:T(8,128)(2,1)} async-done(((bf16[24,512,128]{2,1,0:T(8,128)(2,1)}), bf16[24,512,128]{2,1,0:T(8,128)(2,1)}, u32[]{:S(2)}, u32[]{:S(2)}) %all-to-all-start) | async-done | bytes 3145760 | tf_op jit(solution)/shard_map/all_to_all | solution.py:857
  170.0 1.1 probe2.1
  171.1 1.3 collective-permute-start.10
  172.4 3.7 %place.1 = (f32[512,2048]{1,0:T(8,128)}, f32[2048,512]{1,0:T(8,128)}) custom-call(s32[16]{0:T(128)S(1)} %get-tuple-element.181.order_ref, s32[16]{0:T(128)S(1)} %broadcast_clamp_fusion.2.slot_ref, bf16[24,512,128]{2,1,0:T(8,128)(2,1)} %all-to-all-done.arrived_ref.refs_8_, ...), custom_call_target="tpu_custom_call", output_to_operand_aliasing={{0}: (3, {}), {1}: (4, {})} | custom-call | bytes 8388608 | tf_op jit(solution)/shard_map/place/pallas_call | solution.py:874
  176.1 50.8 %collective-permute-done.10.received_ref = bf16[14,16,512]{2,1,0:T(8,128)(2,1)S(1)} collective-permute-done((bf16[14,16,512]{2,1,0:T(8,128)(2,1)S(1)}, bf16[14,16,512]{2,1,0:T(8,128)(2,1)S(1)}, u32[]{:S(2)}, u32[]{:S(2)}) %collective-permute-start.10) | collective-permute-done | bytes 229408 | tf_op jit(solution)/shard_map/ppermute | solution.py:931
  226.9 8.7 %probe3.1 = (bf16[14,16,512]{2,1,0:T(8,128)(2,1)}, bf16[14,14,512]{2,1,0:T(8,128)(2,1)}) custom-call(s32[1]{0:T(128)} %bitcast.2.sec_ref, s32[32]{0:T(128)S(1)} %bitcast.100, s32[32]{0:T(128)S(1)} %get-tuple-element.185.slot_ref, bf16[14,16,512]{2,1,0:T(8,128)(2,1)S(1)} %pad_bitcast_fusion.image_ref.received_ref, ...), custom_call_target="tpu_custom_call", output_to_operand_aliasing={{1}: (14, {})} | custom-call | flops 939524096 | bytes 8388608 | tf_op jit(solution)/shard_map/probe3/pallas_call | solution.py:904
  (67 shorter events, 11.8 us)
Async XLA Ops:
  0.6 3.5 %copy-start.10 = (f32[1,1,512,2048]{3,2,1,0:T(8,128)S(1)}, f32[1,1,512,2048]{3,2,1,0:T(8,128)}, u32[]{:S(2)}) copy-start(f32[1,1,512,2048]{3,2,1,0:T(8,128)} %param.21) | copy-start | bytes 12582916
  4.1 1.0 copy-start.11
  5.1 53.9 %copy-start = (bf16[512,2048]{1,0:T(8,128)(2,1)}, bf16[512,2048]{1,0:T(8,128)(2,1)S(1)}, u32[]{:S(2)}) copy-start(bf16[512,2048]{1,0:T(8,128)(2,1)S(1)} %bitcast_convert_fusion.1.refs_7_.refs_3_) | copy-start | bytes 6291460
  5.1 1.0 copy-start.4
  5.1 1.0 copy-start.6
  5.1 1.0 copy-start.7
  5.1 1.1 copy-start.8
  6.3 0.7 collective-permute-start
  7.2 0.7 collective-permute-start.1
  8.0 29.7 %collective-permute-start.2 = (bf16[14,16,512]{2,1,0:T(8,128)(2,1)S(1)}, bf16[14,16,512]{2,1,0:T(8,128)(2,1)S(1)}, u32[]{:S(2)}, u32[]{:S(2)}) collective-permute-start(bf16[14,16,512]{2,1,0:T(8,128)(2,1)S(1)} %get-tuple-element.106), channel_id=1, source_target_pairs={{1,2},{2,3},{5,6},{6,7},{9,10},{10,11},{13,14},{14,15},{17,18},{18... | collective-permute-start | bytes 688136 | tf_op jit(solution)/shard_map/ppermute | solution.py:819
  37.7 8.3 %copy-start.12 = (bf16[1,2,1,14,14,512]{5,1,4,3,2,0:T(2,128)(2,1)S(1)}, bf16[1,2,1,14,14,512]{5,1,4,3,2,0:T(2,128)(2,1)}, u32[]{:S(2)}) copy-start(bf16[1,2,1,14,14,512]{5,1,4,3,2,0:T(2,128)(2,1)} %param.15) | copy-start | bytes 1204228
  44.7 6.7 %collective-permute-start.3 = (bf16[14,16,512]{2,1,0:T(8,128)(2,1)S(1)}, bf16[14,16,512]{2,1,0:T(8,128)(2,1)S(1)}, u32[]{:S(2)}, u32[]{:S(2)}) collective-permute-start(bf16[14,16,512]{2,1,0:T(8,128)(2,1)S(1)} %get-tuple-element.114), channel_id=1, source_target_pairs={{2,3},{6,7},{10,11},{14,15},{18,19},{22,23},{26,27},{30,31}} | collective-permute-start | bytes 688136 | tf_op jit(solution)/shard_map/ppermute | solution.py:819
  64.7 2.4 %collective-permute-start.4 = (bf16[14,16,512]{2,1,0:T(8,128)(2,1)S(1)}, bf16[14,16,512]{2,1,0:T(8,128)(2,1)S(1)}, u32[]{:S(2)}, u32[]{:S(2)}) collective-permute-start(bf16[14,16,512]{2,1,0:T(8,128)(2,1)S(1)} %get-tuple-element.127), channel_id=1, source_target_pairs={{3,2},{7,6},{11,10},{15,14},{19,18},{23,22},{27,26},{31,30}} | collective-permute-start | bytes 688136 | tf_op jit(solution)/shard_map/ppermute | solution.py:841
  67.1 1.6 copy-start.1
  68.7 8.1 %copy-start.14 = (s32[1,32,8]{1,2,0:T(8,128)S(1)}, s32[1,32,8]{1,2,0:T(8,128)}, u32[]{:S(2)}) copy-start(s32[1,32,8]{1,2,0:T(8,128)} %param.27) | copy-start | bytes 3076
  68.7 8.2 %copy-start.9 = (s32[1,32]{1,0:T(1,128)S(1)}, s32[1,32]{1,0:T(1,128)}, u32[]{:S(2)}) copy-start(s32[1,32]{1,0:T(1,128)} %param.26) | copy-start | bytes 388
  74.4 3.4 %collective-permute-start.5 = (bf16[14,16,512]{2,1,0:T(8,128)(2,1)S(1)}, bf16[14,16,512]{2,1,0:T(8,128)(2,1)S(1)}, u32[]{:S(2)}, u32[]{:S(2)}) collective-permute-start(bf16[14,16,512]{2,1,0:T(8,128)(2,1)S(1)} %get-tuple-element.133), channel_id=1, source_target_pairs={{2,1},{3,2},{6,5},{7,6},{10,9},{11,10},{14,13},{15,14},{18,17},{19... | collective-permute-start | bytes 688136 | tf_op jit(solution)/shard_map/ppermute | solution.py:841
  82.1 0.9 collective-permute-start.6
  83.2 0.8 collective-permute-start.7
  94.8 7.4 %copy-start.13 = (bf16[1,1,14,14,512]{4,3,2,1,0:T(8,128)(2,1)S(1)}, bf16[1,1,14,14,512]{4,3,2,1,0:T(8,128)(2,1)}, u32[]{:S(2)}) copy-start(bf16[1,1,14,14,512]{4,3,2,1,0:T(8,128)(2,1)} %param.16) | copy-start | bytes 602116
  94.8 72.0 %all-to-all-start = ((bf16[24,512,128]{2,1,0:T(8,128)(2,1)}), bf16[24,512,128]{2,1,0:T(8,128)(2,1)}, u32[]{:S(2)}, u32[]{:S(2)}) async-start(bf16[24,512,128]{2,1,0:T(8,128)(2,1)} %send.1), calls=%async_computation | async-start | bytes 6291456 | tf_op jit(solution)/shard_map/all_to_all | solution.py:857
  167.7 0.7 collective-permute-start.8
  169.3 0.7 collective-permute-start.9
  171.1 55.8 %collective-permute-start.10 = (bf16[14,16,512]{2,1,0:T(8,128)(2,1)S(1)}, bf16[14,16,512]{2,1,0:T(8,128)(2,1)S(1)}, u32[]{:S(2)}, u32[]{:S(2)}) collective-permute-start(bf16[14,16,512]{2,1,0:T(8,128)(2,1)S(1)} %get-tuple-element.174), channel_id=1, source_target_pairs={{2,3},{6,7},{10,11},{14,15},{18,19},{22,23},{26,27},{30,31}} | collective-permute-start | bytes 688136 | tf_op jit(solution)/shard_map/ppermute | solution.py:931
  (3 other events, 2.9 us)

commit v4 on v3

--- a/solution.py
+++ b/solution.py
@@ -16,36 +16,20 @@
 EDGE = 8
 REACH = 3
 TAPS = 2 * REACH + 1
-VMEM_LIMIT = 30 * 1024 * 1024
-
-ERF_TOP = (
-    0.00022905065861350646,
-    0.0034082910107109506,
-    0.050955695062380861,
-    0.18520832239976145,
-    1.128379143519084,
-)
-ERF_LOW = (
-    -1.1791602954361697e-7,
-    0.000023547966471313185,
-    0.0010179625278914885,
-    0.014070470171167667,
-    0.11098505178285362,
-    0.49746925110067538,
-    1.0,
-)
-
-
-def erf(value):
-    value = jnp.clip(value, -3.832506856900711, 3.832506856900711)
-    square = value * value
-    top = jnp.full_like(square, ERF_TOP[0])
-    for term in ERF_TOP[1:]:
-        top = top * square + term
-    low = jnp.full_like(square, ERF_LOW[0])
-    for term in ERF_LOW[1:]:
-        low = low * square + term
-    return value * top / low
+VMEM_LIMIT = 36 * 1024 * 1024
+
+TURN = 0.3275911 * math.sqrt(0.5)
+TERMS = (1.061405429, -1.453152027, 1.421413741, -0.284496736, 0.254829592)
+
+
+def normal_below(pre):
+    bell = jnp.exp2((pre * pre) * (-0.5 * math.log2(math.e)))
+    turn = 1.0 / (1.0 + TURN * jnp.abs(pre))
+    poly = jnp.full_like(turn, 0.5 * TERMS[0])
+    for term in TERMS[1:]:
+        poly = poly * turn + 0.5 * term
+    tail = poly * turn * bell
+    return jnp.where(pre >= 0.0, 1.0 - tail, tail), bell
 
 
 def whole(array):
@@ -70,7 +54,7 @@
             if flip:
                 at = TAPS * TAPS - 1 - at
             taps.append(kernel_ref[at, 0:1, lanes(chunk)])
-        for line in range(height + TAPS - 1):
+        for line in range(REACH, REACH + height):
             values = padded[chunk, line, pl.ds(EDGE - REACH + col, width), :]
             for row in range(TAPS):
                 out = line - row
@@ -102,12 +86,9 @@
     return offset * inverse, inverse
 
 
-def forward_core(
-    side, vectors, widened, padded, spread, total, weights, n_ref, hat_store, hidden_store
-):
-    kernel_ref, bias_ref, gain_ref, shift_ref, first_bias_ref, second_bias_ref, scale_ref = vectors
+def conv_norm(vectors, widened, padded, spread, n_ref, hat_store):
+    kernel_ref, bias_ref, gain_ref, shift_ref = vectors[:4]
     height, width, channels = widened.shape
-    hid = first_bias_ref.shape[1]
     fill_padded(padded, widened)
 
     def conv_body(chunk, carry):
@@ -123,15 +104,21 @@
     hat, inverse = normalise(spread[...])
     n_ref[...] = (hat * gain_ref[...] + shift_ref[...]).astype(BF16)
     hat_store(hat, inverse)
+
+
+def mix(side, vectors, widened, total, weights, n_ref, hidden_store):
+    first_bias_ref, second_bias_ref, scale_ref = vectors[4:]
+    height, width, channels = widened.shape
+    hid = first_bias_ref.shape[1]
     total[...] = jnp.zeros(total.shape, F32)
 
     def mix_body(piece, carry):
         first, second = weights(piece)
-        at = pl.ds(pl.multiple_of(piece * channels, channels), channels)
+        at = columns(piece, channels)
         pre = jnp.dot(n_ref[...], first, preferred_element_type=F32) + first_bias_ref[:, at]
-        below = 0.5 + 0.5 * erf(pre * math.sqrt(0.5))
+        below, bell = normal_below(pre)
         hidden = (pre * below).astype(BF16)
-        hidden_store(piece, hidden, pre, below)
+        hidden_store(piece, hidden, pre, below, bell)
         total[...] += jnp.dot(hidden, second, preferred_element_type=F32)
         return carry
 
@@ -154,22 +141,57 @@
 def train_kernel(tick, micro, side, kept, sec_ref, image_ref, received_ref, *refs):
     vectors, (first_ref, second_ref) = refs[:7], refs[7:9]
     refs = refs[9 + kept :]
-    y_ref, outs, bufs = refs[0], refs[1:8], refs[8:15]
-    padded, spread, total, sems, piece_sems = refs[15:]
+    y_ref, outs = refs[0], refs[1:8]
+    refs = refs[8:]
+    if tick == 0:
+        low_first, low_second = refs[:2]
+        refs = refs[2:]
+        wide_first, wide_second, wide_sems = refs[12:]
+    bufs = refs[:7]
+    padded, spread, total, sems, piece_sems = refs[7:12]
     x_buf, hat_buf, inverse_buf, n_buf, mixed_buf, h_buf, slope_buf = bufs
     h_out, slope_out = outs[5:]
-
-    @pl.when(is_active(sec_ref, tick, micro))
+    channels = x_buf.shape[-1]
+    pieces = h_buf.shape[-1] // channels
+    active = is_active(sec_ref, tick, micro)
+
+    def wide_copies(piece):
+        at = columns(piece, channels)
+        return [
+            pltpu.make_async_copy(first_ref.at[:, at], wide_first.at[piece], wide_sems.at[0, piece]),
+            pltpu.make_async_copy(second_ref.at[at, :], wide_second.at[piece], wide_sems.at[1, piece]),
+        ]
+
+    def weights(piece):
+        at = columns(piece, channels)
+        if tick > 0:
+            return first_ref[:, at], second_ref[at, :]
+        for copy in wide_copies(piece):
+            copy.wait()
+        first = wide_first[piece].astype(BF16)
+        second = wide_second[piece].astype(BF16)
+        low_first[:, at] = first
+        low_second[at, :] = second
+        return first, second
+
+    if tick == 0:
+        for piece in range(pieces):
+            for copy in wide_copies(piece):
+                copy.start()
+
+        @pl.when(jnp.logical_not(active))
+        def _():
+            def body(piece, carry):
+                weights(piece)
+                return carry
+
+            lax.fori_loop(0, pieces, body, 0)
+
+    @pl.when(active)
     def _():
         slot = tick - sec_ref[0]
-        channels = x_buf.shape[-1]
-        pieces = h_buf.shape[-1] // channels
         entry = jnp.where(sec_ref[0] == 0, image_ref[0].astype(F32), received_ref[...].astype(F32))
         x_buf[...] = entry.astype(BF16)
-
-        def weights(piece):
-            at = columns(piece, channels)
-            return first_ref[:, at], second_ref[at, :]
 
         def piece_copies(piece):
             at = columns(piece, channels)
@@ -180,11 +202,10 @@
                 ),
             ]
 
-        def hidden_store(piece, hidden, pre, below):
+        def hidden_store(piece, hidden, pre, below, bell):
             at = columns(piece, channels)
             h_buf[:, at] = hidden
-            density = jnp.exp(-0.5 * pre * pre) * (1.0 / math.sqrt(2.0 * math.pi))
-            slope_buf[:, at] = (below + pre * density).astype(BF16)
+            slope_buf[:, at] = (below + pre * (bell * (1.0 / math.sqrt(2.0 * math.pi)))).astype(BF16)
             for copy in piece_copies(piece):
                 copy.start()
 
@@ -199,9 +220,8 @@
             for copy in copies[:4]:
                 copy.start()
 
-        result, mixed = forward_core(
-            side, vectors, entry, padded, spread, total, weights, n_buf, hat_store, hidden_store
-        )
+        conv_norm(vectors, entry, padded, spread, n_buf, hat_store)
+        result, mixed = mix(side, vectors, entry, total, weights, n_buf, hidden_store)
         y_ref[...] = result.astype(BF16)
         mixed_buf[...] = mixed
         copies[4].start()
@@ -212,18 +232,29 @@
                 copy.wait()
 
 
-def probe_kernel(tick, side, kept, sec_ref, marked_ref, slot_ref, image_ref, received_ref, *refs):
+def early_kernel(sec_ref, image_ref, *refs):
+    vectors = refs[:4]
+    n_ref, padded, spread = refs[4:]
+
+    @pl.when(sec_ref[0] == 0)
+    def _():
+        conv_norm(
+            vectors, image_ref[...].astype(F32), padded, spread, n_ref, lambda hat, inverse: None
+        )
+
+
+def probe_kernel(tick, side, kept, sec_ref, marked_ref, slot_ref, received_ref, early_ref, *refs):
     vectors, (own_ref, arrived_ref) = refs[:7], refs[7:9]
     refs = refs[9 + kept :]
-    y_ref, feature_ref, feature_buf, tiles_buf, padded, spread, total, n_ref, sems, end_sem = refs
+    y_ref, feature_ref, feature_buf, tiles_buf, padded, spread, total, n_buf, sems, end_sem = refs
 
     @pl.when(sec_ref[0] == tick)
     def _():
         channels = y_ref.shape[-1]
         tiles = channels // TILE
-        blocks = tiles_buf.shape[0]
         groups = vectors[4].shape[1] // channels
-        for block in range(blocks):
+
+        def start(block):
             taken = marked_ref[block] == 1
 
             @pl.when(taken)
@@ -238,28 +269,37 @@
                     own_ref.at[block], tiles_buf.at[block], sems.at[block]
                 ).start()
 
-        entry = image_ref[...] if tick == 0 else received_ref[...]
-
-        def tile(block):
+        for piece in range(groups):
+            for item in range(tiles):
+                start(piece * tiles + item)
+            for item in range(tiles):
+                start(groups * tiles + item * groups + piece)
+
+        entry = received_ref[...].astype(F32)
+
+        def wait(block):
             pltpu.make_async_copy(own_ref.at[block], tiles_buf.at[block], sems.at[block]).wait()
-            return tiles_buf[block]
 
         def weights(piece):
-            first = [tile(piece * tiles + item) for item in range(tiles)]
-            second = [tile(groups * tiles + item * groups + piece) for item in range(tiles)]
-            return jnp.concatenate(first, axis=1), jnp.concatenate(second, axis=1)
-
-        result, mixed = forward_core(
+            first = [piece * tiles + item for item in range(tiles)]
+            second = [groups * tiles + item * groups + piece for item in range(tiles)]
+            for block in first + second:
+                wait(block)
+            return (
+                jnp.concatenate([tiles_buf[block] for block in first], axis=1),
+                jnp.concatenate([tiles_buf[block] for block in second], axis=1),
+            )
+
+        if tick > 0:
+            conv_norm(vectors, entry, padded, spread, n_buf, lambda hat, inverse: None)
+        result, mixed = mix(
             side,
             vectors,
-            entry.astype(F32),
-            padded,
-            spread,
+            entry,
             total,
             weights,
-            n_ref,
-            lambda hat, inverse: None,
-            lambda piece, hidden, pre, below: None,
+            early_ref if tick == 0 else n_buf,
+            lambda piece, hidden, pre, below, bell: None,
         )
         output = result.astype(BF16)
         y_ref[...] = output
@@ -433,7 +473,7 @@
             for row in range(TAPS):
                 acc = None
                 for item in range(micro):
-                    for out in range(height):
+                    for out in range(max(0, REACH - row), min(height, height + REACH - row)):
                         term = (
                             padded[item, out + row, pl.ds(EDGE - REACH + col, width), :]
                             * dspread_ref[item, out * width : (out + 1) * width, at]
@@ -479,6 +519,7 @@
     count = wide_buf.shape[0]
     channels = wide_buf.shape[1]
     micro, rows, _ = both_ref.shape
+    batch = math.gcd(count, 4)
 
     def fetch(step, carry):
         def act(view):
@@ -493,33 +534,40 @@
         target = send_ref.at[slot_ref[step]] if sending else own_ref.at[order_ref[step]]
         return pltpu.make_async_copy(slim_buf.at[step], target, out_sems.at[step])
 
-    def body(step, carry):
-        block = order_ref[step]
-        is_first = block < first_tiles
-        place = jnp.maximum(block - first_tiles, 0)
-        group = jnp.where(is_first, groups, lax.rem(place, groups))
-        column = jnp.where(is_first, block, first_tiles + lax.div(place, groups))
-        grad = jnp.dot(
-            turned_ref[columns(group, channels), :],
-            both_ref[:, :, lanes(column)].reshape(micro * rows, TILE),
-            preferred_element_type=F32,
-        )
-        pltpu.make_async_copy(
-            first_ref.at[:, lanes(0)], wide_buf.at[step], in_sems.at[step]
-        ).wait()
-        updated = wide_buf[step] - learning_rate * grad
-        slim_buf[step] = updated.astype(BF16)
-        slim_copy(step).start()
-        if not sending:
-            wide_buf[step] = updated
-
-            def act(view):
-                pltpu.make_async_copy(wide_buf.at[step], view, wide_sems.at[step]).start()
-
-            block_views(block, first_tiles, groups, channels, new_first, new_second, act)
+    def body(turn, carry):
+        steps = [turn * batch + item for item in range(batch)]
+        for step in steps:
+            pltpu.make_async_copy(
+                first_ref.at[:, lanes(0)], wide_buf.at[step], in_sems.at[step]
+            ).wait()
+        for step in steps:
+            block = order_ref[step]
+            is_first = block < first_tiles
+            place = jnp.maximum(block - first_tiles, 0)
+            group = jnp.where(is_first, groups, lax.rem(place, groups))
+            column = jnp.where(is_first, block, first_tiles + lax.div(place, groups))
+            grad = jnp.dot(
+                turned_ref[columns(group, channels), :],
+                both_ref[:, :, lanes(column)].reshape(micro * rows, TILE),
+                preferred_element_type=F32,
+            )
+            updated = wide_buf[step] - learning_rate * grad
+            slim_buf[step] = updated.astype(BF16)
+            if not sending:
+                wide_buf[step] = updated
+        for step in steps:
+            slim_copy(step).start()
+            if not sending:
+
+                def act(view, step=step):
+                    pltpu.make_async_copy(wide_buf.at[step], view, wide_sems.at[step]).start()
+
+                block_views(
+                    order_ref[step], first_tiles, groups, channels, new_first, new_second, act
+                )
         return carry
 
-    lax.fori_loop(0, count, body, 0)
+    lax.fori_loop(0, count // batch, body, 0)
 
     def drain(step, carry):
         slim_copy(step).wait()
@@ -602,13 +650,21 @@
     in_specs = [pl.BlockSpec((1, height, width, channels), lambda i, s: (at, 0, 0, 0))]
     in_specs += [whole(item) for item in operands[1 : len(operands) - kept]]
     in_specs += [hbm_spec()] * kept
+    more_specs, more_shapes, more_scratch = [], [], []
+    if tick == 0:
+        operands[9:11] = pinned(weights)
+        in_specs[9:11] = [hbm_spec()] * 2
+        more_specs = [whole(item) for item in weights]
+        more_shapes = [shaped(item.shape, BF16) for item in weights]
+        wide = pltpu.VMEM((hid // channels, channels, channels), F32)
+        more_scratch = [wide, wide, pltpu.SemaphoreType.DMA((2, hid // channels))]
     outs = pl.pallas_call(
         functools.partial(train_kernel, tick, micro, side, kept),
         grid_spec=pltpu.PrefetchScalarGridSpec(
             num_scalar_prefetch=1,
             grid=(1,),
             in_specs=in_specs,
-            out_specs=[whole(received)] + [hbm_spec() for _ in saved_shapes],
+            out_specs=[whole(received)] + [hbm_spec() for _ in saved_shapes] + more_specs,
             scratch_shapes=[pltpu.VMEM(shape, dtype) for shape, dtype in saved_shapes]
             + [
                 pltpu.VMEM((channels // TILE, height + 2 * REACH, width + 2 * EDGE, TILE), F32),
@@ -616,16 +672,18 @@
                 pltpu.VMEM((rows, channels), F32),
                 pltpu.SemaphoreType.DMA((5,)),
                 pltpu.SemaphoreType.DMA((2, hid // channels)),
-            ],
+            ]
+            + more_scratch,
         ),
         out_shape=[shaped(received.shape, BF16)]
-        + [pltpu.HBM((micro,) + shape, dtype) for shape, dtype in saved_shapes],
+        + [pltpu.HBM((micro,) + shape, dtype) for shape, dtype in saved_shapes]
+        + more_shapes,
         input_output_aliases={1 + len(operands) - kept + i: 1 + i for i in range(kept)},
         compiler_params=params_of(),
         cost_estimate=cost(4 * rows * channels * hid, 8 << 20),
         name=f"train{tick}",
     )(sec, *operands)
-    return outs[0], outs[1:]
+    return outs[0], outs[1:8], outs[8:] if tick == 0 else weights
 
 
 def back_step(tick, micro, side, sections, sec, slopes, returned, params, saved, kept_out):
@@ -799,7 +857,7 @@
     ]
     first = w_in[0, 0]
     second = w_out[0, 0]
-    lowered = [first.astype(BF16), second.astype(BF16)]
+    lowered = [first, second]
 
     def padded(maps):
         return jnp.pad(maps, ((0, 0), (0, 0), (0, width - side), (0, 0)))
@@ -811,7 +869,7 @@
     received = images[0]
     saved = None
     for tick in range(ticks):
-        current, saved = train_step(
+        current, saved, lowered = train_step(
             tick, micro, side, sec, images, received, vectors, lowered, saved
         )
         if tick < ticks - 1:
@@ -892,10 +950,27 @@
         name="place",
     )(table["marked_order"], table["take_slots"], *pinned((arrived, new_first, new_second)))
 
+    early = pl.pallas_call(
+        early_kernel,
+        grid_spec=pltpu.PrefetchScalarGridSpec(
+            num_scalar_prefetch=1,
+            grid=(1,),
+            in_specs=[whole(trial)] + [whole(item) for item in vectors[:4]],
+            out_specs=pl.BlockSpec((rows, channels), lambda i, s: (0, 0)),
+            scratch_shapes=[
+                pltpu.VMEM((channels // TILE, height + 2 * REACH, width + 2 * EDGE, TILE), F32),
+                pltpu.VMEM((rows, channels), F32),
+            ],
+        ),
+        out_shape=shaped((rows, channels), BF16),
+        compiler_params=params_of(),
+        cost_estimate=cost(1 << 26, 1 << 20),
+        name="early",
+    )(sec, trial, *vectors[:4])
     received = trial
     features = None
     for tick in range(sections):
-        operands = [trial, received, *vectors, *pinned((own, arrived))]
+        operands = [received, early, *vectors, *pinned((own, arrived))]
         in_specs = [whole(item) for item in operands[:-2]] + [hbm_spec(), hbm_spec()]
         kept = 0 if features is None else 1
         if kept:

time: 236 us -> 218 us (0.924)
  waiting for transfers between devices: 132 us -> 122 us
  Pallas kernels: 76.1 us -> 71.8 us
  other arithmetic: 3.64 us -> 0.71 us
    ppermute x4, waiting for transfers between devices: 33.6 us -> 27.2 us  [local(): received = lax.ppermute(current, 'section', pairs)]
    ppermute x3, waiting for transfers between devices: 50.8 us -> 44.9 us  [local(): received = lax.ppermute(result, 'section', [(tick, tick + 1)])]
    pallas_call x2, Pallas kernels: 20.2 us -> 16.9 us  [update_step(): pl.pallas_call(functools.partial(update_kernel, first_tiles, groups, send...]
    convert_element_type x2 -> x0, other arithmetic: 2.93 us -> none  [local(): lowered = [first.astype(BF16), second.astype(BF16)]]
where the time goes in v4:
time: 218 us; the launch traced here: 217 us
  waiting for transfers between devices  122 us (56%)
  Pallas kernels  71.8 us (33%)
  starting transfers between devices  18.6 us (9%)
  local copies, waits for them, and re-layouts  2.99 us (1%)
    all_to_all x1, waiting for transfers between devices, local(): lax.all_to_all(outgoing, 'member', split_axis=0, concat_axis=0, tiled=True)  47.6 us
    ppermute x3, waiting for transfers between devices, local(): received = lax.ppermute(result, 'section', [(tick, tick + 1)])  44.9 us
    ppermute x4, waiting for transfers between devices, local(): received = lax.ppermute(current, 'section', pairs)  27.2 us
    pallas_call x2, Pallas kernels, update_step(): pl.pallas_call(functools.partial(update_kernel, first_tiles, groups, send...  16.9 us
    pallas_call x5, Pallas kernels, train_step(): pl.pallas_call(functools.partial(train_kernel, tick, micro, side, kept),...  16.6 us
    pallas_call x5, Pallas kernels, back_step(): pl.pallas_call(functools.partial(back_kernel, tick, micro, side, sections...  16.3 us
    pallas_call x4, Pallas kernels, local(): pl.pallas_call(functools.partial(probe_kernel, tick, side, kept), grid_sp...  9.75 us
    pallas_call x1, Pallas kernels, small_step(): pl.pallas_call(functools.partial(small_kernel, micro), grid=(1,), in_spec...  8.52 us
  transfers between devices with their start and end apart: 12, of which 6 were waited for; matrix products, arithmetic and copies ran while one was open for 0% of the time, Pallas kernels for 10%

profile of v4, /device:TPU:5, one launch (start us, length us, event | category | flops | bytes accessed | tf_op | source)
XLA Modules:
  0.0 217.1 jit_solution(15392104297633270841)
XLA Ops:
  0.7 1.1 copy.76
  2.0 3.7 %train0.1 = (bf16[14,16,512]{2,1,0:T(8,128)(2,1)S(1)}, bf16[2,14,16,512]{3,2,1,0:T(8,128)(2,1)}, f32[2,224,512]{2,1,0:T(8,128)}, f32[2,224,128]{2,1,0:T(8,128)},...) custom-call(s32[1]{0:T(128)} %bitcast.2.sec_ref, ...), custom_call_target="tpu_custom_call" | custom-call | flops 939524096 | bytes 8388608 | tf_op jit(solution)/shard_map/train0/pallas_call | solution.py:661
  7.4 1.3 collective-permute-start.2
  8.7 21.9 %collective-permute-done.2.received_ref = bf16[14,16,512]{2,1,0:T(8,128)(2,1)S(1)} collective-permute-done((bf16[14,16,512]{2,1,0:T(8,128)(2,1)S(1)}, bf16[14,16,512]{2,1,0:T(8,128)(2,1)S(1)}, u32[]{:S(2)}, u32[]{:S(2)}) %collective-permute-start.2) | collective-permute-done | bytes 229408 | tf_op jit(solution)/shard_map/ppermute | solution.py:877
  30.6 5.9 %train3.1 = (bf16[14,16,512]{2,1,0:T(8,128)(2,1)S(1)}, bf16[2,14,16,512]{3,2,1,0:T(8,128)(2,1)}, f32[2,224,512]{2,1,0:T(8,128)}, f32[2,224,128]{2,1,0:T(8,128)},...) custom-call(s32[1]{0:T(128)} %bitcast.2.sec_ref, ...), custom_call_target="tpu_custom_call", output_to_operand_aliasing={{1}: (12, {}), {2}: (13, {}), {3}: (14, {}), {4}: (15, {}),... | custom-call | flops 939524096 | bytes 8388608 | tf_op jit(solution)/shard_map/train3/pallas_call | solution.py:661
  36.6 1.3 collective-permute-start.3
  38.0 5.2 %collective-permute-done.3.received_ref = bf16[14,16,512]{2,1,0:T(8,128)(2,1)S(1)} collective-permute-done((bf16[14,16,512]{2,1,0:T(8,128)(2,1)S(1)}, bf16[14,16,512]{2,1,0:T(8,128)(2,1)S(1)}, u32[]{:S(2)}, u32[]{:S(2)}) %collective-permute-start.3) | collective-permute-done | bytes 229408 | tf_op jit(solution)/shard_map/ppermute | solution.py:877
  43.3 6.6 %train4.1 = (bf16[14,16,512]{2,1,0:T(8,128)(2,1)}, bf16[2,14,16,512]{3,2,1,0:T(8,128)(2,1)}, f32[2,224,512]{2,1,0:T(8,128)}, f32[2,224,128]{2,1,0:T(8,128)}, bf1...) custom-call(s32[1]{0:T(128)} %bitcast.2.sec_ref, ...), custom_call_target="tpu_custom_call", output_to_operand_aliasing={{1}: (12, {}), {2}: (13, {}), {3}: (14, {}), {4}: (15, {}),... | custom-call | flops 939524096 | bytes 8388608 | tf_op jit(solution)/shard_map/train4/pallas_call | solution.py:661
  49.9 5.5 %back0.1 = (bf16[14,16,512]{2,1,0:T(8,128)(2,1)S(1)}, bf16[2,224,512]{2,1,0:T(8,128)(2,1)}, bf16[2,224,512]{2,1,0:T(8,128)(2,1)}, f32[2,224,512]{2,1,0:T(8,128)}...) custom-call(s32[1]{0:T(128)} %bitcast.2.sec_ref, bf16[2,14,16,512]{3,2,1,0:T(8,128)(2,1)S(1)} %pad.11.slope_in_ref, ...), custom_call_target="tpu_custom_call" | custom-call | flops 939524096 | bytes 8388608 | tf_op jit(solution)/shard_map/back0/pallas_call | solution.py:709
  55.4 1.3 collective-permute-start.4
  56.7 1.1 collective-permute-done.4.returned_ref
  57.8 1.6 copy-done.1
  59.4 5.5 %back1.1 = (bf16[14,16,512]{2,1,0:T(8,128)(2,1)S(1)}, bf16[2,224,512]{2,1,0:T(8,128)(2,1)}, bf16[2,224,512]{2,1,0:T(8,128)(2,1)}, f32[2,224,512]{2,1,0:T(8,128)}...) custom-call(s32[1]{0:T(128)} %bitcast.2.sec_ref, ...), custom_call_target="tpu_custom_call", output_to_operand_aliasing={{1}: (13, {}), {2}: (14, {}), {3}: (15, {}), {4}: (16, {}),... | custom-call | flops 939524096 | bytes 8388608 | tf_op jit(solution)/shard_map/back1/pallas_call | solution.py:709
  64.9 2.3 %collective-permute-start.5 = (bf16[14,16,512]{2,1,0:T(8,128)(2,1)S(1)}, bf16[14,16,512]{2,1,0:T(8,128)(2,1)S(1)}, u32[]{:S(2)}, u32[]{:S(2)}) collective-permute-start(bf16[14,16,512]{2,1,0:T(8,128)(2,1)S(1)} %get-tuple-element.137), channel_id=1, source_target_pairs={{2,1},{3,2},{6,5},{7,6},{10,9},{11,10},{14,13},{15,14},{18,17},{19... | collective-permute-start | bytes 688136 | tf_op jit(solution)/shard_map/ppermute | solution.py:899
  68.3 4.3 %back2.1 = (bf16[14,16,512]{2,1,0:T(8,128)(2,1)S(1)}, bf16[2,224,512]{2,1,0:T(8,128)(2,1)}, bf16[2,224,512]{2,1,0:T(8,128)(2,1)}, f32[2,224,512]{2,1,0:T(8,128)}...) custom-call(s32[1]{0:T(128)} %bitcast.2.sec_ref, ...), custom_call_target="tpu_custom_call", output_to_operand_aliasing={{1}: (13, {}), {2}: (14, {}), {3}: (15, {}), {4}: (16, {}),... | custom-call | flops 939524096 | bytes 8388608 | tf_op jit(solution)/shard_map/back2/pallas_call | solution.py:709
  75.4 8.2 %send.1 = bf16[24,512,128]{2,1,0:T(8,128)(2,1)} custom-call(s32[16]{0:T(128)S(1)} %get-tuple-element.185.order_ref, s32[16]{0:T(128)S(1)} %broadcast_clamp_fusion.1.slot_ref, bf16[2560,448]{1,0:T(8,128)(2,1)} %get-tuple-element.155.turned_ref, bf16[2,224,2560]{2,1,0:T(8,128)(2,1)} %get-tuple-element.156.both_ref.refs_13_, f32[512,2048]{1,0:T(8,128)} %bitcast.100, ...), custom_call_target="tpu_custom_call" | custom-call | flops 1073741824 | bytes 8388608 | tf_op jit(solution)/shard_map/send/pallas_call | solution.py:804
  83.6 7.1 %all-to-all-start = ((bf16[24,512,128]{2,1,0:T(8,128)(2,1)}), bf16[24,512,128]{2,1,0:T(8,128)(2,1)}, u32[]{:S(2)}, u32[]{:S(2)}) async-start(bf16[24,512,128]{2,1,0:T(8,128)(2,1)} %send.1), calls=%async_computation | async-start | bytes 6291456 | tf_op jit(solution)/shard_map/all_to_all | solution.py:915
  91.0 8.5 %small.1 = (f32[49,1,512]{2,1,0:T(1,128)S(1)}, f32[1,512]{1,0:T(1,128)S(1)}, f32[1,512]{1,0:T(1,128)S(1)}, f32[1,512]{1,0:T(1,128)S(1)}, f32[1,2048]{1,0:T(1,128...) custom-call(f32[49,1,512]{2,1,0:T(1,128)S(1)} %bitcast.48, f32[1,512]{1,0:T(1,128)S(1)} %bitcast.82, ...), custom_call_target="tpu_custom_call" | custom-call | flops 268435456 | bytes 8388608 | tf_op jit(solution)/shard_map/small/pallas_call | solution.py:746
  99.6 8.7 %keep.1 = (bf16[32,512,128]{2,1,0:T(8,128)(2,1)}, f32[512,2048]{1,0:T(8,128)}, f32[2048,512]{1,0:T(8,128)}) custom-call(s32[16]{0:T(128)S(1)} %select_reduce_fusion.order_ref.slot_ref, s32[16]{0:T(128)S(1)} %select_reduce_fusion.order_ref.slot_ref, bf16[2560,448]{1,0:T(8,128)(2,1)} %get-tuple-element.155.turned_ref, ...), custom_call_target="tpu_custom_call" | custom-call | flops 1073741824 | bytes 8388608 | tf_op jit(solution)/shard_map/keep/pallas_call | solution.py:804
  108.2 47.6 %all-to-all-done.arrived_ref.refs_8_ = bf16[24,512,128]{2,1,0:T(8,128)(2,1)} async-done(((bf16[24,512,128]{2,1,0:T(8,128)(2,1)}), bf16[24,512,128]{2,1,0:T(8,128)(2,1)}, u32[]{:S(2)}, u32[]{:S(2)}) %all-to-all-start) | async-done | bytes 3145760 | tf_op jit(solution)/shard_map/all_to_all | solution.py:915
  159.8 1.3 collective-permute-start.10
  161.1 3.7 %place.1 = (f32[512,2048]{1,0:T(8,128)}, f32[2048,512]{1,0:T(8,128)}) custom-call(s32[16]{0:T(128)S(1)} %get-tuple-element.185.order_ref, s32[16]{0:T(128)S(1)} %broadcast_clamp_fusion.2.slot_ref, bf16[24,512,128]{2,1,0:T(8,128)(2,1)} %all-to-all-done.arrived_ref.refs_8_, ...), custom_call_target="tpu_custom_call", output_to_operand_aliasing={{0}: (3, {}), {1}: (4, {})} | custom-call | bytes 8388608 | tf_op jit(solution)/shard_map/place/pallas_call | solution.py:932
  164.9 44.9 %collective-permute-done.10.received_ref = bf16[14,16,512]{2,1,0:T(8,128)(2,1)S(1)} collective-permute-done((bf16[14,16,512]{2,1,0:T(8,128)(2,1)S(1)}, bf16[14,16,512]{2,1,0:T(8,128)(2,1)S(1)}, u32[]{:S(2)}, u32[]{:S(2)}) %collective-permute-start.10) | collective-permute-done | bytes 229408 | tf_op jit(solution)/shard_map/ppermute | solution.py:1006
  209.8 7.2 %probe3.1 = (bf16[14,16,512]{2,1,0:T(8,128)(2,1)}, bf16[14,14,512]{2,1,0:T(8,128)(2,1)}) custom-call(s32[1]{0:T(128)} %bitcast.2.sec_ref, s32[32]{0:T(128)S(1)} %bitcast.98, s32[32]{0:T(128)S(1)} %get-tuple-element.189.slot_ref, bf16[14,16,512]{2,1,0:T(8,128)(2,1)S(1)} %collective-permute-done.10.received_ref, ...), custom_call_target="tpu_custom_call", output_to_operand_aliasing={{1}: (14, {})} | custom-call | flops 939524096 | bytes 8388608 | tf_op jit(solution)/shard_map/probe3/pallas_call | solution.py:979
  (62 shorter events, 9.8 us)
Async XLA Ops:
  0.6 1.3 copy-start.2
  0.6 1.3 copy-start.4
  0.7 1.3 copy-start.5
  0.7 1.3 copy-start.6
  0.7 1.3 copy-start.7
  0.7 1.3 copy-start.3
  5.7 44.2 %copy-start = (bf16[2048,512]{1,0:T(8,128)(2,1)}, bf16[2048,512]{1,0:T(8,128)(2,1)S(1)}, u32[]{:S(2)}) copy-start(bf16[2048,512]{1,0:T(8,128)(2,1)S(1)} %get-tuple-element.93.refs_8_.refs_4_) | copy-start | bytes 6291460
  5.7 0.7 collective-permute-start
  6.6 0.7 collective-permute-start.1
  7.4 23.2 %collective-permute-start.2 = (bf16[14,16,512]{2,1,0:T(8,128)(2,1)S(1)}, bf16[14,16,512]{2,1,0:T(8,128)(2,1)S(1)}, u32[]{:S(2)}, u32[]{:S(2)}) collective-permute-start(bf16[14,16,512]{2,1,0:T(8,128)(2,1)S(1)} %get-tuple-element.110), channel_id=1, source_target_pairs={{1,2},{2,3},{5,6},{6,7},{9,10},{10,11},{13,14},{14,15},{17,18},{18... | collective-permute-start | bytes 688136 | tf_op jit(solution)/shard_map/ppermute | solution.py:877
  30.6 7.3 %copy-start.10 = (bf16[1,2,1,14,14,512]{5,1,4,3,2,0:T(2,128)(2,1)S(1)}, bf16[1,2,1,14,14,512]{5,1,4,3,2,0:T(2,128)(2,1)}, u32[]{:S(2)}) copy-start(bf16[1,2,1,14,14,512]{5,1,4,3,2,0:T(2,128)(2,1)} %param.15) | copy-start | bytes 1204228
  36.6 6.7 %collective-permute-start.3 = (bf16[14,16,512]{2,1,0:T(8,128)(2,1)S(1)}, bf16[14,16,512]{2,1,0:T(8,128)(2,1)S(1)}, u32[]{:S(2)}, u32[]{:S(2)}) collective-permute-start(bf16[14,16,512]{2,1,0:T(8,128)(2,1)S(1)} %get-tuple-element.118), channel_id=1, source_target_pairs={{2,3},{6,7},{10,11},{14,15},{18,19},{22,23},{26,27},{30,31}} | collective-permute-start | bytes 688136 | tf_op jit(solution)/shard_map/ppermute | solution.py:877
  55.4 2.4 %collective-permute-start.4 = (bf16[14,16,512]{2,1,0:T(8,128)(2,1)S(1)}, bf16[14,16,512]{2,1,0:T(8,128)(2,1)S(1)}, u32[]{:S(2)}, u32[]{:S(2)}) collective-permute-start(bf16[14,16,512]{2,1,0:T(8,128)(2,1)S(1)} %get-tuple-element.131), channel_id=1, source_target_pairs={{3,2},{7,6},{11,10},{15,14},{19,18},{23,22},{27,26},{31,30}} | collective-permute-start | bytes 688136 | tf_op jit(solution)/shard_map/ppermute | solution.py:899
  57.8 1.6 copy-start.1
  59.4 7.9 %copy-start.12 = (s32[1,32,8]{1,2,0:T(8,128)S(1)}, s32[1,32,8]{1,2,0:T(8,128)}, u32[]{:S(2)}) copy-start(s32[1,32,8]{1,2,0:T(8,128)} %param.27) | copy-start | bytes 3076
  59.4 7.9 %copy-start.9 = (s32[1,32]{1,0:T(1,128)S(1)}, s32[1,32]{1,0:T(1,128)}, u32[]{:S(2)}) copy-start(s32[1,32]{1,0:T(1,128)} %param.26) | copy-start | bytes 388
  64.9 3.4 %collective-permute-start.5 = (bf16[14,16,512]{2,1,0:T(8,128)(2,1)S(1)}, bf16[14,16,512]{2,1,0:T(8,128)(2,1)S(1)}, u32[]{:S(2)}, u32[]{:S(2)}) collective-permute-start(bf16[14,16,512]{2,1,0:T(8,128)(2,1)S(1)} %get-tuple-element.137), channel_id=1, source_target_pairs={{2,1},{3,2},{6,5},{7,6},{10,9},{11,10},{14,13},{15,14},{18,17},{19... | collective-permute-start | bytes 688136 | tf_op jit(solution)/shard_map/ppermute | solution.py:899
  72.6 0.9 collective-permute-start.6
  73.7 0.8 collective-permute-start.7
  83.6 7.4 %copy-start.11 = (bf16[1,1,14,14,512]{4,3,2,1,0:T(8,128)(2,1)S(1)}, bf16[1,1,14,14,512]{4,3,2,1,0:T(8,128)(2,1)}, u32[]{:S(2)}) copy-start(bf16[1,1,14,14,512]{4,3,2,1,0:T(8,128)(2,1)} %param.16) | copy-start | bytes 602116
  83.6 72.2 %all-to-all-start = ((bf16[24,512,128]{2,1,0:T(8,128)(2,1)}), bf16[24,512,128]{2,1,0:T(8,128)(2,1)}, u32[]{:S(2)}, u32[]{:S(2)}) async-start(bf16[24,512,128]{2,1,0:T(8,128)(2,1)} %send.1), calls=%async_computation | async-start | bytes 6291456 | tf_op jit(solution)/shard_map/all_to_all | solution.py:915
  156.7 0.7 collective-permute-start.8
  158.2 0.7 collective-permute-start.9
  159.8 50.0 %collective-permute-start.10 = (bf16[14,16,512]{2,1,0:T(8,128)(2,1)S(1)}, bf16[14,16,512]{2,1,0:T(8,128)(2,1)S(1)}, u32[]{:S(2)}, u32[]{:S(2)}) collective-permute-start(bf16[14,16,512]{2,1,0:T(8,128)(2,1)S(1)} %get-tuple-element.178), channel_id=1, source_target_pairs={{2,3},{6,7},{10,11},{14,15},{18,19},{22,23},{26,27},{30,31}} | collective-permute-start | bytes 688136 | tf_op jit(solution)/shard_map/ppermute | solution.py:1006
  (1 other events, 1.3 us)

commit v5 on v4

--- a/solution.py
+++ b/solution.py
@@ -129,21 +129,17 @@
     return result, mixed
 
 
-def is_active(sec_ref, tick, count):
-    which = tick - sec_ref[0]
-    return (which >= 0) & (which < count)
-
-
 def columns(piece, channels):
     return pl.ds(pl.multiple_of(piece * channels, channels), channels)
 
 
-def train_kernel(tick, micro, side, kept, sec_ref, image_ref, received_ref, *refs):
+def train_kernel(owner, slot, side, kept, sec_ref, entry_ref, *refs):
     vectors, (first_ref, second_ref) = refs[:7], refs[7:9]
     refs = refs[9 + kept :]
     y_ref, outs = refs[0], refs[1:8]
     refs = refs[8:]
-    if tick == 0:
+    leading = kept == 0
+    if leading:
         low_first, low_second = refs[:2]
         refs = refs[2:]
         wide_first, wide_second, wide_sems = refs[12:]
@@ -153,7 +149,7 @@
     h_out, slope_out = outs[5:]
     channels = x_buf.shape[-1]
     pieces = h_buf.shape[-1] // channels
-    active = is_active(sec_ref, tick, micro)
+    active = sec_ref[0] == owner
 
     def wide_copies(piece):
         at = columns(piece, channels)
@@ -164,7 +160,7 @@
 
     def weights(piece):
         at = columns(piece, channels)
-        if tick > 0:
+        if not leading:
             return first_ref[:, at], second_ref[at, :]
         for copy in wide_copies(piece):
             copy.wait()
@@ -174,7 +170,7 @@
         low_second[at, :] = second
         return first, second
 
-    if tick == 0:
+    if leading:
         for piece in range(pieces):
             for copy in wide_copies(piece):
                 copy.start()
@@ -189,9 +185,8 @@
 
     @pl.when(active)
     def _():
-        slot = tick - sec_ref[0]
-        entry = jnp.where(sec_ref[0] == 0, image_ref[0].astype(F32), received_ref[...].astype(F32))
-        x_buf[...] = entry.astype(BF16)
+        entry = entry_ref[...].astype(F32)
+        x_buf[...] = entry_ref[...]
 
         def piece_copies(piece):
             at = columns(piece, channels)
@@ -309,7 +304,7 @@
         done.wait()
 
 
-def back_kernel(tick, micro, side, sections, kept, turns, sec_ref, slope_in_ref, returned_ref, *refs):
+def back_kernel(owner, which, side, turning, kept, sec_ref, returned_ref, *refs):
     kernel_ref, gain_ref, scale_ref, first_ref, second_ref = refs[:5]
     hat_ref, inverse_ref, slope_ref, n_ref, h_ref = refs[5:10]
     refs = refs[10 + kept :]
@@ -318,12 +313,11 @@
     hat_buf, inverse_buf, slope_buf, n_buf, h_buf = refs[11:16]
     padded, total, conv_out, sems, piece_sems, in_sems = refs[16:]
     both_out = outs[3]
-    which = tick - (sections - 1 - sec_ref[0])
     channels = dx_ref.shape[-1]
     hid = h_buf.shape[-1]
     pieces = hid // channels
 
-    @pl.when((which >= 0) & (which < micro))
+    @pl.when(sec_ref[0] == owner)
     def _():
         height, width, _ = dx_ref.shape
         rows = height * width
@@ -339,9 +333,7 @@
         ins.append(pltpu.make_async_copy(inverse_ref.at[which], inverse_buf, in_sems.at[pieces + 1]))
         for copy in ins:
             copy.start()
-        dy = jnp.where(
-            sec_ref[0] == sections - 1, slope_in_ref[0].astype(F32), returned_ref[...].astype(F32)
-        )
+        dy = returned_ref[...].astype(F32)
         flat = dy.reshape(rows, channels)
         dy_buf[...] = flat.astype(BF16)
         mix_at = columns(pieces, channels)
@@ -391,7 +383,7 @@
         dspread = inverse_buf[:, 0:1] * (dhat - mean - hat * along)
         dspread_buf[...] = dspread
         copies[2].start()
-        if tick < micro + sections - 2:
+        if owner > 0:
             fill_padded(padded, dspread.reshape(height, width, channels))
 
             def conv_body(chunk, carry):
@@ -410,12 +402,10 @@
         for piece in range(pieces + 1):
             both_copy(piece).wait()
 
-    if turns:
-        wanted = which == -1
-        if tick == micro:
-            wanted = wanted | (sec_ref[0] == sections - 1)
-
-        @pl.when(wanted)
+    if turning is not None:
+        low, high = turning
+
+        @pl.when((sec_ref[0] >= low) & (sec_ref[0] < high))
         def _():
             get_n = pltpu.make_async_copy(n_ref, n_buf, sems.at[0])
             get_h = pltpu.make_async_copy(h_ref, h_buf, sems.at[1])
@@ -631,7 +621,7 @@
     return pl.BlockSpec(memory_space=pltpu.HBM)
 
 
-def train_step(tick, micro, side, sec, images, received, vectors, weights, saved):
+def train_step(owner, slot, micro, side, sec, received, vectors, weights, saved):
     height, width, channels = received.shape
     rows = height * width
     hid = vectors[4].shape[1]
@@ -645,21 +635,19 @@
         ((rows, hid), BF16),
     ]
     kept = 0 if saved is None else len(saved)
-    at = min(tick, micro - 1)
-    operands = [images, received, *vectors, *weights] + ([] if saved is None else pinned(saved))
-    in_specs = [pl.BlockSpec((1, height, width, channels), lambda i, s: (at, 0, 0, 0))]
-    in_specs += [whole(item) for item in operands[1 : len(operands) - kept]]
+    operands = [received, *vectors, *weights] + ([] if saved is None else pinned(saved))
+    in_specs = [whole(item) for item in operands[: len(operands) - kept]]
     in_specs += [hbm_spec()] * kept
     more_specs, more_shapes, more_scratch = [], [], []
-    if tick == 0:
-        operands[9:11] = pinned(weights)
-        in_specs[9:11] = [hbm_spec()] * 2
+    if saved is None:
+        operands[8:10] = pinned(weights)
+        in_specs[8:10] = [hbm_spec()] * 2
         more_specs = [whole(item) for item in weights]
         more_shapes = [shaped(item.shape, BF16) for item in weights]
         wide = pltpu.VMEM((hid // channels, channels, channels), F32)
         more_scratch = [wide, wide, pltpu.SemaphoreType.DMA((2, hid // channels))]
     outs = pl.pallas_call(
-        functools.partial(train_kernel, tick, micro, side, kept),
+        functools.partial(train_kernel, owner, slot, side, kept),
         grid_spec=pltpu.PrefetchScalarGridSpec(
             num_scalar_prefetch=1,
             grid=(1,),
@@ -681,12 +669,12 @@
         input_output_aliases={1 + len(operands) - kept + i: 1 + i for i in range(kept)},
         compiler_params=params_of(),
         cost_estimate=cost(4 * rows * channels * hid, 8 << 20),
-        name=f"train{tick}",
+        name=f"train_{owner}_{slot}",
     )(sec, *operands)
-    return outs[0], outs[1:8], outs[8:] if tick == 0 else weights
-
-
-def back_step(tick, micro, side, sections, sec, slopes, returned, params, saved, kept_out):
+    return outs[0], outs[1:8], outs[8:] if saved is None else weights
+
+
+def back_step(owner, which, micro, side, turning, sec, returned, params, saved, kept_out):
     height, width, channels = returned.shape
     rows = height * width
     hid = saved[2].shape[-1]
@@ -698,16 +686,13 @@
     ]
     turned = ((hid + channels, micro * rows), BF16)
     kept = 0 if kept_out is None else len(kept_out)
-    operands = [slopes, returned, *params, *pinned(saved)]
-    at = min(tick, micro - 1)
-    in_specs = [pl.BlockSpec((1, height, width, channels), lambda i, s: (at, 0, 0, 0))]
-    in_specs += [whole(item) for item in operands[1:7]]
+    operands = [returned, *params, *pinned(saved)]
+    in_specs = [whole(item) for item in operands[:6]]
     in_specs += [hbm_spec()] * (len(saved) + kept)
     base = len(operands)
     operands += [] if kept_out is None else pinned(kept_out)
-    turns = tick <= max(sections - 2, micro)
     outs = pl.pallas_call(
-        functools.partial(back_kernel, tick, micro, side, sections, kept, turns),
+        functools.partial(back_kernel, owner, which, side, turning, kept),
         grid_spec=pltpu.PrefetchScalarGridSpec(
             num_scalar_prefetch=1,
             grid=(1,),
@@ -735,7 +720,7 @@
         input_output_aliases={1 + base + i: 1 + i for i in range(kept)},
         compiler_params=params_of(),
         cost_estimate=cost(4 * rows * channels * hid, 8 << 20),
-        name=f"back{tick}",
+        name=f"back_{owner}_{which}",
     )(sec, *operands)
     return outs[0], outs[1:]
 
@@ -865,38 +850,40 @@
     images = padded(inputs[0, :, 0])
     slopes = padded(cotangent[0, :, 0])
     trial = padded(probe[0])[0]
-    ticks = micro + sections - 1
-    received = images[0]
+    entries = [images[item] for item in range(micro)]
     saved = None
-    for tick in range(ticks):
-        current, saved, lowered = train_step(
-            tick, micro, side, sec, images, received, vectors, lowered, saved
-        )
-        if tick < ticks - 1:
-            pairs = [(s, s + 1) for s in range(sections - 1) if 0 <= tick - s < micro]
-            received = lax.ppermute(current, "section", pairs)
+    for owner in range(sections):
+        leaving = []
+        for item in range(micro):
+            current, saved, lowered = train_step(
+                owner, item, micro, side, sec, entries[item], vectors, lowered, saved
+            )
+            if owner < sections - 1:
+                leaving.append(lax.ppermute(current, "section", [(owner, owner + 1)]))
+        entries = leaving
     xs, hats, inverses, ns, mixes, hs, gelu_slopes = saved
     kernel, gain, scale = vectors[0], vectors[2], vectors[6]
-    returned = slopes[0]
+    entries = [slopes[item] for item in range(micro)]
     grads = None
-    for tick in range(ticks):
-        current, grads = back_step(
-            tick,
-            micro,
-            side,
-            sections,
-            sec,
-            slopes,
-            returned,
-            (kernel, gain, scale, *lowered),
-            (hats, inverses, gelu_slopes, ns, hs),
-            grads,
-        )
-        if tick < ticks - 1:
-            pairs = [
-                (s, s - 1) for s in range(1, sections) if 0 <= tick - (sections - 1 - s) < micro
-            ]
-            returned = lax.ppermute(current, "section", pairs)
+    turnings = {(sections - 1, 0): (0, sections - 1), (max(sections - 2, 0), micro - 1): (sections - 1, sections)}
+    for owner in reversed(range(sections)):
+        leaving = []
+        for item in range(micro):
+            current, grads = back_step(
+                owner,
+                item,
+                micro,
+                side,
+                turnings.get((owner, item)),
+                sec,
+                entries[item],
+                (kernel, gain, scale, *lowered),
+                (hats, inverses, gelu_slopes, ns, hs),
+                grads,
+            )
+            if owner > 0:
+                leaving.append(lax.ppermute(current, "section", [(owner, owner - 1)]))
+        entries = leaving
     dys, dns, dspreads, boths, turned = grads
 
     table = tables(shuffle_mask[0], source_member[0])

time: 218 us -> 212 us (0.972)
  waiting for transfers between devices: 122 us -> 105 us
  local copies, waits for them, and re-layouts: 2.99 us -> 8.29 us
  Pallas kernels: 71.8 us -> 75.3 us
    ppermute x8 -> x12, waiting for transfers between devices: 29.2 us -> 18.4 us  [the longest x6 18.3 us: local(): leaving.append(lax.ppermute(current, 'section', [(owner, owner + 1)]))]
    ppermute x3, waiting for transfers between devices: 44.9 us -> 38.4 us  [local(): received = lax.ppermute(result, 'section', [(tick, tick + 1)])]
    unnamed x28 -> x42, local copies, waits for them, and re-layouts: 2.83 us -> 8.17 us
    pallas_call x10 -> x16, Pallas kernels: 32.9 us -> 36.2 us  [the longest x8 18.1 us: train_step(): pl.pallas_call(functools.partial(train_kernel, owner, slot, side, kept),...]
    ppermute x8 -> x12, starting transfers between devices: 8.89 us -> 10.6 us  [the longest x6 5.31 us: local(): leaving.append(lax.ppermute(current, 'section', [(owner, owner - 1)]))]
  transfers between devices with their start and end apart: 12 -> 16, of which waited for: 6 -> 4; matrix products, arithmetic and copies ran while one was open for 0% -> 0% of each run, Pallas kernels for 10% -> 19%
where the time goes in v5:
time: 212 us; the launch traced here: 211 us
  waiting for transfers between devices  105 us (50%)
  Pallas kernels  75.3 us (36%)
  starting transfers between devices  20.4 us (10%)
  local copies, waits for them, and re-layouts  8.29 us (4%)
    all_to_all x1, waiting for transfers between devices, local(): lax.all_to_all(outgoing, 'member', split_axis=0, concat_axis=0, tiled=True)  48.6 us
    ppermute x3, waiting for transfers between devices, local(): received = lax.ppermute(result, 'section', [(tick, tick + 1)])  38.4 us
    ppermute x6, waiting for transfers between devices, local(): leaving.append(lax.ppermute(current, 'section', [(owner, owner + 1)]))  18.3 us
    pallas_call x8, Pallas kernels, train_step(): pl.pallas_call(functools.partial(train_kernel, owner, slot, side, kept),...  18.1 us
    pallas_call x8, Pallas kernels, back_step(): pl.pallas_call(functools.partial(back_kernel, owner, which, side, turning...  18.1 us
    pallas_call x2, Pallas kernels, update_step(): pl.pallas_call(functools.partial(update_kernel, first_tiles, groups, send...  16.8 us
    pallas_call x4, Pallas kernels, local(): pl.pallas_call(functools.partial(probe_kernel, tick, side, kept), grid_sp...  9.97 us
    pallas_call x1, Pallas kernels, small_step(): pl.pallas_call(functools.partial(small_kernel, micro), grid=(1,), in_spec...  8.53 us
  transfers between devices with their start and end apart: 16, of which 4 were waited for; matrix products, arithmetic and copies ran while one was open for 0% of the time, Pallas kernels for 19%

profile of v5, /device:TPU:5, one launch (start us, length us, event | category | flops | bytes accessed | tf_op | source)
XLA Modules:
  0.0 211.5 jit_solution(457480435316352285)
XLA Ops:
  0.6 1.1 copy.112
  1.8 0.9 copy-done.2
  6.8 3.7 %train_0_0.1 = (bf16[14,16,512]{2,1,0:T(8,128)(2,1)S(1)}, bf16[2,14,16,512]{3,2,1,0:T(8,128)(2,1)}, f32[2,224,512]{2,1,0:T(8,128)}, f32[2,224,128]{2,1,0:T(8,128...) custom-call(s32[1]{0:T(128)} %bitcast.2.sec_ref, ...), custom_call_target="tpu_custom_call" | custom-call | flops 939524096 | bytes 8388608 | tf_op jit(solution)/shard_map/train_0_0/pallas_call | solution.py:649
  12.6 1.6 copy-done.1
  16.0 1.3 collective-permute-start.5
  17.4 1.3 collective-permute-start.4
  18.9 17.6 %collective-permute-done.5.entry_ref = bf16[14,16,512]{2,1,0:T(8,128)(2,1)S(1)} collective-permute-done((bf16[14,16,512]{2,1,0:T(8,128)(2,1)S(1)}, bf16[14,16,512]{2,1,0:T(8,128)(2,1)S(1)}, u32[]{:S(2)}, u32[]{:S(2)}) %collective-permute-start.5) | collective-permute-done | bytes 229408 | tf_op jit(solution)/shard_map/ppermute | solution.py:862
  36.5 6.9 %train_3_0.1 = (bf16[14,16,512]{2,1,0:T(8,128)(2,1)}, bf16[2,14,16,512]{3,2,1,0:T(8,128)(2,1)}, f32[2,224,512]{2,1,0:T(8,128)}, f32[2,224,128]{2,1,0:T(8,128)}, ...) custom-call(s32[1]{0:T(128)} %bitcast.2.sec_ref, ...), custom_call_target="tpu_custom_call", output_to_operand_aliasing={{1}: (11, {}), {2}: (12, {}), {3}: (13, {}), {4}: (14, {}),... | custom-call | flops 939524096 | bytes 8388608 | tf_op jit(solution)/shard_map/train_3_0/pallas_call | solution.py:649
  44.1 6.9 %train_3_1.1 = (bf16[14,16,512]{2,1,0:T(8,128)(2,1)}, bf16[2,14,16,512]{3,2,1,0:T(8,128)(2,1)}, f32[2,224,512]{2,1,0:T(8,128)}, f32[2,224,128]{2,1,0:T(8,128)}, ...) custom-call(s32[1]{0:T(128)} %bitcast.2.sec_ref, ...), custom_call_target="tpu_custom_call", output_to_operand_aliasing={{1}: (11, {}), {2}: (12, {}), {3}: (13, {}), {4}: (14, {}),... | custom-call | flops 939524096 | bytes 8388608 | tf_op jit(solution)/shard_map/train_3_1/pallas_call | solution.py:649
  51.0 5.7 %back_3_0.1 = (bf16[14,16,512]{2,1,0:T(8,128)(2,1)S(1)}, bf16[2,224,512]{2,1,0:T(8,128)(2,1)}, bf16[2,224,512]{2,1,0:T(8,128)(2,1)}, f32[2,224,512]{2,1,0:T(8,12...) custom-call(s32[1]{0:T(128)} %bitcast.2.sec_ref, bf16[14,16,512]{2,1,0:T(8,128)(2,1)S(1)} %get-tuple-element.271.returned_ref, ...), custom_call_target="tpu_custom_call" | custom-call | flops 939524096 | bytes 8388608 | tf_op jit(solution)/shard_map/back_3_0/pallas_call | solution.py:694
  56.7 1.3 collective-permute-start.7
  58.0 5.7 %back_3_1.1 = (bf16[14,16,512]{2,1,0:T(8,128)(2,1)S(1)}, bf16[2,224,512]{2,1,0:T(8,128)(2,1)}, bf16[2,224,512]{2,1,0:T(8,128)(2,1)}, f32[2,224,512]{2,1,0:T(8,12...) custom-call(s32[1]{0:T(128)} %bitcast.2.sec_ref, ...), custom_call_target="tpu_custom_call", output_to_operand_aliasing={{1}: (12, {}), {2}: (13, {}), {3}: (14, {}), {4}: (15, {}),... | custom-call | flops 939524096 | bytes 8388608 | tf_op jit(solution)/shard_map/back_3_1/pallas_call | solution.py:694
  63.7 1.3 collective-permute-start.6
  66.2 4.3 %back_2_1.1 = (bf16[14,16,512]{2,1,0:T(8,128)(2,1)S(1)}, bf16[2,224,512]{2,1,0:T(8,128)(2,1)}, bf16[2,224,512]{2,1,0:T(8,128)(2,1)}, f32[2,224,512]{2,1,0:T(8,12...) custom-call(s32[1]{0:T(128)} %bitcast.2.sec_ref, ...), custom_call_target="tpu_custom_call", output_to_operand_aliasing={{1}: (12, {}), {2}: (13, {}), {3}: (14, {}), {4}: (15, {}),... | custom-call | flops 939524096 | bytes 8388608 | tf_op jit(solution)/shard_map/back_2_1/pallas_call | solution.py:694
  74.0 1.1 back_0_1.1
  75.0 8.2 %send.1 = bf16[24,512,128]{2,1,0:T(8,128)(2,1)} custom-call(s32[16]{0:T(128)S(1)} %get-tuple-element.265.order_ref, s32[16]{0:T(128)S(1)} %broadcast_clamp_fusion.1.slot_ref, bf16[2560,448]{1,0:T(8,128)(2,1)} %get-tuple-element.235.turned_ref, bf16[2,224,2560]{2,1,0:T(8,128)(2,1)} %get-tuple-element.236.both_ref.refs_13_, f32[512,2048]{1,0:T(8,128)} %bitcast.134, ...), custom_call_target="tpu_custom_call" | custom-call | flops 1073741824 | bytes 8388608 | tf_op jit(solution)/shard_map/send/pallas_call | solution.py:789
  83.2 7.2 %all-to-all-start = ((bf16[24,512,128]{2,1,0:T(8,128)(2,1)}), bf16[24,512,128]{2,1,0:T(8,128)(2,1)}, u32[]{:S(2)}, u32[]{:S(2)}) async-start(bf16[24,512,128]{2,1,0:T(8,128)(2,1)} %send.1), calls=%async_computation | async-start | bytes 6291456 | tf_op jit(solution)/shard_map/all_to_all | solution.py:902
  90.7 8.5 %small.1 = (f32[49,1,512]{2,1,0:T(1,128)S(1)}, f32[1,512]{1,0:T(1,128)S(1)}, f32[1,512]{1,0:T(1,128)S(1)}, f32[1,512]{1,0:T(1,128)S(1)}, f32[1,2048]{1,0:T(1,128...) custom-call(f32[49,1,512]{2,1,0:T(1,128)S(1)} %bitcast.58, f32[1,512]{1,0:T(1,128)S(1)} %bitcast.110, ...), custom_call_target="tpu_custom_call" | custom-call | flops 268435456 | bytes 8388608 | tf_op jit(solution)/shard_map/small/pallas_call | solution.py:731
  99.2 8.7 %keep.1 = (bf16[32,512,128]{2,1,0:T(8,128)(2,1)}, f32[512,2048]{1,0:T(8,128)}, f32[2048,512]{1,0:T(8,128)}) custom-call(s32[16]{0:T(128)S(1)} %select_reduce_fusion.order_ref.slot_ref, s32[16]{0:T(128)S(1)} %select_reduce_fusion.order_ref.slot_ref, bf16[2560,448]{1,0:T(8,128)(2,1)} %get-tuple-element.235.turned_ref, ...), custom_call_target="tpu_custom_call" | custom-call | flops 1073741824 | bytes 8388608 | tf_op jit(solution)/shard_map/keep/pallas_call | solution.py:789
  107.9 48.6 %all-to-all-done.arrived_ref.refs_8_ = bf16[24,512,128]{2,1,0:T(8,128)(2,1)} async-done(((bf16[24,512,128]{2,1,0:T(8,128)(2,1)}), bf16[24,512,128]{2,1,0:T(8,128)(2,1)}, u32[]{:S(2)}, u32[]{:S(2)}) %all-to-all-start) | async-done | bytes 3145760 | tf_op jit(solution)/shard_map/all_to_all | solution.py:902
  160.5 1.3 collective-permute-start.14
  161.8 3.7 %place.1 = (f32[512,2048]{1,0:T(8,128)}, f32[2048,512]{1,0:T(8,128)}) custom-call(s32[16]{0:T(128)S(1)} %get-tuple-element.265.order_ref, s32[16]{0:T(128)S(1)} %broadcast_clamp_fusion.2.slot_ref, bf16[24,512,128]{2,1,0:T(8,128)(2,1)} %all-to-all-done.arrived_ref.refs_8_, ...), custom_call_target="tpu_custom_call", output_to_operand_aliasing={{0}: (3, {}), {1}: (4, {})} | custom-call | bytes 8388608 | tf_op jit(solution)/shard_map/place/pallas_call | solution.py:919
  165.5 38.4 %collective-permute-done.14.received_ref = bf16[14,16,512]{2,1,0:T(8,128)(2,1)S(1)} collective-permute-done((bf16[14,16,512]{2,1,0:T(8,128)(2,1)S(1)}, bf16[14,16,512]{2,1,0:T(8,128)(2,1)S(1)}, u32[]{:S(2)}, u32[]{:S(2)}) %collective-permute-start.14) | collective-permute-done | bytes 229408 | tf_op jit(solution)/shard_map/ppermute | solution.py:993
  203.9 7.4 %probe3.1 = (bf16[14,16,512]{2,1,0:T(8,128)(2,1)}, bf16[14,14,512]{2,1,0:T(8,128)(2,1)}) custom-call(s32[1]{0:T(128)} %bitcast.2.sec_ref, s32[32]{0:T(128)S(1)} %bitcast.132, s32[32]{0:T(128)S(1)} %get-tuple-element.269.slot_ref, bf16[14,16,512]{2,1,0:T(8,128)(2,1)S(1)} %collective-permute-done.14.received_ref, ...), custom_call_target="tpu_custom_call", output_to_operand_aliasing={{1}: (14, {})} | custom-call | flops 939524096 | bytes 8388608 | tf_op jit(solution)/shard_map/probe3/pallas_call | solution.py:966
  (88 shorter events, 17.4 us)
Async XLA Ops:
  10.5 1.3 copy-start
  10.5 2.0 collective-permute-start.1
  11.2 1.3 copy-start.3
  11.2 1.3 copy-start.5
  11.2 1.3 copy-start.7
  11.8 3.2 %collective-permute-start = (bf16[14,16,512]{2,1,0:T(8,128)(2,1)S(1)}, bf16[14,16,512]{2,1,0:T(8,128)(2,1)S(1)}, u32[]{:S(2)}, u32[]{:S(2)}) collective-permute-start(bf16[14,16,512]{2,1,0:T(8,128)(2,1)S(1)} %get-tuple-element.141), channel_id=1, source_target_pairs={{0,1},{4,5},{8,9},{12,13},{16,17},{20,21},{24,25},{28,29}} | collective-permute-start | bytes 688136 | tf_op jit(solution)/shard_map/ppermute | solution.py:862
  12.6 1.6 copy-start.1
  14.3 1.6 collective-permute-start.3
  15.1 2.2 %collective-permute-start.2 = (bf16[14,16,512]{2,1,0:T(8,128)(2,1)S(1)}, bf16[14,16,512]{2,1,0:T(8,128)(2,1)S(1)}, u32[]{:S(2)}, u32[]{:S(2)}) collective-permute-start(bf16[14,16,512]{2,1,0:T(8,128)(2,1)S(1)} %get-tuple-element.157), channel_id=1, source_target_pairs={{1,2},{5,6},{9,10},{13,14},{17,18},{21,22},{25,26},{29,30}} | collective-permute-start | bytes 688136 | tf_op jit(solution)/shard_map/ppermute | solution.py:862
  16.0 20.6 %collective-permute-start.5 = (bf16[14,16,512]{2,1,0:T(8,128)(2,1)S(1)}, bf16[14,16,512]{2,1,0:T(8,128)(2,1)S(1)}, u32[]{:S(2)}, u32[]{:S(2)}) collective-permute-start(bf16[14,16,512]{2,1,0:T(8,128)(2,1)S(1)} %get-tuple-element.174), channel_id=1, source_target_pairs={{2,3},{6,7},{10,11},{14,15},{18,19},{22,23},{26,27},{30,31}} | collective-permute-start | bytes 688136 | tf_op jit(solution)/shard_map/ppermute | solution.py:862
  17.3 1.5 copy-start.17
  17.4 26.6 %collective-permute-start.4 = (bf16[14,16,512]{2,1,0:T(8,128)(2,1)S(1)}, bf16[14,16,512]{2,1,0:T(8,128)(2,1)S(1)}, u32[]{:S(2)}, u32[]{:S(2)}) collective-permute-start(bf16[14,16,512]{2,1,0:T(8,128)(2,1)S(1)} %get-tuple-element.173), channel_id=1, source_target_pairs={{2,3},{6,7},{10,11},{14,15},{18,19},{22,23},{26,27},{30,31}} | collective-permute-start | bytes 688136 | tf_op jit(solution)/shard_map/ppermute | solution.py:862
  56.7 8.7 %collective-permute-start.7 = (bf16[14,16,512]{2,1,0:T(8,128)(2,1)S(1)}, bf16[14,16,512]{2,1,0:T(8,128)(2,1)S(1)}, u32[]{:S(2)}, u32[]{:S(2)}) collective-permute-start(bf16[14,16,512]{2,1,0:T(8,128)(2,1)S(1)} %get-tuple-element.200), channel_id=1, source_target_pairs={{3,2},{7,6},{11,10},{15,14},{19,18},{23,22},{27,26},{31,30}} | collective-permute-start | bytes 688136 | tf_op jit(solution)/shard_map/ppermute | solution.py:885
  58.0 7.0 %copy-start.19 = (s32[1,32,8]{1,2,0:T(8,128)S(1)}, s32[1,32,8]{1,2,0:T(8,128)}, u32[]{:S(2)}) copy-start(s32[1,32,8]{1,2,0:T(8,128)} %param.27) | copy-start | bytes 3076
  63.7 2.5 %collective-permute-start.6 = (bf16[14,16,512]{2,1,0:T(8,128)(2,1)S(1)}, bf16[14,16,512]{2,1,0:T(8,128)(2,1)S(1)}, u32[]{:S(2)}, u32[]{:S(2)}) collective-permute-start(bf16[14,16,512]{2,1,0:T(8,128)(2,1)S(1)} %get-tuple-element.199), channel_id=1, source_target_pairs={{3,2},{7,6},{11,10},{15,14},{19,18},{23,22},{27,26},{31,30}} | collective-permute-start | bytes 688136 | tf_op jit(solution)/shard_map/ppermute | solution.py:885
  65.5 5.9 %collective-permute-start.9 = (bf16[14,16,512]{2,1,0:T(8,128)(2,1)S(1)}, bf16[14,16,512]{2,1,0:T(8,128)(2,1)S(1)}, u32[]{:S(2)}, u32[]{:S(2)}) collective-permute-start(bf16[14,16,512]{2,1,0:T(8,128)(2,1)S(1)} %get-tuple-element.212), channel_id=1, source_target_pairs={{2,1},{6,5},{10,9},{14,13},{18,17},{22,21},{26,25},{30,29}} | collective-permute-start | bytes 688136 | tf_op jit(solution)/shard_map/ppermute | solution.py:885
  70.6 1.7 collective-permute-start.8
  71.6 1.5 collective-permute-start.11
  72.4 1.5 collective-permute-start.10
  83.2 7.4 %copy-start.18 = (bf16[1,1,14,14,512]{4,3,2,1,0:T(8,128)(2,1)S(1)}, bf16[1,1,14,14,512]{4,3,2,1,0:T(8,128)(2,1)}, u32[]{:S(2)}) copy-start(bf16[1,1,14,14,512]{4,3,2,1,0:T(8,128)(2,1)} %param.16) | copy-start | bytes 602116
  83.2 73.3 %all-to-all-start = ((bf16[24,512,128]{2,1,0:T(8,128)(2,1)}), bf16[24,512,128]{2,1,0:T(8,128)(2,1)}, u32[]{:S(2)}, u32[]{:S(2)}) async-start(bf16[24,512,128]{2,1,0:T(8,128)(2,1)} %send.1), calls=%async_computation | async-start | bytes 6291456 | tf_op jit(solution)/shard_map/all_to_all | solution.py:902
  157.4 0.7 collective-permute-start.12
  158.9 0.7 collective-permute-start.13
  160.5 43.4 %collective-permute-start.14 = (bf16[14,16,512]{2,1,0:T(8,128)(2,1)S(1)}, bf16[14,16,512]{2,1,0:T(8,128)(2,1)S(1)}, u32[]{:S(2)}, u32[]{:S(2)}) collective-permute-start(bf16[14,16,512]{2,1,0:T(8,128)(2,1)S(1)} %get-tuple-element.258), channel_id=1, source_target_pairs={{2,3},{6,7},{10,11},{14,15},{18,19},{22,23},{26,27},{30,31}} | collective-permute-start | bytes 688136 | tf_op jit(solution)/shard_map/ppermute | solution.py:993
  (12 other events, 11.1 us)

commit v6 on v5

--- a/solution.py
+++ b/solution.py
@@ -133,7 +133,7 @@
     return pl.ds(pl.multiple_of(piece * channels, channels), channels)
 
 
-def train_kernel(owner, slot, side, kept, sec_ref, entry_ref, *refs):
+def train_kernel(owner, slot, side, passing, kept, sec_ref, entry_ref, *refs):
     vectors, (first_ref, second_ref) = refs[:7], refs[7:9]
     refs = refs[9 + kept :]
     y_ref, outs = refs[0], refs[1:8]
@@ -217,7 +217,8 @@
 
         conv_norm(vectors, entry, padded, spread, n_buf, hat_store)
         result, mixed = mix(side, vectors, entry, total, weights, n_buf, hidden_store)
-        y_ref[...] = result.astype(BF16)
+        if passing:
+            y_ref[...] = result.astype(BF16)
         mixed_buf[...] = mixed
         copies[4].start()
         for copy in copies:
@@ -304,103 +305,111 @@
         done.wait()
 
 
+def back_body(owner, which, side, returned_ref, params, saved, dx_ref, outs, bufs):
+    kernel_ref, gain_ref, scale_ref, first_ref, second_ref = params
+    hat_ref, inverse_ref, slope_ref = saved
+    both_out = outs[3]
+    dy_buf, dn_buf, dspread_buf, both_buf, hat_buf, inverse_buf, slope_buf = bufs[:7]
+    padded, total, conv_out, sems, piece_sems, in_sems = bufs[7:]
+    hid = slope_buf.shape[-1]
+    height, width, channels = returned_ref.shape
+    pieces = hid // channels
+    rows = height * width
+    ins = [
+        pltpu.make_async_copy(
+            slope_ref.at[which, :, columns(piece, channels)],
+            slope_buf.at[:, columns(piece, channels)],
+            in_sems.at[piece],
+        )
+        for piece in range(pieces)
+    ]
+    ins.append(pltpu.make_async_copy(hat_ref.at[which], hat_buf, in_sems.at[pieces]))
+    ins.append(pltpu.make_async_copy(inverse_ref.at[which], inverse_buf, in_sems.at[pieces + 1]))
+    for copy in ins:
+        copy.start()
+    dy = returned_ref[...].astype(F32)
+    flat = dy.reshape(rows, channels)
+    dy_buf[...] = flat.astype(BF16)
+    mix_at = columns(pieces, channels)
+    both_buf[:, mix_at] = (flat * scale_ref[...]).astype(BF16)
+    total[...] = jnp.zeros(total.shape, F32)
+    contract = (((1,), (1,)), ((), ()))
+    copies = [
+        pltpu.make_async_copy(buf, out.at[which], sems.at[index])
+        for index, (buf, out) in enumerate(zip((dy_buf, dn_buf, dspread_buf), outs))
+    ]
+    copies[0].start()
+
+    def both_copy(piece):
+        at = columns(piece, channels)
+        return pltpu.make_async_copy(
+            both_buf.at[:, at], both_out.at[which, :, at], piece_sems.at[piece]
+        )
+
+    both_copy(pieces).start()
+
+    def body(piece, carry):
+        at = columns(piece, channels)
+        dh = lax.dot_general(
+            both_buf[:, mix_at], second_ref[at, :], contract, preferred_element_type=F32
+        )
+        pltpu.make_async_copy(
+            slope_ref.at[which, :, at], slope_buf.at[:, at], in_sems.at[piece]
+        ).wait()
+        dpre = (dh * slope_buf[:, at].astype(F32)).astype(BF16)
+        both_buf[:, at] = dpre
+        both_copy(piece).start()
+        total[...] += lax.dot_general(
+            dpre, first_ref[:, at], contract, preferred_element_type=F32
+        )
+        return carry
+
+    lax.fori_loop(0, pieces, body, 0)
+    ins[pieces].wait()
+    ins[pieces + 1].wait()
+    dn = total[...]
+    dn_buf[...] = dn.astype(BF16)
+    copies[1].start()
+    hat = hat_buf[...]
+    dhat = dn * gain_ref[...]
+    mean = jnp.mean(dhat, axis=-1, keepdims=True)
+    along = jnp.mean(dhat * hat, axis=-1, keepdims=True)
+    dspread = inverse_buf[:, 0:1] * (dhat - mean - hat * along)
+    dspread_buf[...] = dspread
+    copies[2].start()
+    if owner > 0:
+        fill_padded(padded, dspread.reshape(height, width, channels))
+
+        def conv_body(chunk, carry):
+            def store(out, value):
+                conv_out[out, :, lanes(chunk)] = value
+
+            convolve(padded, chunk, kernel_ref, height, width, True, store)
+            return carry
+
+        lax.fori_loop(0, channels // TILE, conv_body, 0)
+        dx = dy + conv_out[...]
+        dx = jnp.where(real_columns(dx.shape, side), dx, 0.0)
+        dx_ref[...] = dx.astype(BF16)
+    for copy in copies:
+        copy.wait()
+    for piece in range(pieces + 1):
+        both_copy(piece).wait()
+
+
 def back_kernel(owner, which, side, turning, kept, sec_ref, returned_ref, *refs):
-    kernel_ref, gain_ref, scale_ref, first_ref, second_ref = refs[:5]
-    hat_ref, inverse_ref, slope_ref, n_ref, h_ref = refs[5:10]
+    params, saved, (n_ref, h_ref) = refs[:5], refs[5:8], refs[8:10]
     refs = refs[10 + kept :]
     dx_ref, outs, turned_ref = refs[0], refs[1:5], refs[5]
-    dy_buf, dn_buf, dspread_buf, both_buf, turned_buf = refs[6:11]
-    hat_buf, inverse_buf, slope_buf, n_buf, h_buf = refs[11:16]
-    padded, total, conv_out, sems, piece_sems, in_sems = refs[16:]
-    both_out = outs[3]
-    channels = dx_ref.shape[-1]
-    hid = h_buf.shape[-1]
-    pieces = hid // channels
+    turned_buf, n_buf, h_buf = refs[6:9]
+    bufs = refs[9:]
+    sems = bufs[10]
+    channels = returned_ref.shape[-1]
+    pieces = h_buf.shape[-1] // channels
 
     @pl.when(sec_ref[0] == owner)
     def _():
-        height, width, _ = dx_ref.shape
-        rows = height * width
-        ins = [
-            pltpu.make_async_copy(
-                slope_ref.at[which, :, columns(piece, channels)],
-                slope_buf.at[:, columns(piece, channels)],
-                in_sems.at[piece],
-            )
-            for piece in range(pieces)
-        ]
-        ins.append(pltpu.make_async_copy(hat_ref.at[which], hat_buf, in_sems.at[pieces]))
-        ins.append(pltpu.make_async_copy(inverse_ref.at[which], inverse_buf, in_sems.at[pieces + 1]))
-        for copy in ins:
-            copy.start()
-        dy = returned_ref[...].astype(F32)
-        flat = dy.reshape(rows, channels)
-        dy_buf[...] = flat.astype(BF16)
-        mix_at = columns(pieces, channels)
-        both_buf[:, mix_at] = (flat * scale_ref[...]).astype(BF16)
-        total[...] = jnp.zeros(total.shape, F32)
-        contract = (((1,), (1,)), ((), ()))
-        copies = [
-            pltpu.make_async_copy(buf, out.at[which], sems.at[index])
-            for index, (buf, out) in enumerate(zip((dy_buf, dn_buf, dspread_buf), outs))
-        ]
-        copies[0].start()
-
-        def both_copy(piece):
-            at = columns(piece, channels)
-            return pltpu.make_async_copy(
-                both_buf.at[:, at], both_out.at[which, :, at], piece_sems.at[piece]
-            )
-
-        both_copy(pieces).start()
-
-        def body(piece, carry):
-            at = columns(piece, channels)
-            dh = lax.dot_general(
-                both_buf[:, mix_at], second_ref[at, :], contract, preferred_element_type=F32
-            )
-            pltpu.make_async_copy(
-                slope_ref.at[which, :, at], slope_buf.at[:, at], in_sems.at[piece]
-            ).wait()
-            dpre = (dh * slope_buf[:, at].astype(F32)).astype(BF16)
-            both_buf[:, at] = dpre
-            both_copy(piece).start()
-            total[...] += lax.dot_general(
-                dpre, first_ref[:, at], contract, preferred_element_type=F32
-            )
-            return carry
-
-        lax.fori_loop(0, pieces, body, 0)
-        ins[pieces].wait()
-        ins[pieces + 1].wait()
-        dn = total[...]
-        dn_buf[...] = dn.astype(BF16)
-        copies[1].start()
-        hat = hat_buf[...]
-        dhat = dn * gain_ref[...]
-        mean = jnp.mean(dhat, axis=-1, keepdims=True)
-        along = jnp.mean(dhat * hat, axis=-1, keepdims=True)
-        dspread = inverse_buf[:, 0:1] * (dhat - mean - hat * along)
-        dspread_buf[...] = dspread
-        copies[2].start()
-        if owner > 0:
-            fill_padded(padded, dspread.reshape(height, width, channels))
-
-            def conv_body(chunk, carry):
-                def store(out, value):
-                    conv_out[out, :, lanes(chunk)] = value
-
-                convolve(padded, chunk, kernel_ref, height, width, True, store)
-                return carry
-
-            lax.fori_loop(0, channels // TILE, conv_body, 0)
-            dx = dy + conv_out[...]
-            dx = jnp.where(real_columns(dx.shape, side), dx, 0.0)
-            dx_ref[...] = dx.astype(BF16)
-        for copy in copies:
-            copy.wait()
-        for piece in range(pieces + 1):
-            both_copy(piece).wait()
+        back_body(owner, which, side, returned_ref, params, saved, dx_ref, outs, bufs)
 
     if turning is not None:
         low, high = turning
@@ -499,30 +508,38 @@
         act(second_ref.at[columns(group, channels), lanes(lax.div(place, groups))])
 
 
-def update_kernel(
-    first_tiles, groups, sending, order_ref, slot_ref, turned_ref, both_ref, first_ref, second_ref, *refs
-):
-    if sending:
-        (send_ref, wide_buf, slim_buf, in_sems, out_sems) = refs
-    else:
-        (own_ref, new_first, new_second, wide_buf, slim_buf, in_sems, out_sems, wide_sems) = refs
-    count = wide_buf.shape[0]
-    channels = wide_buf.shape[1]
-    micro, rows, _ = both_ref.shape
-    batch = math.gcd(count, 4)
-
+def fetch_blocks(order_ref, first_tiles, groups, first_ref, second_ref, wide_buf, in_sems):
     def fetch(step, carry):
         def act(view):
             pltpu.make_async_copy(view, wide_buf.at[step], in_sems.at[step]).start()
 
+        channels = wide_buf.shape[1]
         block_views(order_ref[step], first_tiles, groups, channels, first_ref, second_ref, act)
         return carry
 
-    lax.fori_loop(0, count, fetch, 0)
+    lax.fori_loop(0, wide_buf.shape[0], fetch, 0)
+
+
+def update_blocks(
+    first_tiles,
+    groups,
+    order_ref,
+    turned_ref,
+    both_ref,
+    first_ref,
+    wide_buf,
+    slim_buf,
+    in_sems,
+    out_sems,
+    slim_target,
+    wide_out,
+):
+    count, channels, _ = wide_buf.shape
+    micro, rows, _ = both_ref.shape
+    batch = math.gcd(count, 4)
 
     def slim_copy(step):
-        target = send_ref.at[slot_ref[step]] if sending else own_ref.at[order_ref[step]]
-        return pltpu.make_async_copy(slim_buf.at[step], target, out_sems.at[step])
+        return pltpu.make_async_copy(slim_buf.at[step], slim_target(step), out_sems.at[step])
 
     def body(turn, carry):
         steps = [turn * batch + item for item in range(batch)]
@@ -543,11 +560,12 @@
             )
             updated = wide_buf[step] - learning_rate * grad
             slim_buf[step] = updated.astype(BF16)
-            if not sending:
+            if wide_out is not None:
                 wide_buf[step] = updated
         for step in steps:
             slim_copy(step).start()
-            if not sending:
+            if wide_out is not None:
+                new_first, new_second, wide_sems = wide_out
 
                 def act(view, step=step):
                     pltpu.make_async_copy(wide_buf.at[step], view, wide_sems.at[step]).start()
@@ -561,13 +579,84 @@
 
     def drain(step, carry):
         slim_copy(step).wait()
-        if not sending:
+        if wide_out is not None:
+            new_first, new_second, wide_sems = wide_out
             pltpu.make_async_copy(
                 wide_buf.at[step], new_first.at[:, lanes(0)], wide_sems.at[step]
             ).wait()
         return carry
 
     lax.fori_loop(0, count, drain, 0)
+
+
+def keep_kernel(
+    first_tiles, groups, order_ref, turned_ref, both_ref, first_ref, second_ref, *refs
+):
+    own_ref, new_first, new_second, wide_buf, slim_buf, in_sems, out_sems, wide_sems = refs
+    fetch_blocks(order_ref, first_tiles, groups, first_ref, second_ref, wide_buf, in_sems)
+    update_blocks(
+        first_tiles,
+        groups,
+        order_ref,
+        turned_ref,
+        both_ref,
+        first_ref,
+        wide_buf,
+        slim_buf,
+        in_sems,
+        out_sems,
+        lambda step: own_ref.at[order_ref[step]],
+        (new_first, new_second, wide_sems),
+    )
+
+
+def final_kernel(
+    side, first_tiles, groups, sec_ref, order_ref, slot_ref, returned_ref, *refs
+):
+    params, saved, (first_ref, second_ref) = refs[:5], refs[5:8], refs[8:10]
+    old_both, turned_ref = refs[13], refs[14]
+    outs, send_ref = refs[15:19], refs[19]
+    both_all, turned_buf, wide_buf, slim_buf, slot_sems, out_sems, more_sems = refs[20:27]
+    rest = refs[27:]
+    micro, rows, _ = both_all.shape
+    last = micro - 1
+    bufs = rest[:3] + (both_all.at[last],) + rest[3:]
+    idle = [
+        pltpu.make_async_copy(old_both.at[item], both_all.at[item], more_sems.at[item])
+        for item in range(micro)
+    ]
+    get_turned = pltpu.make_async_copy(turned_ref, turned_buf, more_sems.at[micro])
+    for copy in idle[:last]:
+        copy.start()
+    get_turned.start()
+    fetch_blocks(order_ref, first_tiles, groups, first_ref, second_ref, wide_buf, slot_sems)
+
+    @pl.when(sec_ref[0] == 0)
+    def _():
+        back_body(0, last, side, returned_ref, params, saved, None, outs, bufs)
+
+    @pl.when(sec_ref[0] != 0)
+    def _():
+        idle[last].start()
+        idle[last].wait()
+
+    for copy in idle[:last]:
+        copy.wait()
+    get_turned.wait()
+    update_blocks(
+        first_tiles,
+        groups,
+        order_ref,
+        turned_buf,
+        both_all,
+        first_ref,
+        wide_buf,
+        slim_buf,
+        slot_sems,
+        out_sems,
+        lambda step: send_ref.at[slot_ref[step]],
+        None,
+    )
 
 
 def place_kernel(
@@ -621,7 +710,7 @@
     return pl.BlockSpec(memory_space=pltpu.HBM)
 
 
-def train_step(owner, slot, micro, side, sec, received, vectors, weights, saved):
+def train_step(owner, slot, passing, micro, side, sec, received, vectors, weights, saved):
     height, width, channels = received.shape
     rows = height * width
     hid = vectors[4].shape[1]
@@ -636,6 +725,8 @@
     ]
     kept = 0 if saved is None else len(saved)
     operands = [received, *vectors, *weights] + ([] if saved is None else pinned(saved))
+    if saved is None:
+        operands[1:8] = pinned(vectors)
     in_specs = [whole(item) for item in operands[: len(operands) - kept]]
     in_specs += [hbm_spec()] * kept
     more_specs, more_shapes, more_scratch = [], [], []
@@ -647,12 +738,14 @@
         wide = pltpu.VMEM((hid // channels, channels, channels), F32)
         more_scratch = [wide, wide, pltpu.SemaphoreType.DMA((2, hid // channels))]
     outs = pl.pallas_call(
-        functools.partial(train_kernel, owner, slot, side, kept),
+        functools.partial(train_kernel, owner, slot, side, passing, kept),
         grid_spec=pltpu.PrefetchScalarGridSpec(
             num_scalar_prefetch=1,
             grid=(1,),
             in_specs=in_specs,
-            out_specs=[whole(received)] + [hbm_spec() for _ in saved_shapes] + more_specs,
+            out_specs=[whole(received) if passing else hbm_spec()]
+            + [hbm_spec() for _ in saved_shapes]
+            + more_specs,
             scratch_shapes=[pltpu.VMEM(shape, dtype) for shape, dtype in saved_shapes]
             + [
                 pltpu.VMEM((channels // TILE, height + 2 * REACH, width + 2 * EDGE, TILE), F32),
@@ -672,6 +765,61 @@
         name=f"train_{owner}_{slot}",
     )(sec, *operands)
     return outs[0], outs[1:8], outs[8:] if saved is None else weights
+
+
+def back_scratch(height, width, channels, hid):
+    rows = height * width
+    return [
+        pltpu.VMEM((rows, channels), F32),
+        pltpu.VMEM((rows, TILE), F32),
+        pltpu.VMEM((rows, hid), BF16),
+        pltpu.VMEM((channels // TILE, height + 2 * REACH, width + 2 * EDGE, TILE), F32),
+        pltpu.VMEM((rows, channels), F32),
+        pltpu.VMEM((height, width, channels), F32),
+        pltpu.SemaphoreType.DMA((3,)),
+        pltpu.SemaphoreType.DMA((hid // channels + 1,)),
+        pltpu.SemaphoreType.DMA((hid // channels + 2,)),
+    ]
+
+
+def final_step(side, table, sec, returned, params, saved, weights, kept_out):
+    height, width, channels = returned.shape
+    rows = height * width
+    first, second = weights
+    hid = first.shape[1]
+    turned = kept_out[4]
+    micro = kept_out[3].shape[0]
+    count = table["marked_order"].shape[0]
+    operands = [returned, *params, *pinned((*saved, *weights, *kept_out))]
+    in_specs = [whole(item) for item in operands[:6]] + [hbm_spec()] * (len(operands) - 6)
+    shapes = [(item.shape, item.dtype) for item in kept_out[:4]]
+    outs = pl.pallas_call(
+        functools.partial(final_kernel, side, hid // TILE, hid // channels),
+        grid_spec=pltpu.PrefetchScalarGridSpec(
+            num_scalar_prefetch=3,
+            grid=(1,),
+            in_specs=in_specs,
+            out_specs=[hbm_spec()] * 5,
+            scratch_shapes=[
+                pltpu.VMEM((micro, rows, hid + channels), BF16),
+                pltpu.VMEM(turned.shape, BF16),
+                pltpu.VMEM((count, channels, TILE), F32),
+                pltpu.VMEM((count, channels, TILE), BF16),
+                pltpu.SemaphoreType.DMA((count,)),
+                pltpu.SemaphoreType.DMA((count,)),
+                pltpu.SemaphoreType.DMA((micro + 1,)),
+            ]
+            + [pltpu.VMEM(shape[1:], dtype) for shape, dtype in shapes[:3]]
+            + back_scratch(height, width, channels, hid),
+        ),
+        out_shape=[pltpu.HBM(shape, dtype) for shape, dtype in shapes]
+        + [pltpu.HBM((table["slots"], channels, TILE), BF16)],
+        input_output_aliases={3 + 11 + i: i for i in range(4)},
+        compiler_params=params_of(),
+        cost_estimate=cost(4 * rows * channels * hid, 8 << 20),
+        name="final",
+    )(sec, table["marked_order"], table["send_slots"], *operands)
+    return [*outs[:4], turned], outs[4]
 
 
 def back_step(owner, which, micro, side, turning, sec, returned, params, saved, kept_out):
@@ -697,22 +845,15 @@
             num_scalar_prefetch=1,
             grid=(1,),
             in_specs=in_specs,
-            out_specs=[whole(returned)] + [hbm_spec()] * (len(shapes) + 1),
-            scratch_shapes=[pltpu.VMEM(shape, dtype) for shape, dtype in shapes]
-            + [
+            out_specs=[whole(returned) if owner > 0 else hbm_spec()]
+            + [hbm_spec()] * (len(shapes) + 1),
+            scratch_shapes=[
                 pltpu.VMEM(*turned),
-                pltpu.VMEM((rows, channels), F32),
-                pltpu.VMEM((rows, TILE), F32),
-                pltpu.VMEM((rows, hid), BF16),
                 pltpu.VMEM((micro, rows, channels), BF16),
                 pltpu.VMEM((micro, rows, hid), BF16),
-                pltpu.VMEM((channels // TILE, height + 2 * REACH, width + 2 * EDGE, TILE), F32),
-                pltpu.VMEM((rows, channels), F32),
-                pltpu.VMEM((height, width, channels), F32),
-                pltpu.SemaphoreType.DMA((3,)),
-                pltpu.SemaphoreType.DMA((hid // channels + 1,)),
-                pltpu.SemaphoreType.DMA((hid // channels + 2,)),
-            ],
+            ]
+            + [pltpu.VMEM(shape, dtype) for shape, dtype in shapes]
+            + back_scratch(height, width, channels, hid),
         ),
         out_shape=[shaped(returned.shape, BF16)]
         + [pltpu.HBM((micro,) + shape, dtype) for shape, dtype in shapes]
@@ -780,30 +921,29 @@
     )
 
 
-def update_step(sending, order, slots, turned, both, first, second, out_shape):
+def keep_step(order, turned, both, first, second, out_shape):
     count = order.shape[0]
     channels = first.shape[0]
     first_tiles = first.shape[1] // TILE
     groups = second.shape[0] // channels
-    sems = [pltpu.SemaphoreType.DMA((count,))] * (2 if sending else 3)
     return pl.pallas_call(
-        functools.partial(update_kernel, first_tiles, groups, sending),
+        functools.partial(keep_kernel, first_tiles, groups),
         grid_spec=pltpu.PrefetchScalarGridSpec(
-            num_scalar_prefetch=2,
+            num_scalar_prefetch=1,
             grid=(1,),
             in_specs=[whole(turned), whole(both), hbm_spec(), hbm_spec()],
             out_specs=[hbm_spec() for _ in out_shape],
             scratch_shapes=[
                 pltpu.VMEM((count, channels, TILE), F32),
                 pltpu.VMEM((count, channels, TILE), BF16),
-                *sems,
-            ],
+            ]
+            + [pltpu.SemaphoreType.DMA((count,))] * 3,
         ),
         out_shape=out_shape,
         compiler_params=params_of(),
         cost_estimate=cost(1 << 30, 8 << 20),
-        name="send" if sending else "keep",
-    )(order, slots, *pinned((turned, both, first, second)))
+        name="keep",
+    )(order, *pinned((turned, both, first, second)))
 
 
 def local(
@@ -856,7 +996,16 @@
         leaving = []
         for item in range(micro):
             current, saved, lowered = train_step(
-                owner, item, micro, side, sec, entries[item], vectors, lowered, saved
+                owner,
+                item,
+                owner < sections - 1,
+                micro,
+                side,
+                sec,
+                entries[item],
+                vectors,
+                lowered,
+                saved,
             )
             if owner < sections - 1:
                 leaving.append(lax.ppermute(current, "section", [(owner, owner + 1)]))
@@ -866,9 +1015,22 @@
     entries = [slopes[item] for item in range(micro)]
     grads = None
     turnings = {(sections - 1, 0): (0, sections - 1), (max(sections - 2, 0), micro - 1): (sections - 1, sections)}
+    table = tables(shuffle_mask[0], source_member[0])
     for owner in reversed(range(sections)):
         leaving = []
         for item in range(micro):
+            if owner == 0 and item == micro - 1 and grads is not None:
+                grads, outgoing = final_step(
+                    side,
+                    table,
+                    sec,
+                    entries[item],
+                    (kernel, gain, scale, *lowered),
+                    (hats, inverses, gelu_slopes),
+                    (first, second),
+                    grads,
+                )
+                continue
             current, grads = back_step(
                 owner,
                 item,
@@ -886,23 +1048,10 @@
         entries = leaving
     dys, dns, dspreads, boths, turned = grads
 
-    table = tables(shuffle_mask[0], source_member[0])
     taken = table["marked_order"].shape[0]
     blocks = shuffle_mask.shape[1]
-    (outgoing,) = update_step(
-        True,
-        table["marked_order"],
-        table["send_slots"],
-        turned,
-        boths,
-        first,
-        second,
-        [pltpu.HBM((table["slots"], channels, TILE), BF16)],
-    )
     arrived = lax.all_to_all(outgoing, "member", split_axis=0, concat_axis=0, tiled=True)
-    own, new_first, new_second = update_step(
-        False,
-        table["plain_order"],
+    own, new_first, new_second = keep_step(
         table["plain_order"],
         turned,
         boths,

time: 212 us -> 207 us (0.976)
  local copies, waits for them, and re-layouts: 8.29 us -> 3.3 us
    unnamed x42 -> x28, local copies, waits for them, and re-layouts: 8.17 us -> 3.19 us
    pallas_call x8 -> x7, Pallas kernels: 18.1 us -> 16.3 us  [back_step(): pl.pallas_call(functools.partial(back_kernel, owner, which, side, turning...]
  transfers between devices with their start and end apart: 16 -> 16, of which waited for: 4 -> 5; matrix products, arithmetic and copies ran while one was open for 0% -> 0% of each run, Pallas kernels for 19% -> 19%
where the time goes in v6:
time: 207 us; the launch traced here: 206 us
  waiting for transfers between devices  107 us (52%)
  Pallas kernels  73.4 us (35%)
  starting transfers between devices  20.4 us (10%)
  local copies, waits for them, and re-layouts  3.3 us (2%)
    all_to_all x1, waiting for transfers between devices, local(): lax.all_to_all(outgoing, 'member', split_axis=0, concat_axis=0, tiled=True)  48.6 us
    ppermute x3, waiting for transfers between devices, local(): received = lax.ppermute(result, 'section', [(tick, tick + 1)])  39.2 us
    ppermute x6, waiting for transfers between devices, local(): leaving.append(lax.ppermute(current, 'section', [(owner, owner + 1)]))  18.8 us
    pallas_call x8, Pallas kernels, train_step(): pl.pallas_call(functools.partial(train_kernel, owner, slot, side, passing...  17.7 us
    pallas_call x7, Pallas kernels, back_step(): pl.pallas_call(functools.partial(back_kernel, owner, which, side, turning...  16.3 us
    pallas_call x4, Pallas kernels, local(): pl.pallas_call(functools.partial(probe_kernel, tick, side, kept), grid_sp...  9.94 us
    pallas_call x1, Pallas kernels, keep_step(): pl.pallas_call(functools.partial(keep_kernel, first_tiles, groups), grid_...  8.65 us
    pallas_call x1, Pallas kernels, small_step(): pl.pallas_call(functools.partial(small_kernel, micro), grid=(1,), in_spec...  8.53 us
  transfers between devices with their start and end apart: 16, of which 5 were waited for; matrix products, arithmetic and copies ran while one was open for 0% of the time, Pallas kernels for 19%

profile of v6, /device:TPU:5, one launch (start us, length us, event | category | flops | bytes accessed | tf_op | source)
XLA Modules:
  0.0 206.1 jit_solution(15292781675028561380)
XLA Ops:
  0.6 1.1 copy.111
  1.8 4.7 %train_0_0.1 = (bf16[14,16,512]{2,1,0:T(8,128)(2,1)S(1)}, bf16[2,14,16,512]{3,2,1,0:T(8,128)(2,1)}, f32[2,224,512]{2,1,0:T(8,128)}, f32[2,224,128]{2,1,0:T(8,128...) custom-call(s32[1]{0:T(128)} %bitcast.2.sec_ref, ...), custom_call_target="tpu_custom_call" | custom-call | flops 939524096 | bytes 8388608 | tf_op jit(solution)/shard_map/train_0_0/pallas_call | solution.py:740
  8.6 1.6 copy-done.1
  12.1 1.3 collective-permute-start.5
  13.6 1.3 collective-permute-start.4
  15.2 17.5 %collective-permute-done.5.entry_ref = bf16[14,16,512]{2,1,0:T(8,128)(2,1)S(1)} collective-permute-done((bf16[14,16,512]{2,1,0:T(8,128)(2,1)S(1)}, bf16[14,16,512]{2,1,0:T(8,128)(2,1)S(1)}, u32[]{:S(2)}, u32[]{:S(2)}) %collective-permute-start.5) | collective-permute-done | bytes 229408 | tf_op jit(solution)/shard_map/ppermute | solution.py:1011
  32.7 6.2 %train_3_0.1 = (bf16[14,16,512]{2,1,0:T(8,128)(2,1)}, bf16[2,14,16,512]{3,2,1,0:T(8,128)(2,1)}, f32[2,224,512]{2,1,0:T(8,128)}, f32[2,224,128]{2,1,0:T(8,128)}, ...) custom-call(s32[1]{0:T(128)} %bitcast.2.sec_ref, ...), custom_call_target="tpu_custom_call", output_to_operand_aliasing={{1}: (11, {}), {2}: (12, {}), {3}: (13, {}), {4}: (14, {}),... | custom-call | flops 939524096 | bytes 8388608 | tf_op jit(solution)/shard_map/train_3_0/pallas_call | solution.py:740
  38.9 1.4 collective-permute-done.4.entry_ref
  40.2 6.2 %train_3_1.1 = (bf16[14,16,512]{2,1,0:T(8,128)(2,1)}, bf16[2,14,16,512]{3,2,1,0:T(8,128)(2,1)}, f32[2,224,512]{2,1,0:T(8,128)}, f32[2,224,128]{2,1,0:T(8,128)}, ...) custom-call(s32[1]{0:T(128)} %bitcast.2.sec_ref, ...), custom_call_target="tpu_custom_call", output_to_operand_aliasing={{1}: (11, {}), {2}: (12, {}), {3}: (13, {}), {4}: (14, {}),... | custom-call | flops 939524096 | bytes 8388608 | tf_op jit(solution)/shard_map/train_3_1/pallas_call | solution.py:740
  46.4 5.7 %back_3_0.1 = (bf16[14,16,512]{2,1,0:T(8,128)(2,1)S(1)}, bf16[2,224,512]{2,1,0:T(8,128)(2,1)}, bf16[2,224,512]{2,1,0:T(8,128)(2,1)}, f32[2,224,512]{2,1,0:T(8,12...) custom-call(s32[1]{0:T(128)} %bitcast.2.sec_ref, bf16[14,16,512]{2,1,0:T(8,128)(2,1)S(1)} %get-tuple-element.271.returned_ref, ...), custom_call_target="tpu_custom_call" | custom-call | flops 939524096 | bytes 8388608 | tf_op jit(solution)/shard_map/back_3_0/pallas_call | solution.py:842
  52.1 1.3 collective-permute-start.7
  53.4 5.7 %back_3_1.1 = (bf16[14,16,512]{2,1,0:T(8,128)(2,1)S(1)}, bf16[2,224,512]{2,1,0:T(8,128)(2,1)}, bf16[2,224,512]{2,1,0:T(8,128)(2,1)}, f32[2,224,512]{2,1,0:T(8,12...) custom-call(s32[1]{0:T(128)} %bitcast.2.sec_ref, ...), custom_call_target="tpu_custom_call", output_to_operand_aliasing={{1}: (12, {}), {2}: (13, {}), {3}: (14, {}), {4}: (15, {}),... | custom-call | flops 939524096 | bytes 8388608 | tf_op jit(solution)/shard_map/back_3_1/pallas_call | solution.py:842
  59.1 1.3 collective-permute-start.6
  61.5 4.3 %back_2_1.1 = (bf16[14,16,512]{2,1,0:T(8,128)(2,1)S(1)}, bf16[2,224,512]{2,1,0:T(8,128)(2,1)}, bf16[2,224,512]{2,1,0:T(8,128)(2,1)}, f32[2,224,512]{2,1,0:T(8,12...) custom-call(s32[1]{0:T(128)} %bitcast.2.sec_ref, ...), custom_call_target="tpu_custom_call", output_to_operand_aliasing={{1}: (12, {}), {2}: (13, {}), {3}: (14, {}), {4}: (15, {}),... | custom-call | flops 939524096 | bytes 8388608 | tf_op jit(solution)/shard_map/back_2_1/pallas_call | solution.py:842
  68.6 8.5 %final.1 = (bf16[2,224,512]{2,1,0:T(8,128)(2,1)}, bf16[2,224,512]{2,1,0:T(8,128)(2,1)}, f32[2,224,512]{2,1,0:T(8,128)}, bf16[2,224,2560]{2,1,0:T(8,128)(2,1)}, bf16[24,512,128]{2,1,0:T(8,128)(2,1)}) custom-call(s32[1]{0:T(128)} %bitcast.2.sec_ref, ...), custom_call_target="tpu_custom_call", output_to_operand_aliasing={{0}: (14, {}), {1}: (15, {}), {2}: (16, {}), {3}: (17, {})} | custom-call | flops 939524096 | bytes 8388608 | tf_op jit(solution)/shard_map/final/pallas_call | solution.py:796
  77.1 7.2 %all-to-all-start = ((bf16[24,512,128]{2,1,0:T(8,128)(2,1)}), bf16[24,512,128]{2,1,0:T(8,128)(2,1)}, u32[]{:S(2)}, u32[]{:S(2)}) async-start(bf16[24,512,128]{2,1,0:T(8,128)(2,1)} %get-tuple-element.235), calls=%async_computation | async-start | bytes 6291456 | tf_op jit(solution)/shard_map/all_to_all | solution.py:1053
  84.5 8.5 %small.1 = (f32[49,1,512]{2,1,0:T(1,128)S(1)}, f32[1,512]{1,0:T(1,128)S(1)}, f32[1,512]{1,0:T(1,128)S(1)}, f32[1,512]{1,0:T(1,128)S(1)}, f32[1,2048]{1,0:T(1,128...) custom-call(f32[49,1,512]{2,1,0:T(1,128)S(1)} %bitcast.58, f32[1,512]{1,0:T(1,128)S(1)} %bitcast.110, ...), custom_call_target="tpu_custom_call" | custom-call | flops 268435456 | bytes 8388608 | tf_op jit(solution)/shard_map/small/pallas_call | solution.py:872
  93.1 8.6 %keep.1 = (bf16[32,512,128]{2,1,0:T(8,128)(2,1)}, f32[512,2048]{1,0:T(8,128)}, f32[2048,512]{1,0:T(8,128)}) custom-call(s32[16]{0:T(128)S(1)} %select_reduce_fusion.order_ref, bf16[2560,448]{1,0:T(8,128)(2,1)} %get-tuple-element.234.refs_14_.turned_ref, bf16[2,224,2560]{2,1,0:T(8,128)(2,1)} %get-tuple-element.236.both_ref.refs_13_, f32[512,2048]{1,0:T(8,128)} %bitcast.135, ...), custom_call_target="tpu_custom_call" | custom-call | flops 1073741824 | bytes 8388608 | tf_op jit(solution)/shard_map/keep/pallas_call | solution.py:929
  101.8 48.6 %all-to-all-done.arrived_ref.refs_8_ = bf16[24,512,128]{2,1,0:T(8,128)(2,1)} async-done(((bf16[24,512,128]{2,1,0:T(8,128)(2,1)}), bf16[24,512,128]{2,1,0:T(8,128)(2,1)}, u32[]{:S(2)}, u32[]{:S(2)}) %all-to-all-start) | async-done | bytes 3145760 | tf_op jit(solution)/shard_map/all_to_all | solution.py:1053
  151.9 0.9 probe1.1
  154.3 1.3 collective-permute-start.14
  155.7 3.7 %place.1 = (f32[512,2048]{1,0:T(8,128)}, f32[2048,512]{1,0:T(8,128)}) custom-call(s32[16]{0:T(128)S(1)} %get-tuple-element.265.order_ref, s32[16]{0:T(128)S(1)} %broadcast_clamp_fusion.2.slot_ref, bf16[24,512,128]{2,1,0:T(8,128)(2,1)} %all-to-all-done.arrived_ref.refs_8_, ...), custom_call_target="tpu_custom_call", output_to_operand_aliasing={{0}: (3, {}), {1}: (4, {})} | custom-call | bytes 8388608 | tf_op jit(solution)/shard_map/place/pallas_call | solution.py:1068
  159.4 39.1 %collective-permute-done.14.received_ref = bf16[14,16,512]{2,1,0:T(8,128)(2,1)S(1)} collective-permute-done((bf16[14,16,512]{2,1,0:T(8,128)(2,1)S(1)}, bf16[14,16,512]{2,1,0:T(8,128)(2,1)S(1)}, u32[]{:S(2)}, u32[]{:S(2)}) %collective-permute-start.14) | collective-permute-done | bytes 229408 | tf_op jit(solution)/shard_map/ppermute | solution.py:1142
  198.6 7.4 %probe3.1 = (bf16[14,16,512]{2,1,0:T(8,128)(2,1)}, bf16[14,14,512]{2,1,0:T(8,128)(2,1)}) custom-call(s32[1]{0:T(128)} %bitcast.2.sec_ref, s32[32]{0:T(128)S(1)} %bitcast.132, s32[32]{0:T(128)S(1)} %get-tuple-element.269.slot_ref, bf16[14,16,512]{2,1,0:T(8,128)(2,1)S(1)} %collective-permute-done.14.received_ref, ...), custom_call_target="tpu_custom_call", output_to_operand_aliasing={{1}: (14, {})} | custom-call | flops 939524096 | bytes 8388608 | tf_op jit(solution)/shard_map/probe3/pallas_call | solution.py:1115
  (74 shorter events, 11.3 us)
Async XLA Ops:
  1.8 5.5 %copy-start.2 = (f32[1,1,7,7,512]{4,1,3,2,0:T(1,128)S(1)}, f32[1,1,7,7,512]{4,1,3,2,0:T(1,128)}, u32[]{:S(2)}) copy-start(f32[1,1,7,7,512]{4,1,3,2,0:T(1,128)} %param.17) | copy-start | bytes 301060
  1.8 5.5 %copy-start.3 = (f32[1,1,2048]{2,1,0:T(1,128)S(1)}, f32[1,1,2048]{2,1,0:T(1,128)}, u32[]{:S(2)}) copy-start(f32[1,1,2048]{2,1,0:T(1,128)} %param.22) | copy-start | bytes 24580
  1.8 5.5 %copy-start.4 = (f32[1,1,512]{2,1,0:T(1,128)S(1)}, f32[1,1,512]{2,1,0:T(1,128)}, u32[]{:S(2)}) copy-start(f32[1,1,512]{2,1,0:T(1,128)} %param.19) | copy-start | bytes 6148
  1.8 5.5 %copy-start.5 = (f32[1,1,512]{2,1,0:T(1,128)S(1)}, f32[1,1,512]{2,1,0:T(1,128)}, u32[]{:S(2)}) copy-start(f32[1,1,512]{2,1,0:T(1,128)} %param.25) | copy-start | bytes 6148
  1.8 5.5 %copy-start.6 = (f32[1,1,512]{2,1,0:T(1,128)S(1)}, f32[1,1,512]{2,1,0:T(1,128)}, u32[]{:S(2)}) copy-start(f32[1,1,512]{2,1,0:T(1,128)} %param.18) | copy-start | bytes 6148
  1.8 5.5 %copy-start.7 = (f32[1,1,512]{2,1,0:T(1,128)S(1)}, f32[1,1,512]{2,1,0:T(1,128)}, u32[]{:S(2)}) copy-start(f32[1,1,512]{2,1,0:T(1,128)} %param.20) | copy-start | bytes 6148
  1.8 5.5 %copy-start.8 = (f32[1,1,512]{2,1,0:T(1,128)S(1)}, f32[1,1,512]{2,1,0:T(1,128)}, u32[]{:S(2)}) copy-start(f32[1,1,512]{2,1,0:T(1,128)} %param.24) | copy-start | bytes 6148
  6.6 2.0 collective-permute-start.1
  7.9 3.1 %collective-permute-start = (bf16[14,16,512]{2,1,0:T(8,128)(2,1)S(1)}, bf16[14,16,512]{2,1,0:T(8,128)(2,1)S(1)}, u32[]{:S(2)}, u32[]{:S(2)}) collective-permute-start(bf16[14,16,512]{2,1,0:T(8,128)(2,1)S(1)} %get-tuple-element.141), channel_id=1, source_target_pairs={{0,1},{4,5},{8,9},{12,13},{16,17},{20,21},{24,25},{28,29}} | collective-permute-start | bytes 688136 | tf_op jit(solution)/shard_map/ppermute | solution.py:1011
  10.3 1.6 collective-permute-start.3
  11.2 2.2 %collective-permute-start.2 = (bf16[14,16,512]{2,1,0:T(8,128)(2,1)S(1)}, bf16[14,16,512]{2,1,0:T(8,128)(2,1)S(1)}, u32[]{:S(2)}, u32[]{:S(2)}) collective-permute-start(bf16[14,16,512]{2,1,0:T(8,128)(2,1)S(1)} %get-tuple-element.157), channel_id=1, source_target_pairs={{1,2},{5,6},{9,10},{13,14},{17,18},{21,22},{25,26},{29,30}} | collective-permute-start | bytes 688136 | tf_op jit(solution)/shard_map/ppermute | solution.py:1011
  12.1 20.6 %collective-permute-start.5 = (bf16[14,16,512]{2,1,0:T(8,128)(2,1)S(1)}, bf16[14,16,512]{2,1,0:T(8,128)(2,1)S(1)}, u32[]{:S(2)}, u32[]{:S(2)}) collective-permute-start(bf16[14,16,512]{2,1,0:T(8,128)(2,1)S(1)} %get-tuple-element.174), channel_id=1, source_target_pairs={{2,3},{6,7},{10,11},{14,15},{18,19},{22,23},{26,27},{30,31}} | collective-permute-start | bytes 688136 | tf_op jit(solution)/shard_map/ppermute | solution.py:1011
  13.6 26.6 %collective-permute-start.4 = (bf16[14,16,512]{2,1,0:T(8,128)(2,1)S(1)}, bf16[14,16,512]{2,1,0:T(8,128)(2,1)S(1)}, u32[]{:S(2)}, u32[]{:S(2)}) collective-permute-start(bf16[14,16,512]{2,1,0:T(8,128)(2,1)S(1)} %get-tuple-element.173), channel_id=1, source_target_pairs={{2,3},{6,7},{10,11},{14,15},{18,19},{22,23},{26,27},{30,31}} | collective-permute-start | bytes 688136 | tf_op jit(solution)/shard_map/ppermute | solution.py:1011
  52.1 8.4 %collective-permute-start.7 = (bf16[14,16,512]{2,1,0:T(8,128)(2,1)S(1)}, bf16[14,16,512]{2,1,0:T(8,128)(2,1)S(1)}, u32[]{:S(2)}, u32[]{:S(2)}) collective-permute-start(bf16[14,16,512]{2,1,0:T(8,128)(2,1)S(1)} %get-tuple-element.200), channel_id=1, source_target_pairs={{3,2},{7,6},{11,10},{15,14},{19,18},{23,22},{27,26},{31,30}} | collective-permute-start | bytes 688136 | tf_op jit(solution)/shard_map/ppermute | solution.py:1047
  59.1 2.4 %collective-permute-start.6 = (bf16[14,16,512]{2,1,0:T(8,128)(2,1)S(1)}, bf16[14,16,512]{2,1,0:T(8,128)(2,1)S(1)}, u32[]{:S(2)}, u32[]{:S(2)}) collective-permute-start(bf16[14,16,512]{2,1,0:T(8,128)(2,1)S(1)} %get-tuple-element.199), channel_id=1, source_target_pairs={{3,2},{7,6},{11,10},{15,14},{19,18},{23,22},{27,26},{31,30}} | collective-permute-start | bytes 688136 | tf_op jit(solution)/shard_map/ppermute | solution.py:1047
  60.6 6.1 %collective-permute-start.9 = (bf16[14,16,512]{2,1,0:T(8,128)(2,1)S(1)}, bf16[14,16,512]{2,1,0:T(8,128)(2,1)S(1)}, u32[]{:S(2)}, u32[]{:S(2)}) collective-permute-start(bf16[14,16,512]{2,1,0:T(8,128)(2,1)S(1)} %get-tuple-element.212), channel_id=1, source_target_pairs={{2,1},{6,5},{10,9},{14,13},{18,17},{22,21},{26,25},{30,29}} | collective-permute-start | bytes 688136 | tf_op jit(solution)/shard_map/ppermute | solution.py:1047
  65.9 1.7 collective-permute-start.8
  66.9 1.5 collective-permute-start.11
  67.7 0.9 collective-permute-start.10
  77.1 7.4 %copy-start.11 = (bf16[1,1,14,14,512]{4,3,2,1,0:T(8,128)(2,1)S(1)}, bf16[1,1,14,14,512]{4,3,2,1,0:T(8,128)(2,1)}, u32[]{:S(2)}) copy-start(bf16[1,1,14,14,512]{4,3,2,1,0:T(8,128)(2,1)} %param.16) | copy-start | bytes 602116
  77.1 73.3 %all-to-all-start = ((bf16[24,512,128]{2,1,0:T(8,128)(2,1)}), bf16[24,512,128]{2,1,0:T(8,128)(2,1)}, u32[]{:S(2)}, u32[]{:S(2)}) async-start(bf16[24,512,128]{2,1,0:T(8,128)(2,1)} %get-tuple-element.235), calls=%async_computation | async-start | bytes 6291456 | tf_op jit(solution)/shard_map/all_to_all | solution.py:1053
  151.2 0.7 collective-permute-start.12
  152.8 0.7 collective-permute-start.13
  154.3 44.2 %collective-permute-start.14 = (bf16[14,16,512]{2,1,0:T(8,128)(2,1)S(1)}, bf16[14,16,512]{2,1,0:T(8,128)(2,1)S(1)}, u32[]{:S(2)}, u32[]{:S(2)}) collective-permute-start(bf16[14,16,512]{2,1,0:T(8,128)(2,1)S(1)} %get-tuple-element.258), channel_id=1, source_target_pairs={{2,3},{6,7},{10,11},{14,15},{18,19},{22,23},{26,27},{30,31}} | collective-permute-start | bytes 688136 | tf_op jit(solution)/shard_map/ppermute | solution.py:1142
  (5 other events, 6.7 us)
